TPU v7x, 32 devices: a whole 2x2x4 slice. The times are simulated.
32 devices in a mesh: rep: 2 (over y), frame: 16 (over z, x, core).
Axes of the slice: x: 2, y: 2, z: 4, core: 2. Of those that a mesh axis runs over, the one named last changes fastest.
Arguments:
- frames: bfloat16 [4096, 512], P(('rep', 'frame')), parts along dimension 0, may hold values from -6 to 6
- segment: int32 [4096], P(('rep', 'frame')), parts along dimension 0, may hold values from 0 to 8, as said below
- latents: bfloat16 [2048, 1024], P('frame'), may hold values from -1.5 to 1.5
- latent_queries: bfloat16 [2048, 1024], P('frame'), may hold values from -240 to 240
- w_kv: bfloat16 [512, 2048], replicated, may hold values from -0.25 to 0.25
- w_cross_out: bfloat16 [1024, 1024], replicated, may hold values from -0.1875 to 0.1875
- w_self_qkv: bfloat16 [1024, 3072], replicated
- w_self_out: bfloat16 [1024, 1024], replicated, may hold values from -0.1875 to 0.1875
Outputs:
- encoded: bfloat16 [4096, 1024], P(('rep', 'frame')), parts along dimension 0
There are 2 independent parts, one for each index of `rep`. A program takes and returns all parts, laid end to end along the dimension named above; an argument that names none is the same for every part. Nothing has to cross between parts.
Inputs may be any that keep to these rules, and one draw needn't show every extreme that they name: `segment`: ids are constant over aligned runs of 64 frames; 0 marks silence; every id from 1 to 8 labels some frame; the share of silent frames differs between regions of the recording.
All inputs are finite; a program needn't handle non-finite values.
Results may differ from a plain program's by a relative error of at most 0.014.
The roundings to bfloat16 on the way count: a program that leaves them out, or rounds other values in their place, can miss the bound.
Values may be sent and summed in bfloat16 or wider, within the bound.
No kernel may reach another device: no remote copies, remote signals or barrier semaphores. Data moves between devices by JAX's collectives and lax.ppermute only.
A program may use at most 128 MiB of HBM per device.

v0:
```python
import functools
import math

import jax
import jax.numpy as jnp
from jax import lax
from jax.experimental import pallas as pl
from jax.experimental.pallas import tpu as pltpu
from jax.sharding import PartitionSpec as P

H = 16
HEAD_DIM = 64
L = 2048
NB = 8


NEG = -1e30


def layer_norm(inputs):
    centre = inputs - jnp.mean(inputs, axis=-1, keepdims=True)
    spread = jnp.mean(centre * centre, axis=-1, keepdims=True)
    return centre * lax.rsqrt(spread + 1e-05)


def shards_any(frames, segment, latents, latent_queries, w_kv, w_cross_out, w_self_qkv, w_self_out):
    feature_width = w_kv.shape[1] // 2
    owned_rows = latents.shape[0]
    frame_count = frames.shape[0]
    scale = 1.0 / math.sqrt(HEAD_DIM)
    block_rows = L // NB
    latent_full = latents.astype(jnp.float32)
    normed = layer_norm(frames.astype(jnp.float32)).astype(jnp.bfloat16)
    keyval = jnp.dot(normed, w_kv, preferred_element_type=jnp.float32).astype(jnp.bfloat16)
    key_heads = keyval[:, :feature_width].reshape(frame_count, H, HEAD_DIM).transpose(1, 0, 2)
    value_heads = keyval[:, feature_width:].reshape(frame_count, H, HEAD_DIM).transpose(1, 0, 2)
    total_rows = owned_rows * lax.axis_size("frame")
    piece = lax.all_gather(latent_queries, "frame", axis=0, tiled=True)
    piece_rows = piece.shape[0]
    block_ids = jnp.arange(piece_rows, dtype=jnp.int32) // block_rows + 1
    allowed = segment[None, :] == block_ids[:, None]
    query_heads = piece.reshape(piece_rows, H, HEAD_DIM).transpose(1, 0, 2)

    def one_head(item):
        query_head, key_head, value_head = item
        score = (
            jnp.einsum("re,fe->rf", query_head, key_head, preferred_element_type=jnp.float32)
            * scale
        )
        score = jnp.where(allowed, score, NEG)
        block_max = jnp.max(score, axis=1)
        weights = jnp.where(allowed, jnp.exp(score - block_max[:, None]), 0.0)
        block_total = jnp.sum(weights, axis=1)
        summed = jnp.dot(
            weights.astype(jnp.bfloat16), value_head, preferred_element_type=jnp.float32
        )
        return (block_max, block_total, summed)

    block_max, block_total, summed = lax.map(one_head, (query_heads, key_heads, value_heads))
    run_max = block_max.T
    run_total = block_total.T
    joined = summed.transpose(1, 0, 2).reshape(piece_rows, feature_width)
    run_acc = joined
    run_max, run_total, run_acc = (run_max, run_total, run_acc)
    sources = lax.axis_size("frame")
    got_acc, got_max, got_total = (
        lax.all_to_all(
            run_acc.reshape(sources, owned_rows, feature_width),
            "frame",
            split_axis=0,
            concat_axis=0,
            tiled=True,
        ),
        lax.all_to_all(
            run_max.reshape(sources, owned_rows, H),
            "frame",
            split_axis=0,
            concat_axis=0,
            tiled=True,
        ),
        lax.all_to_all(
            run_total.reshape(sources, owned_rows, H),
            "frame",
            split_axis=0,
            concat_axis=0,
            tiled=True,
        ),
    )
    global_max = jnp.max(got_max, axis=0)
    factor = jnp.exp(got_max - global_max[None])
    norms = jnp.sum(got_total * factor, axis=0)
    sums = jnp.sum(
        got_acc.reshape(sources, owned_rows, H, HEAD_DIM) * factor[:, :, :, None], axis=0
    )
    cross = (sums / norms[:, :, None]).reshape(owned_rows, feature_width)
    cross = cross.astype(jnp.bfloat16)
    mixed = latent_full + jnp.dot(cross, w_cross_out, preferred_element_type=jnp.float32)
    normed_latent = layer_norm(mixed).astype(jnp.bfloat16)
    triple = jnp.dot(normed_latent, w_self_qkv, preferred_element_type=jnp.float32).astype(
        jnp.bfloat16
    )
    self_query = triple[:, :feature_width].reshape(owned_rows, H, HEAD_DIM)
    self_key = triple[:, feature_width : 2 * feature_width]
    self_value = triple[:, 2 * feature_width :]
    every_key, every_value = (
        lax.all_gather(self_key, "frame", axis=0, tiled=True),
        lax.all_gather(self_value, "frame", axis=0, tiled=True),
    )
    every_key = every_key.reshape(total_rows, H, HEAD_DIM)
    every_value = every_value.reshape(total_rows, H, HEAD_DIM)
    score = (
        jnp.einsum("rhe,mhe->hrm", self_query, every_key, preferred_element_type=jnp.float32)
        * scale
    )
    peak = jnp.max(score, axis=2, keepdims=True)
    expo = jnp.exp(score - peak)
    probs = (expo / jnp.sum(expo, axis=2, keepdims=True)).astype(jnp.bfloat16)
    attended = jnp.einsum("hrm,mhe->rhe", probs, every_value, preferred_element_type=jnp.float32)
    attended = attended.reshape(owned_rows, feature_width).astype(jnp.bfloat16)
    return (mixed + jnp.dot(attended, w_self_out, preferred_element_type=jnp.float32)).astype(
        jnp.bfloat16
    )


RUN = 64
PAD = 8
GROUP = 4
LATE = 2
WIDE = 256
PAIR = 2 * HEAD_DIM
BF16 = jnp.bfloat16
F32 = jnp.float32
VMEM = pltpu.VMEM


def norm(v):
    centre = v - jnp.mean(v, axis=-1, keepdims=True)
    spread = jnp.mean(centre * centre, axis=-1, keepdims=True)
    return centre * lax.rsqrt(spread + 1e-05)


def fill_stacks(stacks, j, blocks):
    for q in range(WIDE // PAIR):
        i = j * (WIDE // PAIR) + q
        wide = stacks.shape[2] // 2
        at = 0
        for block in blocks:
            turned = block[:, q * PAIR : (q + 1) * PAIR].T
            n = turned.shape[1]
            none = jnp.zeros((HEAD_DIM, n), BF16)
            stacks[i, :HEAD_DIM, at : at + n] = turned[:HEAD_DIM]
            stacks[i, HEAD_DIM:, at : at + n] = none
            stacks[i, :HEAD_DIM, wide + at : wide + at + n] = none
            stacks[i, HEAD_DIM:, wide + at : wide + at + n] = turned[HEAD_DIM:]
            at += n


def project(normed, weights, at, width, keys, values):
    n = normed.shape[0]
    for j in range(width // WIDE):
        cols = slice(j * WIDE, (j + 1) * WIDE)
        k = jnp.dot(normed, weights[:, at + j * WIDE : at + (j + 1) * WIDE], preferred_element_type=F32)
        keys[:n, cols] = k.astype(BF16)
        v = jnp.dot(
            normed, weights[:, at + width + j * WIDE : at + width + (j + 1) * WIDE], preferred_element_type=F32
        )
        values[cols, :n] = v.astype(BF16).T


def attend(n, left, stacks, keys, values, scores, probs, old, new):
    pairs, wide = stacks.shape[0], stacks.shape[2]
    half = wide // 2
    tops, totals, accs = new
    masked = left is not None
    if masked:
        valid = lax.broadcasted_iota(jnp.int32, (n, wide), 0) < left
    for i in range(pairs):
        score = jnp.dot(keys[:n, i * PAIR : (i + 1) * PAIR], stacks[i], preferred_element_type=F32)
        if masked:
            score = jnp.where(valid, score, NEG)
        scores[i, :n] = score
        top = jnp.max(score, axis=0, keepdims=True)
        tops[i : i + 1] = top if old is None else jnp.maximum(old[0][i : i + 1], top)
    for i in range(pairs):
        top = tops[i : i + 1]
        weights = jnp.exp(scores[i, :n] - top)
        if masked:
            weights = jnp.where(valid, weights, 0.0)
        total = jnp.sum(weights, axis=0, keepdims=True)
        if old is not None:
            total = total + old[1][i : i + 1] * jnp.exp(old[0][i : i + 1] - top)
        totals[i : i + 1] = total
        probs[i, :n] = weights.astype(BF16)
    for i in range(pairs):
        out = jnp.dot(values[i * PAIR : (i + 1) * PAIR, :n], probs[i, :n], preferred_element_type=F32)
        if old is not None:
            fade = jnp.exp(old[0][i : i + 1] - tops[i : i + 1])
        for h in range(2):
            rows = slice(i * PAIR + h * HEAD_DIM, i * PAIR + (h + 1) * HEAD_DIM)
            cols = slice(h * half, (h + 1) * half)
            part = out[h * HEAD_DIM : (h + 1) * HEAD_DIM, cols]
            if old is not None:
                part = part + old[2][rows, :] * fade[:, cols]
            accs[rows, :] = part


def tag_kernel(segment, frames, out, labels, sems):
    parts = [(frames.at[:RUN], out.at[:RUN]), (frames.at[RUN:], out.at[RUN + PAD :]), (segment, labels)]
    copies = [pltpu.make_async_copy(src, dst, sems.at[i]) for i, (src, dst) in enumerate(parts)]
    for copy in copies:
        copy.start()
    copies[2].wait()
    upper = lax.broadcasted_iota(jnp.int32, (PAD, out.shape[1]), 0) < PAD // 2
    out[RUN : RUN + PAD] = jnp.where(upper, labels[0].astype(F32), labels[RUN].astype(F32)).astype(BF16)
    copies[0].wait()
    copies[1].wait()


def queries_kernel(queries, stacks):
    scale = 1.0 / math.sqrt(HEAD_DIM)
    for j in range(queries.shape[1] // WIDE):
        block = queries[:, j * WIDE : (j + 1) * WIDE].astype(F32) * scale
        fill_stacks(stacks, j, [block.astype(BF16)])


def pick_runs(pieces, mine, picked, count):
    ids = [
        jnp.max(ref[label - label % PAD : label - label % PAD + PAD, :128][label % PAD : label % PAD + PAD // 2].astype(F32))
        for ref, spots in pieces for _, label in spots
    ]
    spots = [(ref, row) for ref, places in pieces for row, _ in places]
    count[0] = 0
    for label, (ref, row) in zip(ids, spots):
        @pl.when(label.astype(jnp.int32) == mine)
        def _(ref=ref, row=row):
            at = count[0]
            picked[at] = ref[row : row + RUN, :]
            count[0] = at + 1
    found = count[0]
    for extra in range(GROUP - 1):
        picked[found + extra] = jnp.zeros(picked.shape[1:], BF16)
    return found


def cross_groups(found, group, picked, w_kv, stacks, keys, values, scores, probs, state):
    width = state[2].shape[0]

    def one_group(g, carry):
        n = group * RUN
        frames = picked[pl.ds(g * group, group)].reshape(n, picked.shape[2])
        project(norm(frames.astype(F32)).astype(BF16), w_kv, 0, width, keys, values)
        old = (state[0][...], state[1][...], state[2])
        attend(n, (found - g * group) * RUN, stacks, keys, values, scores, probs, old, state)
        return carry

    lax.fori_loop(0, (found + group - 1) // group, one_group, 0)


def places(shape):
    if shape[0] == 2 * RUN + PAD:
        return [(0, RUN), (RUN + PAD, RUN + PAD // 2)]
    return None


def early_kernel(n_pieces, rows, *refs):
    pieces = [(ref, places(ref.shape)) for ref in refs[:n_pieces]]
    stacks, w_kv, tops, totals, accs, picked, keys, values, scores, probs, count = refs[n_pieces:]
    mine = (lax.axis_index("frame") * rows) // (L // NB) + 1
    tops[...] = jnp.full(tops.shape, NEG, F32)
    totals[...] = jnp.zeros(totals.shape, F32)
    accs[...] = jnp.zeros(accs.shape, F32)
    found = pick_runs(pieces, mine, picked, count)
    cross_groups(found, GROUP, picked, w_kv, stacks, keys, values, scores, probs, (tops, totals, accs))


def cross_kernel(n_pieces, *refs):
    (latents, stacks, w_kv, w_out, old_tops, old_totals, _, mixed_out, normed_out, tops, totals, accs,
     picked, keys, values, scores, probs, joined, count) = refs[n_pieces:]
    rows, _ = latents.shape
    mine = (lax.axis_index("frame") * rows) // (L // NB) + 1
    pieces = []
    for at, ref in enumerate(refs[:n_pieces]):
        half = [(0, RUN)] if at % 2 == 0 else [(PAD, PAD // 2)]
        pieces.append((ref, places(ref.shape) or half))
    tops[...], totals[...] = old_tops[...], old_totals[...]
    found = pick_runs(pieces, mine, picked, count)
    cross_groups(found, LATE, picked, w_kv, stacks, keys, values, scores, probs, (tops, totals, accs))
    finish(accs, totals, joined)
    mixed = latents[...].astype(F32) + jnp.dot(joined[...], w_out[...], preferred_element_type=F32)
    mixed_out[...] = mixed
    normed_out[...] = norm(mixed).astype(BF16)


def finish(accs, totals, joined):
    half = totals.shape[1] // 2
    for i in range(totals.shape[0]):
        parts = []
        for h in range(2):
            rows = slice(i * PAIR + h * HEAD_DIM, i * PAIR + (h + 1) * HEAD_DIM)
            parts.append(accs[rows, :] / totals[i : i + 1, h * half : (h + 1) * half])
        joined[:, i * PAIR : (i + 1) * PAIR] = jnp.concatenate(parts, axis=0).astype(BF16).T


def first_kernel(mine, other, w_qkv, stacks, tops, totals, accs, keys, values, scores, probs):
    rows, width = mine.shape
    scale = 1.0 / math.sqrt(HEAD_DIM)
    both = jnp.concatenate([mine[...], other[...]], axis=0)
    for j in range(width // WIDE):
        query = jnp.dot(both, w_qkv[:, j * WIDE : (j + 1) * WIDE], preferred_element_type=F32).astype(BF16)
        fill_stacks(stacks, j, [(query.astype(F32) * scale).astype(BF16)])
    project(mine[...], w_qkv, width, width, keys, values)
    attend(rows, None, stacks, keys, values, scores, probs, None, (tops, totals, accs))


def next_kernel(n_pieces, *refs):
    sources = refs[:n_pieces]
    (w_qkv, stacks, old_tops, old_totals, old_accs, tops, totals, accs, keys, values, scores, probs) = refs[n_pieces:]
    width = accs.shape[0]
    block = jnp.concatenate([s[...] for s in sources], axis=0)
    project(block, w_qkv, width, width, keys, values)
    old = (old_tops[...], old_totals[...], old_accs)
    attend(block.shape[0], None, stacks, keys, values, scores, probs, old, (tops, totals, accs))


def final_kernel(tops, totals, accs, far, mixed, w_out, out, joined, merged, sums):
    width, rows = far.shape[0] - 2 * 2 * tops.shape[0], far.shape[1]
    for i in range(tops.shape[0]):
        for h in range(2):
            at = 2 * i + h
            here = slice(h * 2 * rows, h * 2 * rows + rows)
            lines = slice(i * PAIR + h * HEAD_DIM, i * PAIR + (h + 1) * HEAD_DIM)
            near_top, far_top = tops[i : i + 1, here], far[width + at : width + at + 1]
            top = jnp.maximum(near_top, far_top)
            near_fade, far_fade = jnp.exp(near_top - top), jnp.exp(far_top - top)
            far_total = far[width + 2 * tops.shape[0] + at : width + 2 * tops.shape[0] + at + 1]
            sums[i : i + 1, h * rows : (h + 1) * rows] = totals[i : i + 1, here] * near_fade + far_total * far_fade
            merged[lines] = accs[lines, :rows] * near_fade + far[lines] * far_fade
    finish(merged, sums, joined)
    out[...] = (mixed[...] + jnp.dot(joined[...], w_out[...], preferred_element_type=F32)).astype(BF16)


def last_kernel(n_pieces, *refs):
    sources = refs[:n_pieces]
    (w_qkv, stacks, old_tops, old_totals, old_accs, tops, totals, accs, away,
     keys, values, scores, probs) = refs[n_pieces:]
    next_kernel(n_pieces, *sources, w_qkv, stacks, old_tops, old_totals, old_accs, tops, totals, accs,
                keys, values, scores, probs)
    width, rows = accs.shape[0], accs.shape[1] // 2
    away[:width] = accs[:, rows:]
    for i in range(tops.shape[0]):
        for h in range(2):
            there = slice(h * 2 * rows + rows, (h + 1) * 2 * rows)
            at = 2 * i + h
            away[width + at : width + at + 1] = tops[i : i + 1, there]
            at += 2 * tops.shape[0]
            away[width + at : width + at + 1] = totals[i : i + 1, there]


def on_chip(x):
    return pltpu.with_memory_space_constraint(x, VMEM)


def call(kernel, args, outs, scratch, flops, limit, aliases=None, scalars=0):
    specs = [pl.BlockSpec(memory_space=pltpu.SMEM)] * scalars
    specs += [pl.BlockSpec(memory_space=VMEM)] * (len(args) - scalars)
    return pl.pallas_call(
        kernel,
        out_shape=outs,
        in_specs=specs,
        out_specs=jax.tree.map(lambda _: pl.BlockSpec(memory_space=VMEM), outs, is_leaf=lambda o: hasattr(o, "shape")),
        scratch_shapes=scratch,
        compiler_params=pltpu.CompilerParams(vmem_limit_bytes=limit << 20),
        cost_estimate=pl.CostEstimate(flops=flops, bytes_accessed=1 << 20, transcendentals=0),
        input_output_aliases=aliases or {},
    )(*args[:scalars], *[on_chip(a) for a in args[scalars:]])


def shards_ring(frames, segment, latents, latent_queries, w_kv, w_cross_out, w_self_qkv, w_self_out):
    chips = lax.axis_size("frame") // 2
    rows, width = latents.shape
    channels = frames.shape[1]
    order = [2 * k for k in range(chips // 2)] + [2 * k + 1 for k in reversed(range(chips // 2))]
    swap = [(i, i ^ 1) for i in range(2 * chips)]
    ahead = [(2 * order[k] + c, 2 * order[(k + 1) % chips] + c) for k in range(chips) for c in range(2)]
    behind = [(there, here) for here, there in ahead]

    def cross_over(x):
        return lax.ppermute(x, "frame", swap)

    def both_ways(fore, aft):
        fore = lax.ppermute(fore, "frame", ahead)
        aft = lax.ppermute(aft, "frame", behind)
        return fore, aft

    def swapped(fore, aft):
        fore = cross_over(fore)
        aft = cross_over(aft)
        return fore, aft

    def ring(x):
        fore, aft = x, x
        found = []
        for _ in range(1, chips // 2):
            fore, aft = both_ways(fore, aft)
            found.append([fore, aft])
        cut = x.shape[0] // 2
        return found + [list(both_ways(fore[:cut], aft[cut:]))]

    def gather(tagged):
        cut = tagged.shape[0] // 2 + PAD // 2
        found = [[tagged, cross_over(tagged)]]
        fore, aft = tagged, tagged
        for _ in range(1, chips // 2):
            fore, aft = both_ways(fore, aft)
            found.append([fore, aft, *swapped(fore, aft)])
        fore, aft = both_ways(fore[:cut], aft[-cut:])
        return found + [[fore, aft, cross_over(fore), cross_over(aft)]]

    pairs = width // PAIR
    tagged = pl.pallas_call(
        tag_kernel,
        out_shape=VMEM((frames.shape[0] + PAD, channels), BF16),
        in_specs=[pl.BlockSpec(memory_space=pl.ANY)] * 2,
        out_specs=pl.BlockSpec(memory_space=VMEM),
        scratch_shapes=[pltpu.SMEM(segment.shape, jnp.int32), pltpu.SemaphoreType.DMA((3,))],
        compiler_params=pltpu.CompilerParams(vmem_limit_bytes=2 << 20),
        cost_estimate=pl.CostEstimate(flops=1 << 34, bytes_accessed=1 << 20, transcendentals=0),
        name="tag",
    )(*[pltpu.with_memory_space_constraint(x, pltpu.HBM) for x in (segment, frames)])
    stacks = call(queries_kernel, [latent_queries], VMEM((pairs, PAIR, 2 * rows), BF16), [], 1 << 28, 4)

    def state(queries):
        return (VMEM((pairs, 2 * queries), F32), VMEM((pairs, 2 * queries), F32), VMEM((width, queries), F32))

    def work(n, queries):
        return [
            VMEM((n, width), BF16), VMEM((width, n), BF16),
            VMEM((pairs, n, 2 * queries), F32), VMEM((pairs, n, 2 * queries), BF16),
        ]

    pieces = gather(tagged)
    soon = [piece for group in pieces[:-2] for piece in group]
    late = [piece for group in pieces[-2:] for piece in group]
    kept = call(
        functools.partial(early_kernel, len(soon), rows), soon + [stacks, w_kv], state(rows),
        [VMEM((2 * len(soon) + GROUP, RUN, channels), BF16), *work(GROUP * RUN, rows), pltpu.SMEM((1,), jnp.int32)],
        1 << 30, 16,
    )
    n = len(late)
    mixed, normed, *_ = call(
        functools.partial(cross_kernel, n),
        late + [latents, stacks, w_kv, w_cross_out, *kept],
        (VMEM((rows, width), F32), VMEM((rows, width), BF16), *state(rows)),
        [
            VMEM((2 * n + GROUP, RUN, channels), BF16), *work(LATE * RUN, rows),
            VMEM((rows, width), BF16), pltpu.SMEM((1,), jnp.int32),
        ],
        4 << 30, 16, {n + 4: 2, n + 5: 3, n + 6: 4},
    )
    arrivals = ring(normed)
    stacks, *kept = call(
        first_kernel, [normed, cross_over(normed), w_self_qkv],
        (VMEM((pairs, PAIR, 4 * rows), BF16), *state(2 * rows)), work(rows, 2 * rows), 1 << 30, 16,
    )
    for sources in arrivals[:-1]:
        n = len(sources)
        kept = call(
            functools.partial(next_kernel, n), sources + [w_self_qkv, stacks, *kept],
            state(2 * rows), work(n * rows, 2 * rows), n << 30, 20, {n + 2: 0, n + 3: 1, n + 4: 2},
        )
    sources = arrivals[-1]
    n = len(sources)
    *kept, away = call(
        functools.partial(last_kernel, n), sources + [w_self_qkv, stacks, *kept],
        (*state(2 * rows), VMEM((width + 4 * pairs, rows), F32)), work(rows, 2 * rows), 1 << 30, 20,
        {n + 2: 0, n + 3: 1, n + 4: 2},
    )
    return call(
        final_kernel, [*kept, cross_over(away), mixed, w_self_out],
        jax.ShapeDtypeStruct((rows, width), BF16),
        [VMEM((rows, width), BF16), VMEM((width, rows), F32), VMEM((pairs, 2 * rows), F32)],
        1 << 30, 12,
    )


def solution(mesh):
    placed = (
        P(("rep", "frame"), None),
        P(("rep", "frame")),
        P("frame", None),
        P("frame", None),
        P(),
        P(),
        P(),
        P(),
    )
    if mesh.shape["frame"] != 16:
        return jax.shard_map(
            shards_any, mesh=mesh, in_specs=placed, out_specs=P(("rep", "frame"), None), check_vma=False
        )

    return jax.shard_map(shards_ring, mesh=mesh, in_specs=placed, out_specs=P(("rep", "frame"), None), check_vma=False)
```

profile of v0, /device:TPU:13, one launch (start us, length us, event | category | flops | bytes accessed | tf_op | source)
XLA Modules:
  0.0 66.7 jit_solution(15558277838740320403)
XLA Ops:
  1.1 1.3 %collective-permute-start = (bf16[136,512]{1,0:T(8,128)(2,1)S(1)}, bf16[136,512]{1,0:T(8,128)(2,1)S(1)}, u32[]{:S(2)}, u32[]{:S(2)}) collective-permute-start(bf16[136,512]{1,0:T(8,128)(2,1)S(1)} %tag.1.refs_0_), channel_id=1, source_target_pairs={{0,4},{1,5},{4,8},{5,9},{8,12},{9,13},{12,14},{13,15},{14,10},{15,... | collective-permute-start | bytes 417800 | tf_op jit(solution)/shard_map/ppermute | solution.py:391
  2.6 3.1 %collective-permute-done.refs_2_ = bf16[136,512]{1,0:T(8,128)(2,1)S(1)} collective-permute-done((bf16[136,512]{1,0:T(8,128)(2,1)S(1)}, bf16[136,512]{1,0:T(8,128)(2,1)S(1)}, u32[]{:S(2)}, u32[]{:S(2)}) %collective-permute-start) | collective-permute-done | bytes 139296 | tf_op jit(solution)/shard_map/ppermute | solution.py:391
  5.7 1.3 %collective-permute-start.1 = (bf16[136,512]{1,0:T(8,128)(2,1)S(1)}, bf16[136,512]{1,0:T(8,128)(2,1)S(1)}, u32[]{:S(2)}, u32[]{:S(2)}) collective-permute-start(bf16[136,512]{1,0:T(8,128)(2,1)S(1)} %collective-permute-done.refs_2_), channel_id=1, source_target_pairs={{0,4},{1,5},{4,8},{5,9},{8,12},{9,13},{12,14},{13,15},{14,10},{15,... | collective-permute-start | bytes 417800 | tf_op jit(solution)/shard_map/ppermute | solution.py:391
  7.1 2.4 %collective-permute-done.1.refs_6_ = bf16[136,512]{1,0:T(8,128)(2,1)S(1)} collective-permute-done((bf16[136,512]{1,0:T(8,128)(2,1)S(1)}, bf16[136,512]{1,0:T(8,128)(2,1)S(1)}, u32[]{:S(2)}, u32[]{:S(2)}) %collective-permute-start.1) | collective-permute-done | bytes 139296 | tf_op jit(solution)/shard_map/ppermute | solution.py:391
  11.3 2.9 %collective-permute-start.12 = (bf16[136,512]{1,0:T(8,128)(2,1)S(1)}, bf16[136,512]{1,0:T(8,128)(2,1)S(1)}, u32[]{:S(2)}, u32[]{:S(2)}) collective-permute-start(bf16[136,512]{1,0:T(8,128)(2,1)S(1)} %tag.1.refs_0_), channel_id=1, source_target_pairs={{0,1},{1,0},{2,3},{3,2},{4,5},{5,4},{6,7},{7,6},{8,9},{9,8},{10,11... | collective-permute-start | bytes 417800 | tf_op jit(solution)/shard_map/ppermute | solution.py:388
  14.8 2.5 %collective-permute-start.15 = (bf16[136,512]{1,0:T(8,128)(2,1)S(1)}, bf16[136,512]{1,0:T(8,128)(2,1)S(1)}, u32[]{:S(2)}, u32[]{:S(2)}) collective-permute-start(bf16[136,512]{1,0:T(8,128)(2,1)S(1)} %collective-permute-done.1.refs_6_), channel_id=1, source_target_pairs={{0,1},{1,0},{2,3},{3,2},{4,5},{5,4},{6,7},{7,6},{8,9},{9,8},{10,11... | collective-permute-start | bytes 417800 | tf_op jit(solution)/shard_map/ppermute | solution.py:388
  17.3 1.6 %collective-permute-start.16 = (bf16[136,512]{1,0:T(8,128)(2,1)S(1)}, bf16[136,512]{1,0:T(8,128)(2,1)S(1)}, u32[]{:S(2)}, u32[]{:S(2)}) collective-permute-start(bf16[136,512]{1,0:T(8,128)(2,1)S(1)} %collective-permute-done.4.refs_7_), channel_id=1, source_target_pairs={{0,1},{1,0},{2,3},{3,2},{4,5},{5,4},{6,7},{7,6},{8,9},{9,8},{10,11... | collective-permute-start | bytes 417800 | tf_op jit(solution)/shard_map/ppermute | solution.py:388
  18.9 1.3 %collective-permute-start.8 = (bf16[72,512]{1,0:T(8,128)(2,1)S(1)}, bf16[72,512]{1,0:T(8,128)(2,1)S(1)}, u32[]{:S(2)}, u32[]{:S(2)}) collective-permute-start(bf16[72,512]{1,0:T(8,128)(2,1)S(1)} %slice.16), channel_id=1, source_target_pairs={{0,4},{1,5},{4,8},{5,9},{8,12},{9,13},{12,14},{13,15},{14,10},{15,... | collective-permute-start | bytes 221192 | tf_op jit(solution)/shard_map/ppermute | solution.py:391
  21.3 1.5 %collective-permute-done.8.refs_4_ = bf16[72,512]{1,0:T(8,128)(2,1)S(1)} collective-permute-done((bf16[72,512]{1,0:T(8,128)(2,1)S(1)}, bf16[72,512]{1,0:T(8,128)(2,1)S(1)}, u32[]{:S(2)}, u32[]{:S(2)}) %collective-permute-start.8) | collective-permute-done | bytes 73760 | tf_op jit(solution)/shard_map/ppermute | solution.py:391
  25.0 2.3 %shard_map.83 = (f32[8,256]{1,0:T(8,128)S(1)}, f32[8,256]{1,0:T(8,128)S(1)}, f32[1024,128]{1,0:T(8,128)S(1)}) custom-call(bf16[136,512]{1,0:T(8,128)(2,1)S(1)} %tag.1.refs_0_, bf16[136,512]{1,0:T(8,128)(2,1)S(1)} %collective-permute-done.12.refs_1_, bf16[136,512]{1,0:T(8,128)(2,1)S(1)} %collective-permute-done.refs_2_, ...), custom_call_target="tpu_custom_call" | custom-call | flops 1073741824 | bytes 1048576 | tf_op jit(solution)/shard_map/pallas_call | solution.py:366
  27.3 2.1 %shard_map.84 = (f32[128,1024]{1,0:T(8,128)S(1)}, bf16[128,1024]{1,0:T(8,128)(2,1)S(1)}, f32[8,256]{1,0:T(8,128)S(1)}, f32[8,256]{1,0:T(8,128)S(1)}, f32[1024,128]{1,0:T(8,128)S(1)}) custom-call(bf16[136,512]{1,0:T(8,128)(2,1)S(1)} %collective-permute-done.2.refs_0_, ...), custom_call_target="tpu_custom_call", output_to_operand_aliasing={{2}: (12, {}), {3}: (13, {}), {4}: (14, {})} | custom-call | flops 4294967296 | bytes 1048576 | tf_op jit(solution)/shard_map/pallas_call | solution.py:366
  29.5 2.5 %collective-permute-start.17 = (bf16[128,1024]{1,0:T(8,128)(2,1)S(1)}, bf16[128,1024]{1,0:T(8,128)(2,1)S(1)}, u32[]{:S(2)}, u32[]{:S(2)}) collective-permute-start(bf16[128,1024]{1,0:T(8,128)(2,1)S(1)} %get-tuple-element.30.mine), channel_id=1, source_target_pairs={{0,4},{1,5},{4,8},{5,9},{8,12},{9,13},{12,14},{13,15},{14,10},{15,... | collective-permute-start | bytes 786440 | tf_op jit(solution)/shard_map/ppermute | solution.py:391
  32.2 5.4 %collective-permute-done.17.refs_0_ = bf16[128,1024]{1,0:T(8,128)(2,1)S(1)} collective-permute-done((bf16[128,1024]{1,0:T(8,128)(2,1)S(1)}, bf16[128,1024]{1,0:T(8,128)(2,1)S(1)}, u32[]{:S(2)}, u32[]{:S(2)}) %collective-permute-start.17) | collective-permute-done | bytes 262176 | tf_op jit(solution)/shard_map/ppermute | solution.py:391
  37.6 2.2 %collective-permute-start.18 = (bf16[128,1024]{1,0:T(8,128)(2,1)S(1)}, bf16[128,1024]{1,0:T(8,128)(2,1)S(1)}, u32[]{:S(2)}, u32[]{:S(2)}) collective-permute-start(bf16[128,1024]{1,0:T(8,128)(2,1)S(1)} %collective-permute-done.17.refs_0_), channel_id=1, source_target_pairs={{0,4},{1,5},{4,8},{5,9},{8,12},{9,13},{12,14},{13,15},{14,10},{15,... | collective-permute-start | bytes 786440 | tf_op jit(solution)/shard_map/ppermute | solution.py:391
  39.8 2.0 %shard_map.85 = (bf16[8,128,512]{2,1,0:T(8,128)(2,1)S(1)}, f32[8,512]{1,0:T(8,128)S(1)}, f32[8,512]{1,0:T(8,128)S(1)}, f32[1024,256]{1,0:T(8,128)S(1)}) custom-call(bf16[128,1024]{1,0:T(8,128)(2,1)S(1)} %get-tuple-element.30.mine, bf16[128,1024]{1,0:T(8,128)(2,1)S(1)} %collective-permute-done.25.other, bf16[1024,3072]{1,0:T(8,128)(2,1)S(1)} %bitcast.1), custom_call_target="tpu_custom_call" | custom-call | flops 1073741824 | bytes 1048576 | tf_op jit(solution)/shard_map/pallas_call | solution.py:366
  41.9 2.7 %collective-permute-done.18.refs_0_ = bf16[128,1024]{1,0:T(8,128)(2,1)S(1)} collective-permute-done((bf16[128,1024]{1,0:T(8,128)(2,1)S(1)}, bf16[128,1024]{1,0:T(8,128)(2,1)S(1)}, u32[]{:S(2)}, u32[]{:S(2)}) %collective-permute-start.18) | collective-permute-done | bytes 262176 | tf_op jit(solution)/shard_map/ppermute | solution.py:391
  44.6 2.2 %collective-permute-start.19 = (bf16[128,1024]{1,0:T(8,128)(2,1)S(1)}, bf16[128,1024]{1,0:T(8,128)(2,1)S(1)}, u32[]{:S(2)}, u32[]{:S(2)}) collective-permute-start(bf16[128,1024]{1,0:T(8,128)(2,1)S(1)} %collective-permute-done.18.refs_0_), channel_id=1, source_target_pairs={{0,4},{1,5},{4,8},{5,9},{8,12},{9,13},{12,14},{13,15},{14,10},{15,... | collective-permute-start | bytes 786440 | tf_op jit(solution)/shard_map/ppermute | solution.py:391
  46.8 3.0 %shard_map.86 = (f32[8,512]{1,0:T(8,128)S(1)}, f32[8,512]{1,0:T(8,128)S(1)}, f32[1024,256]{1,0:T(8,128)S(1)}) custom-call(bf16[128,1024]{1,0:T(8,128)(2,1)S(1)} %collective-permute-done.17.refs_0_, bf16[128,1024]{1,0:T(8,128)(2,1)S(1)} %collective-permute-done.21.refs_1_, ...), custom_call_target="tpu_custom_call", output_to_operand_aliasing={{0}: (4, {}), {1}: (5, {}), {2}: (6, {})} | custom-call | flops 2147483648 | bytes 1048576 | tf_op jit(solution)/shard_map/pallas_call | solution.py:366
  49.9 3.0 %shard_map.87 = (f32[8,512]{1,0:T(8,128)S(1)}, f32[8,512]{1,0:T(8,128)S(1)}, f32[1024,256]{1,0:T(8,128)S(1)}) custom-call(bf16[128,1024]{1,0:T(8,128)(2,1)S(1)} %collective-permute-done.18.refs_0_, bf16[128,1024]{1,0:T(8,128)(2,1)S(1)} %collective-permute-done.22.refs_1_, ...), custom_call_target="tpu_custom_call", output_to_operand_aliasing={{0}: (4, {}), {1}: (5, {}), {2}: (6, {})} | custom-call | flops 2147483648 | bytes 1048576 | tf_op jit(solution)/shard_map/pallas_call | solution.py:366
  52.9 1.5 %collective-permute-start.20 = (bf16[64,1024]{1,0:T(8,128)(2,1)S(1)}, bf16[64,1024]{1,0:T(8,128)(2,1)S(1)}, u32[]{:S(2)}, u32[]{:S(2)}) collective-permute-start(bf16[64,1024]{1,0:T(8,128)(2,1)S(1)} %slice.18), channel_id=1, source_target_pairs={{0,4},{1,5},{4,8},{5,9},{8,12},{9,13},{12,14},{13,15},{14,10},{15,... | collective-permute-start | bytes 393224 | tf_op jit(solution)/shard_map/ppermute | solution.py:391
  54.5 3.0 %shard_map.88 = (f32[8,512]{1,0:T(8,128)S(1)}, f32[8,512]{1,0:T(8,128)S(1)}, f32[1024,256]{1,0:T(8,128)S(1)}) custom-call(bf16[128,1024]{1,0:T(8,128)(2,1)S(1)} %collective-permute-done.19.refs_0_, bf16[128,1024]{1,0:T(8,128)(2,1)S(1)} %collective-permute-done.23.refs_1_, ...), custom_call_target="tpu_custom_call", output_to_operand_aliasing={{0}: (4, {}), {1}: (5, {}), {2}: (6, {})} | custom-call | flops 2147483648 | bytes 1048576 | tf_op jit(solution)/shard_map/pallas_call | solution.py:366
  58.6 1.7 %shard_map.89 = (f32[8,512]{1,0:T(8,128)S(1)}, f32[8,512]{1,0:T(8,128)S(1)}, f32[1024,256]{1,0:T(8,128)S(1)}, f32[1056,128]{1,0:T(8,128)S(1)}) custom-call(bf16[64,1024]{1,0:T(8,128)(2,1)S(1)} %collective-permute-done.20.refs_0_, bf16[64,1024]{1,0:T(8,128)(2,1)S(1)} %collective-permute-done.24.refs_1_, ...), custom_call_target="tpu_custom_call", output_to_operand_aliasing={{0}: (4, {}), {1}: (5, {}), {2}: (6, {})} | custom-call | flops 1073741824 | bytes 1048576 | tf_op jit(solution)/shard_map/pallas_call | solution.py:366
  60.3 3.5 %collective-permute-start.26 = (f32[1056,128]{1,0:T(8,128)S(1)}, f32[1056,128]{1,0:T(8,128)S(1)}, u32[]{:S(2)}, u32[]{:S(2)}) collective-permute-start(f32[1056,128]{1,0:T(8,128)S(1)} %get-tuple-element.47), channel_id=1, source_target_pairs={{0,1},{1,0},{2,3},{3,2},{4,5},{5,4},{6,7},{7,6},{8,9},{9,8},{10,11... | collective-permute-start | bytes 1622024 | tf_op jit(solution)/shard_map/ppermute | solution.py:388
  63.8 1.6 %collective-permute-done.26.far = f32[1056,128]{1,0:T(8,128)S(1)} collective-permute-done((f32[1056,128]{1,0:T(8,128)S(1)}, f32[1056,128]{1,0:T(8,128)S(1)}, u32[]{:S(2)}, u32[]{:S(2)}) %collective-permute-start.26) | collective-permute-done | bytes 540704 | tf_op jit(solution)/shard_map/ppermute | solution.py:388
  (59 shorter events, 9.6 us)
Async XLA Ops:
  1.1 4.6 %collective-permute-start = (bf16[136,512]{1,0:T(8,128)(2,1)S(1)}, bf16[136,512]{1,0:T(8,128)(2,1)S(1)}, u32[]{:S(2)}, u32[]{:S(2)}) collective-permute-start(bf16[136,512]{1,0:T(8,128)(2,1)S(1)} %tag.1.refs_0_), channel_id=1, source_target_pairs={{0,4},{1,5},{4,8},{5,9},{8,12},{9,13},{12,14},{13,15},{14,10},{15,... | collective-permute-start | bytes 417800 | tf_op jit(solution)/shard_map/ppermute | solution.py:391
  2.4 4.6 %collective-permute-start.3 = (bf16[136,512]{1,0:T(8,128)(2,1)S(1)}, bf16[136,512]{1,0:T(8,128)(2,1)S(1)}, u32[]{:S(2)}, u32[]{:S(2)}) collective-permute-start(bf16[136,512]{1,0:T(8,128)(2,1)S(1)} %tag.1.refs_0_), channel_id=1, source_target_pairs={{4,0},{5,1},{8,4},{9,5},{12,8},{13,9},{14,12},{15,13},{10,14},{11,... | collective-permute-start | bytes 417800 | tf_op jit(solution)/shard_map/ppermute | solution.py:392
  5.7 3.9 %collective-permute-start.1 = (bf16[136,512]{1,0:T(8,128)(2,1)S(1)}, bf16[136,512]{1,0:T(8,128)(2,1)S(1)}, u32[]{:S(2)}, u32[]{:S(2)}) collective-permute-start(bf16[136,512]{1,0:T(8,128)(2,1)S(1)} %collective-permute-done.refs_2_), channel_id=1, source_target_pairs={{0,4},{1,5},{4,8},{5,9},{8,12},{9,13},{12,14},{13,15},{14,10},{15,... | collective-permute-start | bytes 417800 | tf_op jit(solution)/shard_map/ppermute | solution.py:391
  7.0 4.2 %collective-permute-start.4 = (bf16[136,512]{1,0:T(8,128)(2,1)S(1)}, bf16[136,512]{1,0:T(8,128)(2,1)S(1)}, u32[]{:S(2)}, u32[]{:S(2)}) collective-permute-start(bf16[136,512]{1,0:T(8,128)(2,1)S(1)} %collective-permute-done.3.refs_3_), channel_id=1, source_target_pairs={{4,0},{5,1},{8,4},{9,5},{12,8},{13,9},{14,12},{15,13},{10,14},{11,... | collective-permute-start | bytes 417800 | tf_op jit(solution)/shard_map/ppermute | solution.py:392
  9.6 5.2 %collective-permute-start.2 = (bf16[136,512]{1,0:T(8,128)(2,1)S(1)}, bf16[136,512]{1,0:T(8,128)(2,1)S(1)}, u32[]{:S(2)}, u32[]{:S(2)}) collective-permute-start(bf16[136,512]{1,0:T(8,128)(2,1)S(1)} %collective-permute-done.1.refs_6_), channel_id=1, source_target_pairs={{0,4},{1,5},{4,8},{5,9},{8,12},{9,13},{12,14},{13,15},{14,10},{15,... | collective-permute-start | bytes 417800 | tf_op jit(solution)/shard_map/ppermute | solution.py:391
  11.2 6.1 %collective-permute-start.5 = (bf16[136,512]{1,0:T(8,128)(2,1)S(1)}, bf16[136,512]{1,0:T(8,128)(2,1)S(1)}, u32[]{:S(2)}, u32[]{:S(2)}) collective-permute-start(bf16[136,512]{1,0:T(8,128)(2,1)S(1)} %collective-permute-done.4.refs_7_), channel_id=1, source_target_pairs={{4,0},{5,1},{8,4},{9,5},{12,8},{13,9},{14,12},{15,13},{10,14},{11,... | collective-permute-start | bytes 417800 | tf_op jit(solution)/shard_map/ppermute | solution.py:392
  11.3 7.6 %collective-permute-start.12 = (bf16[136,512]{1,0:T(8,128)(2,1)S(1)}, bf16[136,512]{1,0:T(8,128)(2,1)S(1)}, u32[]{:S(2)}, u32[]{:S(2)}) collective-permute-start(bf16[136,512]{1,0:T(8,128)(2,1)S(1)} %tag.1.refs_0_), channel_id=1, source_target_pairs={{0,1},{1,0},{2,3},{3,2},{4,5},{5,4},{6,7},{7,6},{8,9},{9,8},{10,11... | collective-permute-start | bytes 417800 | tf_op jit(solution)/shard_map/ppermute | solution.py:388
  14.3 6.0 %collective-permute-start.13 = (bf16[136,512]{1,0:T(8,128)(2,1)S(1)}, bf16[136,512]{1,0:T(8,128)(2,1)S(1)}, u32[]{:S(2)}, u32[]{:S(2)}) collective-permute-start(bf16[136,512]{1,0:T(8,128)(2,1)S(1)} %collective-permute-done.refs_2_), channel_id=1, source_target_pairs={{0,1},{1,0},{2,3},{3,2},{4,5},{5,4},{6,7},{7,6},{8,9},{9,8},{10,11... | collective-permute-start | bytes 417800 | tf_op jit(solution)/shard_map/ppermute | solution.py:388
  14.3 6.2 %collective-permute-start.14 = (bf16[136,512]{1,0:T(8,128)(2,1)S(1)}, bf16[136,512]{1,0:T(8,128)(2,1)S(1)}, u32[]{:S(2)}, u32[]{:S(2)}) collective-permute-start(bf16[136,512]{1,0:T(8,128)(2,1)S(1)} %collective-permute-done.3.refs_3_), channel_id=1, source_target_pairs={{0,1},{1,0},{2,3},{3,2},{4,5},{5,4},{6,7},{7,6},{8,9},{9,8},{10,11... | collective-permute-start | bytes 417800 | tf_op jit(solution)/shard_map/ppermute | solution.py:388
  14.8 6.2 %collective-permute-start.15 = (bf16[136,512]{1,0:T(8,128)(2,1)S(1)}, bf16[136,512]{1,0:T(8,128)(2,1)S(1)}, u32[]{:S(2)}, u32[]{:S(2)}) collective-permute-start(bf16[136,512]{1,0:T(8,128)(2,1)S(1)} %collective-permute-done.1.refs_6_), channel_id=1, source_target_pairs={{0,1},{1,0},{2,3},{3,2},{4,5},{5,4},{6,7},{7,6},{8,9},{9,8},{10,11... | collective-permute-start | bytes 417800 | tf_op jit(solution)/shard_map/ppermute | solution.py:388
  17.3 7.6 %collective-permute-start.16 = (bf16[136,512]{1,0:T(8,128)(2,1)S(1)}, bf16[136,512]{1,0:T(8,128)(2,1)S(1)}, u32[]{:S(2)}, u32[]{:S(2)}) collective-permute-start(bf16[136,512]{1,0:T(8,128)(2,1)S(1)} %collective-permute-done.4.refs_7_), channel_id=1, source_target_pairs={{0,1},{1,0},{2,3},{3,2},{4,5},{5,4},{6,7},{7,6},{8,9},{9,8},{10,11... | collective-permute-start | bytes 417800 | tf_op jit(solution)/shard_map/ppermute | solution.py:388
  20.4 6.8 %collective-permute-start.6 = (bf16[136,512]{1,0:T(8,128)(2,1)S(1)}, bf16[136,512]{1,0:T(8,128)(2,1)S(1)}, u32[]{:S(2)}, u32[]{:S(2)}) collective-permute-start(bf16[136,512]{1,0:T(8,128)(2,1)S(1)} %collective-permute-done.2.refs_0_), channel_id=1, source_target_pairs={{0,1},{1,0},{2,3},{3,2},{4,5},{5,4},{6,7},{7,6},{8,9},{9,8},{10,11... | collective-permute-start | bytes 417800 | tf_op jit(solution)/shard_map/ppermute | solution.py:388
  21.0 6.3 %collective-permute-start.7 = (bf16[136,512]{1,0:T(8,128)(2,1)S(1)}, bf16[136,512]{1,0:T(8,128)(2,1)S(1)}, u32[]{:S(2)}, u32[]{:S(2)}) collective-permute-start(bf16[136,512]{1,0:T(8,128)(2,1)S(1)} %collective-permute-done.5.refs_1_), channel_id=1, source_target_pairs={{0,1},{1,0},{2,3},{3,2},{4,5},{5,4},{6,7},{7,6},{8,9},{9,8},{10,11... | collective-permute-start | bytes 417800 | tf_op jit(solution)/shard_map/ppermute | solution.py:388
  22.8 4.5 %collective-permute-start.10 = (bf16[72,512]{1,0:T(8,128)(2,1)S(1)}, bf16[72,512]{1,0:T(8,128)(2,1)S(1)}, u32[]{:S(2)}, u32[]{:S(2)}) collective-permute-start(bf16[72,512]{1,0:T(8,128)(2,1)S(1)} %collective-permute-done.8.refs_4_), channel_id=1, source_target_pairs={{0,1},{1,0},{2,3},{3,2},{4,5},{5,4},{6,7},{7,6},{8,9},{9,8},{10,11... | collective-permute-start | bytes 221192 | tf_op jit(solution)/shard_map/ppermute | solution.py:388
  29.5 8.1 %collective-permute-start.17 = (bf16[128,1024]{1,0:T(8,128)(2,1)S(1)}, bf16[128,1024]{1,0:T(8,128)(2,1)S(1)}, u32[]{:S(2)}, u32[]{:S(2)}) collective-permute-start(bf16[128,1024]{1,0:T(8,128)(2,1)S(1)} %get-tuple-element.30.mine), channel_id=1, source_target_pairs={{0,4},{1,5},{4,8},{5,9},{8,12},{9,13},{12,14},{13,15},{14,10},{15,... | collective-permute-start | bytes 786440 | tf_op jit(solution)/shard_map/ppermute | solution.py:391
  32.0 7.9 %collective-permute-start.21 = (bf16[128,1024]{1,0:T(8,128)(2,1)S(1)}, bf16[128,1024]{1,0:T(8,128)(2,1)S(1)}, u32[]{:S(2)}, u32[]{:S(2)}) collective-permute-start(bf16[128,1024]{1,0:T(8,128)(2,1)S(1)} %get-tuple-element.30.mine), channel_id=1, source_target_pairs={{4,0},{5,1},{8,4},{9,5},{12,8},{13,9},{14,12},{15,13},{10,14},{11,... | collective-permute-start | bytes 786440 | tf_op jit(solution)/shard_map/ppermute | solution.py:392
  32.0 7.9 %collective-permute-start.25 = (bf16[128,1024]{1,0:T(8,128)(2,1)S(1)}, bf16[128,1024]{1,0:T(8,128)(2,1)S(1)}, u32[]{:S(2)}, u32[]{:S(2)}) collective-permute-start(bf16[128,1024]{1,0:T(8,128)(2,1)S(1)} %get-tuple-element.30.mine), channel_id=1, source_target_pairs={{0,1},{1,0},{2,3},{3,2},{4,5},{5,4},{6,7},{7,6},{8,9},{9,8},{10,11... | collective-permute-start | bytes 786440 | tf_op jit(solution)/shard_map/ppermute | solution.py:388
  37.6 7.0 %collective-permute-start.18 = (bf16[128,1024]{1,0:T(8,128)(2,1)S(1)}, bf16[128,1024]{1,0:T(8,128)(2,1)S(1)}, u32[]{:S(2)}, u32[]{:S(2)}) collective-permute-start(bf16[128,1024]{1,0:T(8,128)(2,1)S(1)} %collective-permute-done.17.refs_0_), channel_id=1, source_target_pairs={{0,4},{1,5},{4,8},{5,9},{8,12},{9,13},{12,14},{13,15},{14,10},{15,... | collective-permute-start | bytes 786440 | tf_op jit(solution)/shard_map/ppermute | solution.py:391
  39.8 7.0 %collective-permute-start.22 = (bf16[128,1024]{1,0:T(8,128)(2,1)S(1)}, bf16[128,1024]{1,0:T(8,128)(2,1)S(1)}, u32[]{:S(2)}, u32[]{:S(2)}) collective-permute-start(bf16[128,1024]{1,0:T(8,128)(2,1)S(1)} %collective-permute-done.21.refs_1_), channel_id=1, source_target_pairs={{4,0},{5,1},{8,4},{9,5},{12,8},{13,9},{14,12},{15,13},{10,14},{11,... | collective-permute-start | bytes 786440 | tf_op jit(solution)/shard_map/ppermute | solution.py:392
  44.6 8.3 %collective-permute-start.19 = (bf16[128,1024]{1,0:T(8,128)(2,1)S(1)}, bf16[128,1024]{1,0:T(8,128)(2,1)S(1)}, u32[]{:S(2)}, u32[]{:S(2)}) collective-permute-start(bf16[128,1024]{1,0:T(8,128)(2,1)S(1)} %collective-permute-done.18.refs_0_), channel_id=1, source_target_pairs={{0,4},{1,5},{4,8},{5,9},{8,12},{9,13},{12,14},{13,15},{14,10},{15,... | collective-permute-start | bytes 786440 | tf_op jit(solution)/shard_map/ppermute | solution.py:391
  46.8 7.6 %collective-permute-start.23 = (bf16[128,1024]{1,0:T(8,128)(2,1)S(1)}, bf16[128,1024]{1,0:T(8,128)(2,1)S(1)}, u32[]{:S(2)}, u32[]{:S(2)}) collective-permute-start(bf16[128,1024]{1,0:T(8,128)(2,1)S(1)} %collective-permute-done.22.refs_1_), channel_id=1, source_target_pairs={{4,0},{5,1},{8,4},{9,5},{12,8},{13,9},{14,12},{15,13},{10,14},{11,... | collective-permute-start | bytes 786440 | tf_op jit(solution)/shard_map/ppermute | solution.py:392
  52.9 4.7 %collective-permute-start.20 = (bf16[64,1024]{1,0:T(8,128)(2,1)S(1)}, bf16[64,1024]{1,0:T(8,128)(2,1)S(1)}, u32[]{:S(2)}, u32[]{:S(2)}) collective-permute-start(bf16[64,1024]{1,0:T(8,128)(2,1)S(1)} %slice.18), channel_id=1, source_target_pairs={{0,4},{1,5},{4,8},{5,9},{8,12},{9,13},{12,14},{13,15},{14,10},{15,... | collective-permute-start | bytes 393224 | tf_op jit(solution)/shard_map/ppermute | solution.py:391
  54.5 4.2 %collective-permute-start.24 = (bf16[64,1024]{1,0:T(8,128)(2,1)S(1)}, bf16[64,1024]{1,0:T(8,128)(2,1)S(1)}, u32[]{:S(2)}, u32[]{:S(2)}) collective-permute-start(bf16[64,1024]{1,0:T(8,128)(2,1)S(1)} %slice.19), channel_id=1, source_target_pairs={{4,0},{5,1},{8,4},{9,5},{12,8},{13,9},{14,12},{15,13},{10,14},{11,... | collective-permute-start | bytes 393224 | tf_op jit(solution)/shard_map/ppermute | solution.py:392
  60.3 5.0 %collective-permute-start.26 = (f32[1056,128]{1,0:T(8,128)S(1)}, f32[1056,128]{1,0:T(8,128)S(1)}, u32[]{:S(2)}, u32[]{:S(2)}) collective-permute-start(f32[1056,128]{1,0:T(8,128)S(1)} %get-tuple-element.47), channel_id=1, source_target_pairs={{0,1},{1,0},{2,3},{3,2},{4,5},{5,4},{6,7},{7,6},{8,9},{9,8},{10,11... | collective-permute-start | bytes 1622024 | tf_op jit(solution)/shard_map/ppermute | solution.py:388
  (10 other events, 100.9 us)
where the time goes:
time: 66.8 us; the launch traced here: 66.7 us
  starting transfers between devices  28.4 us (43%)
  Pallas kernels  19.7 us (29%)
  waiting for transfers between devices  18.3 us (27%)
    pallas_call x9, Pallas kernels, call(): pl.pallas_call(kernel, out_shape=outs, in_specs=specs, out_specs=jax.tree...  18.7 us
    ppermute x8, waiting for transfers between devices, both_ways(): fore = lax.ppermute(fore, 'frame', ahead)  15.2 us
    ppermute x11, starting transfers between devices, cross_over(): return lax.ppermute(x, 'frame', swap)  14 us
    ppermute x8, starting transfers between devices, both_ways(): fore = lax.ppermute(fore, 'frame', ahead)  13.7 us
    ppermute x11, waiting for transfers between devices, cross_over(): return lax.ppermute(x, 'frame', swap)  1.59 us
    ppermute x8, waiting for transfers between devices, both_ways(): aft = lax.ppermute(aft, 'frame', behind)  1.51 us
  transfers between devices with their start and end apart: 27, of which 9 were waited for; matrix products, arithmetic and copies ran while one was open for 0% of the time, Pallas kernels for 20%

commit v1 on v0

--- a/solution.py
+++ b/solution.py
@@ -124,8 +124,7 @@
 
 RUN = 64
 PAD = 8
-GROUP = 4
-LATE = 2
+GROUP = 2
 WIDE = 256
 PAIR = 2 * HEAD_DIM
 BF16 = jnp.bfloat16
@@ -264,11 +263,15 @@
 
 def early_kernel(n_pieces, rows, *refs):
     pieces = [(ref, places(ref.shape)) for ref in refs[:n_pieces]]
-    stacks, w_kv, tops, totals, accs, picked, keys, values, scores, probs, count = refs[n_pieces:]
+    stacks, w_kv, *old = refs[n_pieces : len(refs) - 9]
+    tops, totals, accs, picked, keys, values, scores, probs, count = refs[len(refs) - 9 :]
     mine = (lax.axis_index("frame") * rows) // (L // NB) + 1
-    tops[...] = jnp.full(tops.shape, NEG, F32)
-    totals[...] = jnp.zeros(totals.shape, F32)
-    accs[...] = jnp.zeros(accs.shape, F32)
+    if old:
+        tops[...], totals[...] = old[0][...], old[1][...]
+    else:
+        tops[...] = jnp.full(tops.shape, NEG, F32)
+        totals[...] = jnp.zeros(totals.shape, F32)
+        accs[...] = jnp.zeros(accs.shape, F32)
     found = pick_runs(pieces, mine, picked, count)
     cross_groups(found, GROUP, picked, w_kv, stacks, keys, values, scores, probs, (tops, totals, accs))
 
@@ -284,7 +287,7 @@
         pieces.append((ref, places(ref.shape) or half))
     tops[...], totals[...] = old_tops[...], old_totals[...]
     found = pick_runs(pieces, mine, picked, count)
-    cross_groups(found, LATE, picked, w_kv, stacks, keys, values, scores, probs, (tops, totals, accs))
+    cross_groups(found, GROUP, picked, w_kv, stacks, keys, values, scores, probs, (tops, totals, accs))
     finish(accs, totals, joined)
     mixed = latents[...].astype(F32) + jnp.dot(joined[...], w_out[...], preferred_element_type=F32)
     mixed_out[...] = mixed
@@ -398,13 +401,16 @@
         return fore, aft
 
     def ring(x):
-        fore, aft = x, x
-        found = []
+        cut = x.shape[0] // 2
+        red, blue = (x[:cut], x[cut:]), (x[cut:], x[:cut])
+        reds, blues = [], []
         for _ in range(1, chips // 2):
-            fore, aft = both_ways(fore, aft)
-            found.append([fore, aft])
-        cut = x.shape[0] // 2
-        return found + [list(both_ways(fore[:cut], aft[cut:]))]
+            red = both_ways(*red)
+            blue = both_ways(*blue)
+            reds.append(list(red))
+            blues.append(list(blue))
+        reds.append(list(both_ways(*red)))
+        return reds, blues
 
     def gather(tagged):
         cut = tagged.shape[0] // 2 + PAD // 2
@@ -439,34 +445,38 @@
         ]
 
     pieces = gather(tagged)
-    soon = [piece for group in pieces[:-2] for piece in group]
-    late = [piece for group in pieces[-2:] for piece in group]
-    kept = call(
-        functools.partial(early_kernel, len(soon), rows), soon + [stacks, w_kv], state(rows),
-        [VMEM((2 * len(soon) + GROUP, RUN, channels), BF16), *work(GROUP * RUN, rows), pltpu.SMEM((1,), jnp.int32)],
-        1 << 30, 16,
-    )
+    late = pieces[-2] + pieces[-1]
+    kept = []
+    for soon in [pieces[0] + pieces[1], *pieces[2:-2]]:
+        n = len(soon)
+        kept = call(
+            functools.partial(early_kernel, n, rows), soon + [stacks, w_kv, *kept], state(rows),
+            [VMEM((2 * n + GROUP, RUN, channels), BF16), *work(GROUP * RUN, rows), pltpu.SMEM((1,), jnp.int32)],
+            1 << 30, 16, {n + 2: 0, n + 3: 1, n + 4: 2} if kept else None,
+        )
     n = len(late)
     mixed, normed, *_ = call(
         functools.partial(cross_kernel, n),
         late + [latents, stacks, w_kv, w_cross_out, *kept],
         (VMEM((rows, width), F32), VMEM((rows, width), BF16), *state(rows)),
         [
-            VMEM((2 * n + GROUP, RUN, channels), BF16), *work(LATE * RUN, rows),
+            VMEM((2 * n + GROUP, RUN, channels), BF16), *work(GROUP * RUN, rows),
             VMEM((rows, width), BF16), pltpu.SMEM((1,), jnp.int32),
         ],
         4 << 30, 16, {n + 4: 2, n + 5: 3, n + 6: 4},
     )
-    arrivals = ring(normed)
+    reds, blues = ring(normed)
+    arrivals = [reds[0]] + [blue + red for blue, red in zip(blues, reds[1:-1])] + [blues[-1], reds[-1]]
     stacks, *kept = call(
         first_kernel, [normed, cross_over(normed), w_self_qkv],
         (VMEM((pairs, PAIR, 4 * rows), BF16), *state(2 * rows)), work(rows, 2 * rows), 1 << 30, 16,
     )
     for sources in arrivals[:-1]:
         n = len(sources)
+        keys = sum(source.shape[0] for source in sources)
         kept = call(
             functools.partial(next_kernel, n), sources + [w_self_qkv, stacks, *kept],
-            state(2 * rows), work(n * rows, 2 * rows), n << 30, 20, {n + 2: 0, n + 3: 1, n + 4: 2},
+            state(2 * rows), work(keys, 2 * rows), n << 29, 20, {n + 2: 0, n + 3: 1, n + 4: 2},
         )
     sources = arrivals[-1]
     n = len(sources)

time: 66.8 us -> 66 us (0.988)
  the two profiles are of different devices: /device:TPU:13 before, /device:TPU:0 now
where the time goes in v1:
time: 66 us; the launch traced here: 65.4 us
  starting transfers between devices  27 us (41%)
  Pallas kernels  19.4 us (29%)
  waiting for transfers between devices  18.7 us (28%)
    ppermute x11, starting transfers between devices, both_ways(): fore = lax.ppermute(fore, 'frame', ahead)  25 us
    pallas_call x11, Pallas kernels, call(): pl.pallas_call(kernel, out_shape=outs, in_specs=specs, out_specs=jax.tree...  18.3 us
    ppermute x11, waiting for transfers between devices, both_ways(): fore = lax.ppermute(fore, 'frame', ahead)  13.1 us
    ppermute x11, waiting for transfers between devices, both_ways(): aft = lax.ppermute(aft, 'frame', behind)  3.62 us
    ppermute x11, waiting for transfers between devices, cross_over(): return lax.ppermute(x, 'frame', swap)  1.95 us
  transfers between devices with their start and end apart: 33, of which 13 were waited for; matrix products, arithmetic and copies ran while one was open for 0% of the time, Pallas kernels for 22%

profile of v1, /device:TPU:0, one launch (start us, length us, event | category | flops | bytes accessed | tf_op | source)
XLA Modules:
  0.0 65.4 jit_solution(7729142259822221257)
XLA Ops:
  1.1 3.1 %collective-permute-start = (bf16[136,512]{1,0:T(8,128)(2,1)S(1)}, bf16[136,512]{1,0:T(8,128)(2,1)S(1)}, u32[]{:S(2)}, u32[]{:S(2)}) collective-permute-start(bf16[136,512]{1,0:T(8,128)(2,1)S(1)} %tag.1.refs_0_), channel_id=1, source_target_pairs={{0,4},{1,5},{4,8},{5,9},{8,12},{9,13},{12,14},{13,15},{14,10},{15,... | collective-permute-start | bytes 417800 | tf_op jit(solution)/shard_map/ppermute | solution.py:394
  4.2 3.6 %collective-permute-done.refs_2_ = bf16[136,512]{1,0:T(8,128)(2,1)S(1)} collective-permute-done((bf16[136,512]{1,0:T(8,128)(2,1)S(1)}, bf16[136,512]{1,0:T(8,128)(2,1)S(1)}, u32[]{:S(2)}, u32[]{:S(2)}) %collective-permute-start) | collective-permute-done | bytes 139296 | tf_op jit(solution)/shard_map/ppermute | solution.py:394
  7.8 1.8 %collective-permute-start.1 = (bf16[136,512]{1,0:T(8,128)(2,1)S(1)}, bf16[136,512]{1,0:T(8,128)(2,1)S(1)}, u32[]{:S(2)}, u32[]{:S(2)}) collective-permute-start(bf16[136,512]{1,0:T(8,128)(2,1)S(1)} %collective-permute-done.refs_2_), channel_id=1, source_target_pairs={{0,4},{1,5},{4,8},{5,9},{8,12},{9,13},{12,14},{13,15},{14,10},{15,... | collective-permute-start | bytes 417800 | tf_op jit(solution)/shard_map/ppermute | solution.py:394
  9.8 3.0 %collective-permute-done.1.refs_0_ = bf16[136,512]{1,0:T(8,128)(2,1)S(1)} collective-permute-done((bf16[136,512]{1,0:T(8,128)(2,1)S(1)}, bf16[136,512]{1,0:T(8,128)(2,1)S(1)}, u32[]{:S(2)}, u32[]{:S(2)}) %collective-permute-start.1) | collective-permute-done | bytes 139296 | tf_op jit(solution)/shard_map/ppermute | solution.py:394
  12.8 1.8 %collective-permute-start.2 = (bf16[136,512]{1,0:T(8,128)(2,1)S(1)}, bf16[136,512]{1,0:T(8,128)(2,1)S(1)}, u32[]{:S(2)}, u32[]{:S(2)}) collective-permute-start(bf16[136,512]{1,0:T(8,128)(2,1)S(1)} %collective-permute-done.1.refs_0_), channel_id=1, source_target_pairs={{0,4},{1,5},{4,8},{5,9},{8,12},{9,13},{12,14},{13,15},{14,10},{15,... | collective-permute-start | bytes 417800 | tf_op jit(solution)/shard_map/ppermute | solution.py:394
  15.4 2.5 %collective-permute-done.2.refs_0_ = bf16[136,512]{1,0:T(8,128)(2,1)S(1)} collective-permute-done((bf16[136,512]{1,0:T(8,128)(2,1)S(1)}, bf16[136,512]{1,0:T(8,128)(2,1)S(1)}, u32[]{:S(2)}, u32[]{:S(2)}) %collective-permute-start.2) | collective-permute-done | bytes 139296 | tf_op jit(solution)/shard_map/ppermute | solution.py:394
  17.9 1.8 %collective-permute-done.5.refs_1_ = bf16[136,512]{1,0:T(8,128)(2,1)S(1)} collective-permute-done((bf16[136,512]{1,0:T(8,128)(2,1)S(1)}, bf16[136,512]{1,0:T(8,128)(2,1)S(1)}, u32[]{:S(2)}, u32[]{:S(2)}) %collective-permute-start.5) | collective-permute-done | bytes 139296 | tf_op jit(solution)/shard_map/ppermute | solution.py:395
  19.9 1.6 %collective-permute-start.8 = (bf16[72,512]{1,0:T(8,128)(2,1)S(1)}, bf16[72,512]{1,0:T(8,128)(2,1)S(1)}, u32[]{:S(2)}, u32[]{:S(2)}) collective-permute-start(bf16[72,512]{1,0:T(8,128)(2,1)S(1)} %slice.18), channel_id=1, source_target_pairs={{0,4},{1,5},{4,8},{5,9},{8,12},{9,13},{12,14},{13,15},{14,10},{15,... | collective-permute-start | bytes 221192 | tf_op jit(solution)/shard_map/ppermute | solution.py:394
  22.5 1.4 %shard_map.83 = (f32[8,256]{1,0:T(8,128)S(1)}, f32[8,256]{1,0:T(8,128)S(1)}, f32[1024,128]{1,0:T(8,128)S(1)}) custom-call(bf16[136,512]{1,0:T(8,128)(2,1)S(1)} %tag.1.refs_0_, bf16[136,512]{1,0:T(8,128)(2,1)S(1)} %collective-permute-done.14.refs_1_, bf16[136,512]{1,0:T(8,128)(2,1)S(1)} %collective-permute-done.refs_2_, ...), custom_call_target="tpu_custom_call" | custom-call | flops 1073741824 | bytes 1048576 | tf_op jit(solution)/shard_map/pallas_call | solution.py:369
  28.4 2.6 %collective-permute-start.17 = (bf16[64,1024]{1,0:T(8,128)(2,1)S(1)}, bf16[64,1024]{1,0:T(8,128)(2,1)S(1)}, u32[]{:S(2)}, u32[]{:S(2)}) collective-permute-start(bf16[64,1024]{1,0:T(8,128)(2,1)S(1)} %get-tuple-element.62), channel_id=1, source_target_pairs={{0,4},{1,5},{4,8},{5,9},{8,12},{9,13},{12,14},{13,15},{14,10},{15,... | collective-permute-start | bytes 393224 | tf_op jit(solution)/shard_map/ppermute | solution.py:394
  31.0 2.0 %collective-permute-start.26 = (bf16[64,1024]{1,0:T(8,128)(2,1)S(1)}, bf16[64,1024]{1,0:T(8,128)(2,1)S(1)}, u32[]{:S(2)}, u32[]{:S(2)}) collective-permute-start(bf16[64,1024]{1,0:T(8,128)(2,1)S(1)} %get-tuple-element.61), channel_id=1, source_target_pairs={{0,4},{1,5},{4,8},{5,9},{8,12},{9,13},{12,14},{13,15},{14,10},{15,... | collective-permute-start | bytes 393224 | tf_op jit(solution)/shard_map/ppermute | solution.py:394
  33.0 1.9 %collective-permute-done.17.refs_0_ = bf16[64,1024]{1,0:T(8,128)(2,1)S(1)} collective-permute-done((bf16[64,1024]{1,0:T(8,128)(2,1)S(1)}, bf16[64,1024]{1,0:T(8,128)(2,1)S(1)}, u32[]{:S(2)}, u32[]{:S(2)}) %collective-permute-start.17) | collective-permute-done | bytes 131104 | tf_op jit(solution)/shard_map/ppermute | solution.py:394
  34.9 2.5 %collective-permute-start.18 = (bf16[64,1024]{1,0:T(8,128)(2,1)S(1)}, bf16[64,1024]{1,0:T(8,128)(2,1)S(1)}, u32[]{:S(2)}, u32[]{:S(2)}) collective-permute-start(bf16[64,1024]{1,0:T(8,128)(2,1)S(1)} %collective-permute-done.17.refs_0_), channel_id=1, source_target_pairs={{0,4},{1,5},{4,8},{5,9},{8,12},{9,13},{12,14},{13,15},{14,10},{15,... | collective-permute-start | bytes 393224 | tf_op jit(solution)/shard_map/ppermute | solution.py:394
  37.7 2.5 %collective-permute-start.27 = (bf16[64,1024]{1,0:T(8,128)(2,1)S(1)}, bf16[64,1024]{1,0:T(8,128)(2,1)S(1)}, u32[]{:S(2)}, u32[]{:S(2)}) collective-permute-start(bf16[64,1024]{1,0:T(8,128)(2,1)S(1)} %collective-permute-done.26.refs_0_), channel_id=1, source_target_pairs={{0,4},{1,5},{4,8},{5,9},{8,12},{9,13},{12,14},{13,15},{14,10},{15,... | collective-permute-start | bytes 393224 | tf_op jit(solution)/shard_map/ppermute | solution.py:394
  40.9 2.5 %collective-permute-start.19 = (bf16[64,1024]{1,0:T(8,128)(2,1)S(1)}, bf16[64,1024]{1,0:T(8,128)(2,1)S(1)}, u32[]{:S(2)}, u32[]{:S(2)}) collective-permute-start(bf16[64,1024]{1,0:T(8,128)(2,1)S(1)} %collective-permute-done.18.refs_2_), channel_id=1, source_target_pairs={{0,4},{1,5},{4,8},{5,9},{8,12},{9,13},{12,14},{13,15},{14,10},{15,... | collective-permute-start | bytes 393224 | tf_op jit(solution)/shard_map/ppermute | solution.py:394
  44.1 2.5 %collective-permute-start.28 = (bf16[64,1024]{1,0:T(8,128)(2,1)S(1)}, bf16[64,1024]{1,0:T(8,128)(2,1)S(1)}, u32[]{:S(2)}, u32[]{:S(2)}) collective-permute-start(bf16[64,1024]{1,0:T(8,128)(2,1)S(1)} %collective-permute-done.27.refs_0_), channel_id=1, source_target_pairs={{0,4},{1,5},{4,8},{5,9},{8,12},{9,13},{12,14},{13,15},{14,10},{15,... | collective-permute-start | bytes 393224 | tf_op jit(solution)/shard_map/ppermute | solution.py:394
  46.6 2.0 %shard_map.86 = (bf16[8,128,512]{2,1,0:T(8,128)(2,1)S(1)}, f32[8,512]{1,0:T(8,128)S(1)}, f32[8,512]{1,0:T(8,128)S(1)}, f32[1024,256]{1,0:T(8,128)S(1)}) custom-call(bf16[128,1024]{1,0:T(8,128)(2,1)S(1)} %get-tuple-element.39.mine, bf16[128,1024]{1,0:T(8,128)(2,1)S(1)} %collective-permute-done.25.other, bf16[1024,3072]{1,0:T(8,128)(2,1)S(1)} %bitcast.1), custom_call_target="tpu_custom_call" | custom-call | flops 1073741824 | bytes 1048576 | tf_op jit(solution)/shard_map/pallas_call | solution.py:369
  48.6 1.7 %shard_map.87 = (f32[8,512]{1,0:T(8,128)S(1)}, f32[8,512]{1,0:T(8,128)S(1)}, f32[1024,256]{1,0:T(8,128)S(1)}) custom-call(bf16[64,1024]{1,0:T(8,128)(2,1)S(1)} %collective-permute-done.17.refs_0_, bf16[64,1024]{1,0:T(8,128)(2,1)S(1)} %collective-permute-done.21.refs_1_, ...), custom_call_target="tpu_custom_call", output_to_operand_aliasing={{0}: (4, {}), {1}: (5, {}), {2}: (6, {})} | custom-call | flops 1073741824 | bytes 1048576 | tf_op jit(solution)/shard_map/pallas_call | solution.py:369
  50.3 3.0 %shard_map.88 = (f32[8,512]{1,0:T(8,128)S(1)}, f32[8,512]{1,0:T(8,128)S(1)}, f32[1024,256]{1,0:T(8,128)S(1)}) custom-call(bf16[64,1024]{1,0:T(8,128)(2,1)S(1)} %collective-permute-done.26.refs_0_, bf16[64,1024]{1,0:T(8,128)(2,1)S(1)} %collective-permute-done.29.refs_1_, ...), custom_call_target="tpu_custom_call", output_to_operand_aliasing={{0}: (6, {}), {1}: (7, {}), {2}: (8, {})} | custom-call | flops 2147483648 | bytes 1048576 | tf_op jit(solution)/shard_map/pallas_call | solution.py:369
  53.3 2.1 %collective-permute-start.20 = (bf16[64,1024]{1,0:T(8,128)(2,1)S(1)}, bf16[64,1024]{1,0:T(8,128)(2,1)S(1)}, u32[]{:S(2)}, u32[]{:S(2)}) collective-permute-start(bf16[64,1024]{1,0:T(8,128)(2,1)S(1)} %collective-permute-done.19.refs_2_), channel_id=1, source_target_pairs={{0,4},{1,5},{4,8},{5,9},{8,12},{9,13},{12,14},{13,15},{14,10},{15,... | collective-permute-start | bytes 393224 | tf_op jit(solution)/shard_map/ppermute | solution.py:394
  55.4 3.0 %shard_map.89 = (f32[8,512]{1,0:T(8,128)S(1)}, f32[8,512]{1,0:T(8,128)S(1)}, f32[1024,256]{1,0:T(8,128)S(1)}) custom-call(bf16[64,1024]{1,0:T(8,128)(2,1)S(1)} %collective-permute-done.27.refs_0_, bf16[64,1024]{1,0:T(8,128)(2,1)S(1)} %collective-permute-done.30.refs_1_, ...), custom_call_target="tpu_custom_call", output_to_operand_aliasing={{0}: (6, {}), {1}: (7, {}), {2}: (8, {})} | custom-call | flops 2147483648 | bytes 1048576 | tf_op jit(solution)/shard_map/pallas_call | solution.py:369
  58.5 1.7 %shard_map.90 = (f32[8,512]{1,0:T(8,128)S(1)}, f32[8,512]{1,0:T(8,128)S(1)}, f32[1024,256]{1,0:T(8,128)S(1)}) custom-call(bf16[64,1024]{1,0:T(8,128)(2,1)S(1)} %collective-permute-done.28.refs_0_, bf16[64,1024]{1,0:T(8,128)(2,1)S(1)} %collective-permute-done.31.refs_1_, ...), custom_call_target="tpu_custom_call", output_to_operand_aliasing={{0}: (4, {}), {1}: (5, {}), {2}: (6, {})} | custom-call | flops 1073741824 | bytes 1048576 | tf_op jit(solution)/shard_map/pallas_call | solution.py:369
  60.4 1.7 %shard_map.91 = (f32[8,512]{1,0:T(8,128)S(1)}, f32[8,512]{1,0:T(8,128)S(1)}, f32[1024,256]{1,0:T(8,128)S(1)}, f32[1056,128]{1,0:T(8,128)S(1)}) custom-call(bf16[64,1024]{1,0:T(8,128)(2,1)S(1)} %collective-permute-done.20.refs_0_, bf16[64,1024]{1,0:T(8,128)(2,1)S(1)} %collective-permute-done.24.refs_1_, ...), custom_call_target="tpu_custom_call", output_to_operand_aliasing={{0}: (4, {}), {1}: (5, {}), {2}: (6, {})} | custom-call | flops 1073741824 | bytes 1048576 | tf_op jit(solution)/shard_map/pallas_call | solution.py:369
  62.1 1.9 %collective-permute-done.32.far = f32[1056,128]{1,0:T(8,128)S(1)} collective-permute-done((f32[1056,128]{1,0:T(8,128)S(1)}, f32[1056,128]{1,0:T(8,128)S(1)}, u32[]{:S(2)}, u32[]{:S(2)}) %collective-permute-start.32) | collective-permute-done | bytes 540704 | tf_op jit(solution)/shard_map/ppermute | solution.py:391
  (72 shorter events, 10.8 us)
Async XLA Ops:
  1.1 6.7 %collective-permute-start = (bf16[136,512]{1,0:T(8,128)(2,1)S(1)}, bf16[136,512]{1,0:T(8,128)(2,1)S(1)}, u32[]{:S(2)}, u32[]{:S(2)}) collective-permute-start(bf16[136,512]{1,0:T(8,128)(2,1)S(1)} %tag.1.refs_0_), channel_id=1, source_target_pairs={{0,4},{1,5},{4,8},{5,9},{8,12},{9,13},{12,14},{13,15},{14,10},{15,... | collective-permute-start | bytes 417800 | tf_op jit(solution)/shard_map/ppermute | solution.py:394
  4.2 5.4 %collective-permute-start.3 = (bf16[136,512]{1,0:T(8,128)(2,1)S(1)}, bf16[136,512]{1,0:T(8,128)(2,1)S(1)}, u32[]{:S(2)}, u32[]{:S(2)}) collective-permute-start(bf16[136,512]{1,0:T(8,128)(2,1)S(1)} %tag.1.refs_0_), channel_id=1, source_target_pairs={{4,0},{5,1},{8,4},{9,5},{12,8},{13,9},{14,12},{15,13},{10,14},{11,... | collective-permute-start | bytes 417800 | tf_op jit(solution)/shard_map/ppermute | solution.py:395
  7.8 5.1 %collective-permute-start.1 = (bf16[136,512]{1,0:T(8,128)(2,1)S(1)}, bf16[136,512]{1,0:T(8,128)(2,1)S(1)}, u32[]{:S(2)}, u32[]{:S(2)}) collective-permute-start(bf16[136,512]{1,0:T(8,128)(2,1)S(1)} %collective-permute-done.refs_2_), channel_id=1, source_target_pairs={{0,4},{1,5},{4,8},{5,9},{8,12},{9,13},{12,14},{13,15},{14,10},{15,... | collective-permute-start | bytes 417800 | tf_op jit(solution)/shard_map/ppermute | solution.py:394
  9.6 5.1 %collective-permute-start.4 = (bf16[136,512]{1,0:T(8,128)(2,1)S(1)}, bf16[136,512]{1,0:T(8,128)(2,1)S(1)}, u32[]{:S(2)}, u32[]{:S(2)}) collective-permute-start(bf16[136,512]{1,0:T(8,128)(2,1)S(1)} %collective-permute-done.3.refs_3_), channel_id=1, source_target_pairs={{4,0},{5,1},{8,4},{9,5},{12,8},{13,9},{14,12},{15,13},{10,14},{11,... | collective-permute-start | bytes 417800 | tf_op jit(solution)/shard_map/ppermute | solution.py:395
  12.8 5.1 %collective-permute-start.2 = (bf16[136,512]{1,0:T(8,128)(2,1)S(1)}, bf16[136,512]{1,0:T(8,128)(2,1)S(1)}, u32[]{:S(2)}, u32[]{:S(2)}) collective-permute-start(bf16[136,512]{1,0:T(8,128)(2,1)S(1)} %collective-permute-done.1.refs_0_), channel_id=1, source_target_pairs={{0,4},{1,5},{4,8},{5,9},{8,12},{9,13},{12,14},{13,15},{14,10},{15,... | collective-permute-start | bytes 417800 | tf_op jit(solution)/shard_map/ppermute | solution.py:394
  14.8 6.7 %collective-permute-start.15 = (bf16[136,512]{1,0:T(8,128)(2,1)S(1)}, bf16[136,512]{1,0:T(8,128)(2,1)S(1)}, u32[]{:S(2)}, u32[]{:S(2)}) collective-permute-start(bf16[136,512]{1,0:T(8,128)(2,1)S(1)} %collective-permute-done.refs_2_), channel_id=1, source_target_pairs={{0,1},{1,0},{2,3},{3,2},{4,5},{5,4},{6,7},{7,6},{8,9},{9,8},{10,11... | collective-permute-start | bytes 417800 | tf_op jit(solution)/shard_map/ppermute | solution.py:391
  15.3 6.6 %collective-permute-start.16 = (bf16[136,512]{1,0:T(8,128)(2,1)S(1)}, bf16[136,512]{1,0:T(8,128)(2,1)S(1)}, u32[]{:S(2)}, u32[]{:S(2)}) collective-permute-start(bf16[136,512]{1,0:T(8,128)(2,1)S(1)} %collective-permute-done.3.refs_3_), channel_id=1, source_target_pairs={{0,1},{1,0},{2,3},{3,2},{4,5},{5,4},{6,7},{7,6},{8,9},{9,8},{10,11... | collective-permute-start | bytes 417800 | tf_op jit(solution)/shard_map/ppermute | solution.py:391
  19.7 6.2 %collective-permute-start.13 = (bf16[136,512]{1,0:T(8,128)(2,1)S(1)}, bf16[136,512]{1,0:T(8,128)(2,1)S(1)}, u32[]{:S(2)}, u32[]{:S(2)}) collective-permute-start(bf16[136,512]{1,0:T(8,128)(2,1)S(1)} %collective-permute-done.4.refs_1_), channel_id=1, source_target_pairs={{0,1},{1,0},{2,3},{3,2},{4,5},{5,4},{6,7},{7,6},{8,9},{9,8},{10,11... | collective-permute-start | bytes 417800 | tf_op jit(solution)/shard_map/ppermute | solution.py:391
  22.0 5.4 %collective-permute-start.6 = (bf16[136,512]{1,0:T(8,128)(2,1)S(1)}, bf16[136,512]{1,0:T(8,128)(2,1)S(1)}, u32[]{:S(2)}, u32[]{:S(2)}) collective-permute-start(bf16[136,512]{1,0:T(8,128)(2,1)S(1)} %collective-permute-done.2.refs_0_), channel_id=1, source_target_pairs={{0,1},{1,0},{2,3},{3,2},{4,5},{5,4},{6,7},{7,6},{8,9},{9,8},{10,11... | collective-permute-start | bytes 417800 | tf_op jit(solution)/shard_map/ppermute | solution.py:391
  22.0 5.4 %collective-permute-start.7 = (bf16[136,512]{1,0:T(8,128)(2,1)S(1)}, bf16[136,512]{1,0:T(8,128)(2,1)S(1)}, u32[]{:S(2)}, u32[]{:S(2)}) collective-permute-start(bf16[136,512]{1,0:T(8,128)(2,1)S(1)} %collective-permute-done.5.refs_1_), channel_id=1, source_target_pairs={{0,1},{1,0},{2,3},{3,2},{4,5},{5,4},{6,7},{7,6},{8,9},{9,8},{10,11... | collective-permute-start | bytes 417800 | tf_op jit(solution)/shard_map/ppermute | solution.py:391
  28.4 6.5 %collective-permute-start.17 = (bf16[64,1024]{1,0:T(8,128)(2,1)S(1)}, bf16[64,1024]{1,0:T(8,128)(2,1)S(1)}, u32[]{:S(2)}, u32[]{:S(2)}) collective-permute-start(bf16[64,1024]{1,0:T(8,128)(2,1)S(1)} %get-tuple-element.62), channel_id=1, source_target_pairs={{0,4},{1,5},{4,8},{5,9},{8,12},{9,13},{12,14},{13,15},{14,10},{15,... | collective-permute-start | bytes 393224 | tf_op jit(solution)/shard_map/ppermute | solution.py:394
  31.0 6.4 %collective-permute-start.21 = (bf16[64,1024]{1,0:T(8,128)(2,1)S(1)}, bf16[64,1024]{1,0:T(8,128)(2,1)S(1)}, u32[]{:S(2)}, u32[]{:S(2)}) collective-permute-start(bf16[64,1024]{1,0:T(8,128)(2,1)S(1)} %get-tuple-element.61), channel_id=1, source_target_pairs={{4,0},{5,1},{8,4},{9,5},{12,8},{13,9},{14,12},{15,13},{10,14},{11,... | collective-permute-start | bytes 393224 | tf_op jit(solution)/shard_map/ppermute | solution.py:395
  31.0 6.7 %collective-permute-start.26 = (bf16[64,1024]{1,0:T(8,128)(2,1)S(1)}, bf16[64,1024]{1,0:T(8,128)(2,1)S(1)}, u32[]{:S(2)}, u32[]{:S(2)}) collective-permute-start(bf16[64,1024]{1,0:T(8,128)(2,1)S(1)} %get-tuple-element.61), channel_id=1, source_target_pairs={{0,4},{1,5},{4,8},{5,9},{8,12},{9,13},{12,14},{13,15},{14,10},{15,... | collective-permute-start | bytes 393224 | tf_op jit(solution)/shard_map/ppermute | solution.py:394
  33.0 7.2 %collective-permute-start.29 = (bf16[64,1024]{1,0:T(8,128)(2,1)S(1)}, bf16[64,1024]{1,0:T(8,128)(2,1)S(1)}, u32[]{:S(2)}, u32[]{:S(2)}) collective-permute-start(bf16[64,1024]{1,0:T(8,128)(2,1)S(1)} %get-tuple-element.62), channel_id=1, source_target_pairs={{4,0},{5,1},{8,4},{9,5},{12,8},{13,9},{14,12},{15,13},{10,14},{11,... | collective-permute-start | bytes 393224 | tf_op jit(solution)/shard_map/ppermute | solution.py:395
  33.0 13.5 %collective-permute-start.25 = (bf16[128,1024]{1,0:T(8,128)(2,1)S(1)}, bf16[128,1024]{1,0:T(8,128)(2,1)S(1)}, u32[]{:S(2)}, u32[]{:S(2)}) collective-permute-start(bf16[128,1024]{1,0:T(8,128)(2,1)S(1)} %get-tuple-element.39.mine), channel_id=1, source_target_pairs={{0,1},{1,0},{2,3},{3,2},{4,5},{5,4},{6,7},{7,6},{8,9},{9,8},{10,11... | collective-permute-start | bytes 786440 | tf_op jit(solution)/shard_map/ppermute | solution.py:391
  34.9 6.0 %collective-permute-start.18 = (bf16[64,1024]{1,0:T(8,128)(2,1)S(1)}, bf16[64,1024]{1,0:T(8,128)(2,1)S(1)}, u32[]{:S(2)}, u32[]{:S(2)}) collective-permute-start(bf16[64,1024]{1,0:T(8,128)(2,1)S(1)} %collective-permute-done.17.refs_0_), channel_id=1, source_target_pairs={{0,4},{1,5},{4,8},{5,9},{8,12},{9,13},{12,14},{13,15},{14,10},{15,... | collective-permute-start | bytes 393224 | tf_op jit(solution)/shard_map/ppermute | solution.py:394
  37.4 6.3 %collective-permute-start.22 = (bf16[64,1024]{1,0:T(8,128)(2,1)S(1)}, bf16[64,1024]{1,0:T(8,128)(2,1)S(1)}, u32[]{:S(2)}, u32[]{:S(2)}) collective-permute-start(bf16[64,1024]{1,0:T(8,128)(2,1)S(1)} %collective-permute-done.21.refs_1_), channel_id=1, source_target_pairs={{4,0},{5,1},{8,4},{9,5},{12,8},{13,9},{14,12},{15,13},{10,14},{11,... | collective-permute-start | bytes 393224 | tf_op jit(solution)/shard_map/ppermute | solution.py:395
  37.7 6.4 %collective-permute-start.27 = (bf16[64,1024]{1,0:T(8,128)(2,1)S(1)}, bf16[64,1024]{1,0:T(8,128)(2,1)S(1)}, u32[]{:S(2)}, u32[]{:S(2)}) collective-permute-start(bf16[64,1024]{1,0:T(8,128)(2,1)S(1)} %collective-permute-done.26.refs_0_), channel_id=1, source_target_pairs={{0,4},{1,5},{4,8},{5,9},{8,12},{9,13},{12,14},{13,15},{14,10},{15,... | collective-permute-start | bytes 393224 | tf_op jit(solution)/shard_map/ppermute | solution.py:394
  40.2 6.4 %collective-permute-start.30 = (bf16[64,1024]{1,0:T(8,128)(2,1)S(1)}, bf16[64,1024]{1,0:T(8,128)(2,1)S(1)}, u32[]{:S(2)}, u32[]{:S(2)}) collective-permute-start(bf16[64,1024]{1,0:T(8,128)(2,1)S(1)} %collective-permute-done.29.refs_1_), channel_id=1, source_target_pairs={{4,0},{5,1},{8,4},{9,5},{12,8},{13,9},{14,12},{15,13},{10,14},{11,... | collective-permute-start | bytes 393224 | tf_op jit(solution)/shard_map/ppermute | solution.py:395
  40.9 12.4 %collective-permute-start.19 = (bf16[64,1024]{1,0:T(8,128)(2,1)S(1)}, bf16[64,1024]{1,0:T(8,128)(2,1)S(1)}, u32[]{:S(2)}, u32[]{:S(2)}) collective-permute-start(bf16[64,1024]{1,0:T(8,128)(2,1)S(1)} %collective-permute-done.18.refs_2_), channel_id=1, source_target_pairs={{0,4},{1,5},{4,8},{5,9},{8,12},{9,13},{12,14},{13,15},{14,10},{15,... | collective-permute-start | bytes 393224 | tf_op jit(solution)/shard_map/ppermute | solution.py:394
  43.7 11.7 %collective-permute-start.23 = (bf16[64,1024]{1,0:T(8,128)(2,1)S(1)}, bf16[64,1024]{1,0:T(8,128)(2,1)S(1)}, u32[]{:S(2)}, u32[]{:S(2)}) collective-permute-start(bf16[64,1024]{1,0:T(8,128)(2,1)S(1)} %collective-permute-done.22.refs_3_), channel_id=1, source_target_pairs={{4,0},{5,1},{8,4},{9,5},{12,8},{13,9},{14,12},{15,13},{10,14},{11,... | collective-permute-start | bytes 393224 | tf_op jit(solution)/shard_map/ppermute | solution.py:395
  44.1 14.4 %collective-permute-start.28 = (bf16[64,1024]{1,0:T(8,128)(2,1)S(1)}, bf16[64,1024]{1,0:T(8,128)(2,1)S(1)}, u32[]{:S(2)}, u32[]{:S(2)}) collective-permute-start(bf16[64,1024]{1,0:T(8,128)(2,1)S(1)} %collective-permute-done.27.refs_0_), channel_id=1, source_target_pairs={{0,4},{1,5},{4,8},{5,9},{8,12},{9,13},{12,14},{13,15},{14,10},{15,... | collective-permute-start | bytes 393224 | tf_op jit(solution)/shard_map/ppermute | solution.py:394
  46.5 11.9 %collective-permute-start.31 = (bf16[64,1024]{1,0:T(8,128)(2,1)S(1)}, bf16[64,1024]{1,0:T(8,128)(2,1)S(1)}, u32[]{:S(2)}, u32[]{:S(2)}) collective-permute-start(bf16[64,1024]{1,0:T(8,128)(2,1)S(1)} %collective-permute-done.30.refs_1_), channel_id=1, source_target_pairs={{4,0},{5,1},{8,4},{9,5},{12,8},{13,9},{14,12},{15,13},{10,14},{11,... | collective-permute-start | bytes 393224 | tf_op jit(solution)/shard_map/ppermute | solution.py:395
  53.3 6.8 %collective-permute-start.20 = (bf16[64,1024]{1,0:T(8,128)(2,1)S(1)}, bf16[64,1024]{1,0:T(8,128)(2,1)S(1)}, u32[]{:S(2)}, u32[]{:S(2)}) collective-permute-start(bf16[64,1024]{1,0:T(8,128)(2,1)S(1)} %collective-permute-done.19.refs_2_), channel_id=1, source_target_pairs={{0,4},{1,5},{4,8},{5,9},{8,12},{9,13},{12,14},{13,15},{14,10},{15,... | collective-permute-start | bytes 393224 | tf_op jit(solution)/shard_map/ppermute | solution.py:394
  (16 other events, 125.6 us)

commit v2 on v1

--- a/solution.py
+++ b/solution.py
@@ -127,6 +127,7 @@
 GROUP = 2
 WIDE = 256
 PAIR = 2 * HEAD_DIM
+LARGE = 2.0**30
 BF16 = jnp.bfloat16
 F32 = jnp.float32
 VMEM = pltpu.VMEM
@@ -154,15 +155,13 @@
             at += n
 
 
-def project(normed, weights, at, width, keys, values):
+def project(normed, weights, key_at, value_at, keys, values):
     n = normed.shape[0]
-    for j in range(width // WIDE):
+    for j in range(keys.shape[1] // WIDE):
         cols = slice(j * WIDE, (j + 1) * WIDE)
-        k = jnp.dot(normed, weights[:, at + j * WIDE : at + (j + 1) * WIDE], preferred_element_type=F32)
+        k = jnp.dot(normed, weights[:, key_at + j * WIDE : key_at + (j + 1) * WIDE], preferred_element_type=F32)
         keys[:n, cols] = k.astype(BF16)
-        v = jnp.dot(
-            normed, weights[:, at + width + j * WIDE : at + width + (j + 1) * WIDE], preferred_element_type=F32
-        )
+        v = jnp.dot(normed, weights[:, value_at + j * WIDE : value_at + (j + 1) * WIDE], preferred_element_type=F32)
         values[cols, :n] = v.astype(BF16).T
 
 
@@ -191,16 +190,43 @@
         totals[i : i + 1] = total
         probs[i, :n] = weights.astype(BF16)
     for i in range(pairs):
-        out = jnp.dot(values[i * PAIR : (i + 1) * PAIR, :n], probs[i, :n], preferred_element_type=F32)
         if old is not None:
             fade = jnp.exp(old[0][i : i + 1] - tops[i : i + 1])
         for h in range(2):
             rows = slice(i * PAIR + h * HEAD_DIM, i * PAIR + (h + 1) * HEAD_DIM)
             cols = slice(h * half, (h + 1) * half)
-            part = out[h * HEAD_DIM : (h + 1) * HEAD_DIM, cols]
+            part = jnp.dot(values[rows, :n], probs[i, :n, cols], preferred_element_type=F32)
             if old is not None:
                 part = part + old[2][rows, :] * fade[:, cols]
             accs[rows, :] = part
+
+
+def attend_lazily(n, stacks, keys, values, scores, probs, old, new):
+    pairs, half = stacks.shape[0], stacks.shape[2] // 2
+    tops, totals, accs = new
+    old_tops, old_totals, old_accs = old
+    kept_tops, kept_totals = old_tops[...], old_totals[...]
+    largest = None
+    for i in range(pairs):
+        for h in range(2):
+            cols = slice(h * half, (h + 1) * half)
+            score = jnp.dot(keys[:n, i * PAIR : (i + 1) * PAIR], stacks[i][:, cols], preferred_element_type=F32)
+            weights = jnp.exp(score - kept_tops[i : i + 1, cols])
+            total = jnp.sum(weights, axis=0, keepdims=True)
+            totals[i : i + 1, cols] = kept_totals[i : i + 1, cols] + total
+            probs[i, :n, cols] = weights.astype(BF16)
+            largest = total if largest is None else jnp.maximum(largest, total)
+    for i in range(pairs):
+        for h in range(2):
+            cols = slice(h * half, (h + 1) * half)
+            rows = slice(i * PAIR + h * HEAD_DIM, i * PAIR + (h + 1) * HEAD_DIM)
+            out = jnp.dot(values[rows, :n], probs[i, :n, cols], preferred_element_type=F32)
+            accs[rows, :] = out + old_accs[rows, :]
+    tops[...] = kept_tops
+
+    @pl.when(jnp.logical_not(jnp.max(largest) < LARGE))
+    def _():
+        attend(n, None, stacks, keys, values, scores, probs, (old_tops[...], old_totals[...], old_accs), new)
 
 
 def tag_kernel(segment, frames, out, labels, sems):
@@ -311,7 +337,7 @@
     for j in range(width // WIDE):
         query = jnp.dot(both, w_qkv[:, j * WIDE : (j + 1) * WIDE], preferred_element_type=F32).astype(BF16)
         fill_stacks(stacks, j, [(query.astype(F32) * scale).astype(BF16)])
-    project(mine[...], w_qkv, width, width, keys, values)
+    project(mine[...], w_qkv, width, 2 * width, keys, values)
     attend(rows, None, stacks, keys, values, scores, probs, None, (tops, totals, accs))
 
 
@@ -320,43 +346,49 @@
     (w_qkv, stacks, old_tops, old_totals, old_accs, tops, totals, accs, keys, values, scores, probs) = refs[n_pieces:]
     width = accs.shape[0]
     block = jnp.concatenate([s[...] for s in sources], axis=0)
-    project(block, w_qkv, width, width, keys, values)
-    old = (old_tops[...], old_totals[...], old_accs)
-    attend(block.shape[0], None, stacks, keys, values, scores, probs, old, (tops, totals, accs))
-
-
-def final_kernel(tops, totals, accs, far, mixed, w_out, out, joined, merged, sums):
-    width, rows = far.shape[0] - 2 * 2 * tops.shape[0], far.shape[1]
-    for i in range(tops.shape[0]):
-        for h in range(2):
-            at = 2 * i + h
-            here = slice(h * 2 * rows, h * 2 * rows + rows)
-            lines = slice(i * PAIR + h * HEAD_DIM, i * PAIR + (h + 1) * HEAD_DIM)
-            near_top, far_top = tops[i : i + 1, here], far[width + at : width + at + 1]
-            top = jnp.maximum(near_top, far_top)
-            near_fade, far_fade = jnp.exp(near_top - top), jnp.exp(far_top - top)
-            far_total = far[width + 2 * tops.shape[0] + at : width + 2 * tops.shape[0] + at + 1]
-            sums[i : i + 1, h * rows : (h + 1) * rows] = totals[i : i + 1, here] * near_fade + far_total * far_fade
-            merged[lines] = accs[lines, :rows] * near_fade + far[lines] * far_fade
-    finish(merged, sums, joined)
-    out[...] = (mixed[...] + jnp.dot(joined[...], w_out[...], preferred_element_type=F32)).astype(BF16)
-
-
-def last_kernel(n_pieces, *refs):
+    project(block, w_qkv, width, 2 * width, keys, values)
+    old = (old_tops, old_totals, old_accs)
+    attend_lazily(block.shape[0], stacks, keys, values, scores, probs, old, (tops, totals, accs))
+
+
+def last_kernel(n_pieces, part, *refs):
     sources = refs[:n_pieces]
     (w_qkv, stacks, old_tops, old_totals, old_accs, tops, totals, accs, away,
      keys, values, scores, probs) = refs[n_pieces:]
-    next_kernel(n_pieces, *sources, w_qkv, stacks, old_tops, old_totals, old_accs, tops, totals, accs,
-                keys, values, scores, probs)
-    width, rows = accs.shape[0], accs.shape[1] // 2
-    away[:width] = accs[:, rows:]
-    for i in range(tops.shape[0]):
+    pairs, lines, rows = tops.shape[0], accs.shape[0], accs.shape[1] // 2
+    width = old_accs.shape[0]
+    block = jnp.concatenate([s[...] for s in sources], axis=0)
+    project(block, w_qkv, width + part * lines, 2 * width + part * lines, keys, values)
+    span = slice(part * pairs, (part + 1) * pairs)
+    old = (old_tops.at[span], old_totals.at[span], old_accs.at[part * lines : (part + 1) * lines])
+    attend_lazily(
+        block.shape[0], stacks.at[span], keys, values, scores, probs, old, (tops, totals, accs)
+    )
+    away[:lines] = accs[:, rows:]
+    for i in range(pairs):
         for h in range(2):
             there = slice(h * 2 * rows + rows, (h + 1) * 2 * rows)
-            at = 2 * i + h
-            away[width + at : width + at + 1] = tops[i : i + 1, there]
-            at += 2 * tops.shape[0]
-            away[width + at : width + at + 1] = totals[i : i + 1, there]
+            at = lines + 2 * i + h
+            away[at : at + 1] = tops[i : i + 1, there]
+            away[at + 2 * pairs : at + 2 * pairs + 1] = totals[i : i + 1, there]
+
+
+def final_kernel(part, tops, totals, accs, far, base, w_out, out, joined, merged, sums):
+    pairs, lines, rows = tops.shape[0], accs.shape[0], accs.shape[1] // 2
+    for i in range(pairs):
+        for h in range(2):
+            at = lines + 2 * i + h
+            here = slice(h * 2 * rows, h * 2 * rows + rows)
+            span = slice(i * PAIR + h * HEAD_DIM, i * PAIR + (h + 1) * HEAD_DIM)
+            near_top, far_top = tops[i : i + 1, here], far[at : at + 1]
+            top = jnp.maximum(near_top, far_top)
+            near_fade, far_fade = jnp.exp(near_top - top), jnp.exp(far_top - top)
+            far_total = far[at + 2 * pairs : at + 2 * pairs + 1]
+            sums[i : i + 1, h * rows : (h + 1) * rows] = totals[i : i + 1, here] * near_fade + far_total * far_fade
+            merged[span] = accs[span, :rows] * near_fade + far[span] * far_fade
+    finish(merged, sums, joined)
+    share = jnp.dot(joined[...], w_out[part * lines : (part + 1) * lines], preferred_element_type=F32)
+    out[...] = (base[...] + share).astype(out.dtype)
 
 
 def on_chip(x):
@@ -414,13 +446,15 @@
 
     def gather(tagged):
         cut = tagged.shape[0] // 2 + PAD // 2
-        found = [[tagged, cross_over(tagged)]]
+        near, far = [[tagged]], [[cross_over(tagged)]]
         fore, aft = tagged, tagged
-        for _ in range(1, chips // 2):
+        for hop in range(1, chips // 2 + 1):
+            if hop == chips // 2:
+                fore, aft = fore[:cut], aft[-cut:]
             fore, aft = both_ways(fore, aft)
-            found.append([fore, aft, *swapped(fore, aft)])
-        fore, aft = both_ways(fore[:cut], aft[-cut:])
-        return found + [[fore, aft, cross_over(fore), cross_over(aft)]]
+            near.append([fore, aft])
+            far.append(list(swapped(fore, aft)))
+        return near, far
 
     pairs = width // PAIR
     tagged = pl.pallas_call(
@@ -444,10 +478,10 @@
             VMEM((pairs, n, 2 * queries), F32), VMEM((pairs, n, 2 * queries), BF16),
         ]
 
-    pieces = gather(tagged)
-    late = pieces[-2] + pieces[-1]
+    near, far = gather(tagged)
+    late = far[-2] + near[-1] + far[-1]
     kept = []
-    for soon in [pieces[0] + pieces[1], *pieces[2:-2]]:
+    for soon in [near[0] + far[0] + near[1]] + [far[hop - 1] + near[hop] for hop in range(2, chips // 2)]:
         n = len(soon)
         kept = call(
             functools.partial(early_kernel, n, rows), soon + [stacks, w_kv, *kept], state(rows),
@@ -476,21 +510,36 @@
         keys = sum(source.shape[0] for source in sources)
         kept = call(
             functools.partial(next_kernel, n), sources + [w_self_qkv, stacks, *kept],
-            state(2 * rows), work(keys, 2 * rows), n << 29, 20, {n + 2: 0, n + 3: 1, n + 4: 2},
+            state(2 * rows), work(keys, 2 * rows), n << 29, 20,
         )
     sources = arrivals[-1]
     n = len(sources)
-    *kept, away = call(
-        functools.partial(last_kernel, n), sources + [w_self_qkv, stacks, *kept],
-        (*state(2 * rows), VMEM((width + 4 * pairs, rows), F32)), work(rows, 2 * rows), 1 << 30, 20,
-        {n + 2: 0, n + 3: 1, n + 4: 2},
-    )
-    return call(
-        final_kernel, [*kept, cross_over(away), mixed, w_self_out],
-        jax.ShapeDtypeStruct((rows, width), BF16),
-        [VMEM((rows, width), BF16), VMEM((width, rows), F32), VMEM((pairs, 2 * rows), F32)],
-        1 << 30, 12,
-    )
+    parts, lines = pairs // 2, width // 2
+    done = []
+    for part in range(2):
+        *near, away = call(
+            functools.partial(last_kernel, n, part), sources + [w_self_qkv, stacks, *kept],
+            (
+                VMEM((parts, 4 * rows), F32), VMEM((parts, 4 * rows), F32), VMEM((lines, 2 * rows), F32),
+                VMEM((lines + 4 * parts, rows), F32),
+            ),
+            [
+                VMEM((rows, lines), BF16), VMEM((lines, rows), BF16),
+                VMEM((parts, rows, 4 * rows), F32), VMEM((parts, rows, 4 * rows), BF16),
+            ],
+            1 << 29, 16,
+        )
+        far = cross_over(away)
+        done.append([*near, far])
+    out = mixed
+    for part in range(2):
+        whole = jax.ShapeDtypeStruct((rows, width), BF16) if part else VMEM((rows, width), F32)
+        out = call(
+            functools.partial(final_kernel, part), [*done[part], out, w_self_out], whole,
+            [VMEM((rows, lines), BF16), VMEM((lines, rows), F32), VMEM((parts, 2 * rows), F32)],
+            1 << 29, 12,
+        )
+    return out
 
 
 def solution(mesh):

time: 66 us -> 70.3 us (1.065)
  Pallas kernels: 19.4 us -> 24.9 us
  waiting for transfers between devices: 18.7 us -> 16.7 us
  starting transfers between devices: 27 us -> 27.8 us
    pallas_call x11 -> x14, Pallas kernels: 18.3 us -> 23.9 us  [call(): pl.pallas_call(kernel, out_shape=outs, in_specs=specs, out_specs=jax.tree...]
    ppermute x11, waiting for transfers between devices: 3.62 us -> 2.31 us  [both_ways(): aft = lax.ppermute(aft, 'frame', behind)]
    ppermute x11 -> x12, starting transfers between devices: 1.11 us -> 1.67 us  [cross_over(): return lax.ppermute(x, 'frame', swap)]
    ppermute x11 -> x12, waiting for transfers between devices: 1.95 us -> 1.82 us  [cross_over(): return lax.ppermute(x, 'frame', swap)]
  transfers between devices with their start and end apart: 33 -> 34, of which waited for: 13 -> 13; matrix products, arithmetic and copies ran while one was open for 0% -> 0% of each run, Pallas kernels for 22% -> 29%
where the time goes in v2:
time: 70.3 us; the launch traced here: 69.7 us
  starting transfers between devices  27.8 us (40%)
  Pallas kernels  24.9 us (35%)
  waiting for transfers between devices  16.7 us (24%)
    ppermute x11, starting transfers between devices, both_ways(): fore = lax.ppermute(fore, 'frame', ahead)  25.2 us
    pallas_call x14, Pallas kernels, call(): pl.pallas_call(kernel, out_shape=outs, in_specs=specs, out_specs=jax.tree...  23.9 us
    ppermute x11, waiting for transfers between devices, both_ways(): fore = lax.ppermute(fore, 'frame', ahead)  12.6 us
    ppermute x11, waiting for transfers between devices, both_ways(): aft = lax.ppermute(aft, 'frame', behind)  2.31 us
    ppermute x12, waiting for transfers between devices, cross_over(): return lax.ppermute(x, 'frame', swap)  1.82 us
    ppermute x12, starting transfers between devices, cross_over(): return lax.ppermute(x, 'frame', swap)  1.67 us
  transfers between devices with their start and end apart: 34, of which 13 were waited for; matrix products, arithmetic and copies ran while one was open for 0% of the time, Pallas kernels for 29%

profile of v2, /device:TPU:0, one launch (start us, length us, event | category | flops | bytes accessed | tf_op | source)
XLA Modules:
  0.0 69.7 jit_solution(12642840143445398187)
XLA Ops:
  1.1 3.1 %collective-permute-start = (bf16[136,512]{1,0:T(8,128)(2,1)S(1)}, bf16[136,512]{1,0:T(8,128)(2,1)S(1)}, u32[]{:S(2)}, u32[]{:S(2)}) collective-permute-start(bf16[136,512]{1,0:T(8,128)(2,1)S(1)} %tag.1.refs_0_), channel_id=1, source_target_pairs={{0,4},{1,5},{4,8},{5,9},{8,12},{9,13},{12,14},{13,15},{14,10},{15,... | collective-permute-start | bytes 417800 | tf_op jit(solution)/shard_map/ppermute | solution.py:426
  4.2 3.6 %collective-permute-done.refs_2_ = bf16[136,512]{1,0:T(8,128)(2,1)S(1)} collective-permute-done((bf16[136,512]{1,0:T(8,128)(2,1)S(1)}, bf16[136,512]{1,0:T(8,128)(2,1)S(1)}, u32[]{:S(2)}, u32[]{:S(2)}) %collective-permute-start) | collective-permute-done | bytes 139296 | tf_op jit(solution)/shard_map/ppermute | solution.py:426
  7.8 1.8 %collective-permute-start.1 = (bf16[136,512]{1,0:T(8,128)(2,1)S(1)}, bf16[136,512]{1,0:T(8,128)(2,1)S(1)}, u32[]{:S(2)}, u32[]{:S(2)}) collective-permute-start(bf16[136,512]{1,0:T(8,128)(2,1)S(1)} %collective-permute-done.refs_2_), channel_id=1, source_target_pairs={{0,4},{1,5},{4,8},{5,9},{8,12},{9,13},{12,14},{13,15},{14,10},{15,... | collective-permute-start | bytes 417800 | tf_op jit(solution)/shard_map/ppermute | solution.py:426
  9.8 3.0 %collective-permute-done.1.refs_2_ = bf16[136,512]{1,0:T(8,128)(2,1)S(1)} collective-permute-done((bf16[136,512]{1,0:T(8,128)(2,1)S(1)}, bf16[136,512]{1,0:T(8,128)(2,1)S(1)}, u32[]{:S(2)}, u32[]{:S(2)}) %collective-permute-start.1) | collective-permute-done | bytes 139296 | tf_op jit(solution)/shard_map/ppermute | solution.py:426
  12.8 1.8 %collective-permute-start.2 = (bf16[136,512]{1,0:T(8,128)(2,1)S(1)}, bf16[136,512]{1,0:T(8,128)(2,1)S(1)}, u32[]{:S(2)}, u32[]{:S(2)}) collective-permute-start(bf16[136,512]{1,0:T(8,128)(2,1)S(1)} %collective-permute-done.1.refs_2_), channel_id=1, source_target_pairs={{0,4},{1,5},{4,8},{5,9},{8,12},{9,13},{12,14},{13,15},{14,10},{15,... | collective-permute-start | bytes 417800 | tf_op jit(solution)/shard_map/ppermute | solution.py:426
  15.5 2.4 %collective-permute-done.2.refs_2_ = bf16[136,512]{1,0:T(8,128)(2,1)S(1)} collective-permute-done((bf16[136,512]{1,0:T(8,128)(2,1)S(1)}, bf16[136,512]{1,0:T(8,128)(2,1)S(1)}, u32[]{:S(2)}, u32[]{:S(2)}) %collective-permute-start.2) | collective-permute-done | bytes 139296 | tf_op jit(solution)/shard_map/ppermute | solution.py:426
  19.7 1.6 %collective-permute-start.8 = (bf16[72,512]{1,0:T(8,128)(2,1)S(1)}, bf16[72,512]{1,0:T(8,128)(2,1)S(1)}, u32[]{:S(2)}, u32[]{:S(2)}) collective-permute-start(bf16[72,512]{1,0:T(8,128)(2,1)S(1)} %slice.18), channel_id=1, source_target_pairs={{0,4},{1,5},{4,8},{5,9},{8,12},{9,13},{12,14},{13,15},{14,10},{15,... | collective-permute-start | bytes 221192 | tf_op jit(solution)/shard_map/ppermute | solution.py:426
  22.3 1.4 %shard_map.84 = (f32[8,256]{1,0:T(8,128)S(1)}, f32[8,256]{1,0:T(8,128)S(1)}, f32[1024,128]{1,0:T(8,128)S(1)}) custom-call(bf16[136,512]{1,0:T(8,128)(2,1)S(1)} %collective-permute-done.14.refs_0_, bf16[136,512]{1,0:T(8,128)(2,1)S(1)} %collective-permute-done.15.refs_1_, ...), custom_call_target="tpu_custom_call", output_to_operand_aliasing={{0}: (6, {}), {1}: (7, {}), {2}: (8, {})} | custom-call | flops 1073741824 | bytes 1048576 | tf_op jit(solution)/shard_map/pallas_call | solution.py:401
  24.1 1.6 %collective-permute-done.9.refs_3_ = bf16[72,512]{1,0:T(8,128)(2,1)S(1)} collective-permute-done((bf16[72,512]{1,0:T(8,128)(2,1)S(1)}, bf16[72,512]{1,0:T(8,128)(2,1)S(1)}, u32[]{:S(2)}, u32[]{:S(2)}) %collective-permute-start.9) | collective-permute-done | bytes 73760 | tf_op jit(solution)/shard_map/ppermute | solution.py:427
  27.9 2.9 %collective-permute-start.17 = (bf16[64,1024]{1,0:T(8,128)(2,1)S(1)}, bf16[64,1024]{1,0:T(8,128)(2,1)S(1)}, u32[]{:S(2)}, u32[]{:S(2)}) collective-permute-start(bf16[64,1024]{1,0:T(8,128)(2,1)S(1)} %get-tuple-element.76), channel_id=1, source_target_pairs={{0,4},{1,5},{4,8},{5,9},{8,12},{9,13},{12,14},{13,15},{14,10},{15,... | collective-permute-start | bytes 393224 | tf_op jit(solution)/shard_map/ppermute | solution.py:426
  30.8 2.0 %collective-permute-start.26 = (bf16[64,1024]{1,0:T(8,128)(2,1)S(1)}, bf16[64,1024]{1,0:T(8,128)(2,1)S(1)}, u32[]{:S(2)}, u32[]{:S(2)}) collective-permute-start(bf16[64,1024]{1,0:T(8,128)(2,1)S(1)} %get-tuple-element.75), channel_id=1, source_target_pairs={{0,4},{1,5},{4,8},{5,9},{8,12},{9,13},{12,14},{13,15},{14,10},{15,... | collective-permute-start | bytes 393224 | tf_op jit(solution)/shard_map/ppermute | solution.py:426
  32.8 1.9 %collective-permute-done.17.refs_0_ = bf16[64,1024]{1,0:T(8,128)(2,1)S(1)} collective-permute-done((bf16[64,1024]{1,0:T(8,128)(2,1)S(1)}, bf16[64,1024]{1,0:T(8,128)(2,1)S(1)}, u32[]{:S(2)}, u32[]{:S(2)}) %collective-permute-start.17) | collective-permute-done | bytes 131104 | tf_op jit(solution)/shard_map/ppermute | solution.py:426
  34.7 2.5 %collective-permute-start.18 = (bf16[64,1024]{1,0:T(8,128)(2,1)S(1)}, bf16[64,1024]{1,0:T(8,128)(2,1)S(1)}, u32[]{:S(2)}, u32[]{:S(2)}) collective-permute-start(bf16[64,1024]{1,0:T(8,128)(2,1)S(1)} %collective-permute-done.17.refs_0_), channel_id=1, source_target_pairs={{0,4},{1,5},{4,8},{5,9},{8,12},{9,13},{12,14},{13,15},{14,10},{15,... | collective-permute-start | bytes 393224 | tf_op jit(solution)/shard_map/ppermute | solution.py:426
  37.5 2.5 %collective-permute-start.27 = (bf16[64,1024]{1,0:T(8,128)(2,1)S(1)}, bf16[64,1024]{1,0:T(8,128)(2,1)S(1)}, u32[]{:S(2)}, u32[]{:S(2)}) collective-permute-start(bf16[64,1024]{1,0:T(8,128)(2,1)S(1)} %collective-permute-done.26.refs_0_), channel_id=1, source_target_pairs={{0,4},{1,5},{4,8},{5,9},{8,12},{9,13},{12,14},{13,15},{14,10},{15,... | collective-permute-start | bytes 393224 | tf_op jit(solution)/shard_map/ppermute | solution.py:426
  40.7 2.5 %collective-permute-start.19 = (bf16[64,1024]{1,0:T(8,128)(2,1)S(1)}, bf16[64,1024]{1,0:T(8,128)(2,1)S(1)}, u32[]{:S(2)}, u32[]{:S(2)}) collective-permute-start(bf16[64,1024]{1,0:T(8,128)(2,1)S(1)} %collective-permute-done.18.refs_2_), channel_id=1, source_target_pairs={{0,4},{1,5},{4,8},{5,9},{8,12},{9,13},{12,14},{13,15},{14,10},{15,... | collective-permute-start | bytes 393224 | tf_op jit(solution)/shard_map/ppermute | solution.py:426
  43.8 2.5 %collective-permute-start.28 = (bf16[64,1024]{1,0:T(8,128)(2,1)S(1)}, bf16[64,1024]{1,0:T(8,128)(2,1)S(1)}, u32[]{:S(2)}, u32[]{:S(2)}) collective-permute-start(bf16[64,1024]{1,0:T(8,128)(2,1)S(1)} %collective-permute-done.27.refs_0_), channel_id=1, source_target_pairs={{0,4},{1,5},{4,8},{5,9},{8,12},{9,13},{12,14},{13,15},{14,10},{15,... | collective-permute-start | bytes 393224 | tf_op jit(solution)/shard_map/ppermute | solution.py:426
  46.4 2.0 %shard_map.87 = (bf16[8,128,512]{2,1,0:T(8,128)(2,1)S(1)}, f32[8,512]{1,0:T(8,128)S(1)}, f32[8,512]{1,0:T(8,128)S(1)}, f32[1024,256]{1,0:T(8,128)S(1)}) custom-call(bf16[128,1024]{1,0:T(8,128)(2,1)S(1)} %get-tuple-element.49.mine, bf16[128,1024]{1,0:T(8,128)(2,1)S(1)} %collective-permute-done.25.other, bf16[1024,3072]{1,0:T(8,128)(2,1)S(1)} %bitcast.1), custom_call_target="tpu_custom_call" | custom-call | flops 1073741824 | bytes 1048576 | tf_op jit(solution)/shard_map/pallas_call | solution.py:401
  48.4 2.6 %shard_map.88 = (f32[8,512]{1,0:T(8,128)S(1)}, f32[8,512]{1,0:T(8,128)S(1)}, f32[1024,256]{1,0:T(8,128)S(1)}) custom-call(bf16[64,1024]{1,0:T(8,128)(2,1)S(1)} %collective-permute-done.17.refs_0_, bf16[64,1024]{1,0:T(8,128)(2,1)S(1)} %collective-permute-done.21.refs_1_, bf16[1024,3072]{1,0:T(8,128)(2,1)S(1)} %bitcast.1, ...), custom_call_target="tpu_custom_call" | custom-call | flops 1073741824 | bytes 1048576 | tf_op jit(solution)/shard_map/pallas_call | solution.py:401
  50.9 4.2 %shard_map.89 = (f32[8,512]{1,0:T(8,128)S(1)}, f32[8,512]{1,0:T(8,128)S(1)}, f32[1024,256]{1,0:T(8,128)S(1)}) custom-call(bf16[64,1024]{1,0:T(8,128)(2,1)S(1)} %collective-permute-done.26.refs_0_, bf16[64,1024]{1,0:T(8,128)(2,1)S(1)} %collective-permute-done.29.refs_1_, bf16[64,1024]{1,0:T(8,128)(2,1)S(1)} %collective-permute-done.18.refs_2_, ...), custom_call_target="tpu_custom_call" | custom-call | flops 2147483648 | bytes 1048576 | tf_op jit(solution)/shard_map/pallas_call | solution.py:401
  55.1 2.1 %collective-permute-start.20 = (bf16[64,1024]{1,0:T(8,128)(2,1)S(1)}, bf16[64,1024]{1,0:T(8,128)(2,1)S(1)}, u32[]{:S(2)}, u32[]{:S(2)}) collective-permute-start(bf16[64,1024]{1,0:T(8,128)(2,1)S(1)} %collective-permute-done.19.refs_2_), channel_id=1, source_target_pairs={{0,4},{1,5},{4,8},{5,9},{8,12},{9,13},{12,14},{13,15},{14,10},{15,... | collective-permute-start | bytes 393224 | tf_op jit(solution)/shard_map/ppermute | solution.py:426
  57.2 4.2 %shard_map.90 = (f32[8,512]{1,0:T(8,128)S(1)}, f32[8,512]{1,0:T(8,128)S(1)}, f32[1024,256]{1,0:T(8,128)S(1)}) custom-call(bf16[64,1024]{1,0:T(8,128)(2,1)S(1)} %collective-permute-done.27.refs_0_, bf16[64,1024]{1,0:T(8,128)(2,1)S(1)} %collective-permute-done.30.refs_1_, bf16[64,1024]{1,0:T(8,128)(2,1)S(1)} %collective-permute-done.19.refs_2_, ...), custom_call_target="tpu_custom_call" | custom-call | flops 2147483648 | bytes 1048576 | tf_op jit(solution)/shard_map/pallas_call | solution.py:401
  61.4 2.4 %shard_map.91 = (f32[8,512]{1,0:T(8,128)S(1)}, f32[8,512]{1,0:T(8,128)S(1)}, f32[1024,256]{1,0:T(8,128)S(1)}) custom-call(bf16[64,1024]{1,0:T(8,128)(2,1)S(1)} %collective-permute-done.28.refs_0_, bf16[64,1024]{1,0:T(8,128)(2,1)S(1)} %collective-permute-done.31.refs_1_, bf16[1024,3072]{1,0:T(8,128)(2,1)S(1)} %bitcast.1, ...), custom_call_target="tpu_custom_call" | custom-call | flops 1073741824 | bytes 1048576 | tf_op jit(solution)/shard_map/pallas_call | solution.py:401
  63.8 1.5 %shard_map.93 = (f32[4,512]{1,0:T(4,128)S(1)}, f32[4,512]{1,0:T(4,128)S(1)}, f32[512,256]{1,0:T(8,128)S(1)}, f32[528,128]{1,0:T(8,128)S(1)}) custom-call(bf16[64,1024]{1,0:T(8,128)(2,1)S(1)} %collective-permute-done.20.refs_0_, bf16[64,1024]{1,0:T(8,128)(2,1)S(1)} %collective-permute-done.24.refs_1_, bf16[1024,3072]{1,0:T(8,128)(2,1)S(1)} %bitcast.1, ...), custom_call_target="tpu_custom_call" | custom-call | flops 536870912 | bytes 1048576 | tf_op jit(solution)/shard_map/pallas_call | solution.py:401
  65.4 1.5 %shard_map.92 = (f32[4,512]{1,0:T(4,128)S(1)}, f32[4,512]{1,0:T(4,128)S(1)}, f32[512,256]{1,0:T(8,128)S(1)}, f32[528,128]{1,0:T(8,128)S(1)}) custom-call(bf16[64,1024]{1,0:T(8,128)(2,1)S(1)} %collective-permute-done.20.refs_0_, bf16[64,1024]{1,0:T(8,128)(2,1)S(1)} %collective-permute-done.24.refs_1_, bf16[1024,3072]{1,0:T(8,128)(2,1)S(1)} %bitcast.1, ...), custom_call_target="tpu_custom_call" | custom-call | flops 536870912 | bytes 1048576 | tf_op jit(solution)/shard_map/pallas_call | solution.py:401
  (77 shorter events, 12.1 us)
Async XLA Ops:
  1.1 6.7 %collective-permute-start = (bf16[136,512]{1,0:T(8,128)(2,1)S(1)}, bf16[136,512]{1,0:T(8,128)(2,1)S(1)}, u32[]{:S(2)}, u32[]{:S(2)}) collective-permute-start(bf16[136,512]{1,0:T(8,128)(2,1)S(1)} %tag.1.refs_0_), channel_id=1, source_target_pairs={{0,4},{1,5},{4,8},{5,9},{8,12},{9,13},{12,14},{13,15},{14,10},{15,... | collective-permute-start | bytes 417800 | tf_op jit(solution)/shard_map/ppermute | solution.py:426
  4.2 5.4 %collective-permute-start.4 = (bf16[136,512]{1,0:T(8,128)(2,1)S(1)}, bf16[136,512]{1,0:T(8,128)(2,1)S(1)}, u32[]{:S(2)}, u32[]{:S(2)}) collective-permute-start(bf16[136,512]{1,0:T(8,128)(2,1)S(1)} %tag.1.refs_0_), channel_id=1, source_target_pairs={{4,0},{5,1},{8,4},{9,5},{12,8},{13,9},{14,12},{15,13},{10,14},{11,... | collective-permute-start | bytes 417800 | tf_op jit(solution)/shard_map/ppermute | solution.py:427
  7.8 5.1 %collective-permute-start.1 = (bf16[136,512]{1,0:T(8,128)(2,1)S(1)}, bf16[136,512]{1,0:T(8,128)(2,1)S(1)}, u32[]{:S(2)}, u32[]{:S(2)}) collective-permute-start(bf16[136,512]{1,0:T(8,128)(2,1)S(1)} %collective-permute-done.refs_2_), channel_id=1, source_target_pairs={{0,4},{1,5},{4,8},{5,9},{8,12},{9,13},{12,14},{13,15},{14,10},{15,... | collective-permute-start | bytes 417800 | tf_op jit(solution)/shard_map/ppermute | solution.py:426
  9.6 5.1 %collective-permute-start.5 = (bf16[136,512]{1,0:T(8,128)(2,1)S(1)}, bf16[136,512]{1,0:T(8,128)(2,1)S(1)}, u32[]{:S(2)}, u32[]{:S(2)}) collective-permute-start(bf16[136,512]{1,0:T(8,128)(2,1)S(1)} %collective-permute-done.4.refs_3_), channel_id=1, source_target_pairs={{4,0},{5,1},{8,4},{9,5},{12,8},{13,9},{14,12},{15,13},{10,14},{11,... | collective-permute-start | bytes 417800 | tf_op jit(solution)/shard_map/ppermute | solution.py:427
  9.8 5.6 %collective-permute-start.16 = (bf16[136,512]{1,0:T(8,128)(2,1)S(1)}, bf16[136,512]{1,0:T(8,128)(2,1)S(1)}, u32[]{:S(2)}, u32[]{:S(2)}) collective-permute-start(bf16[136,512]{1,0:T(8,128)(2,1)S(1)} %tag.1.refs_0_), channel_id=1, source_target_pairs={{0,1},{1,0},{2,3},{3,2},{4,5},{5,4},{6,7},{7,6},{8,9},{9,8},{10,11... | collective-permute-start | bytes 417800 | tf_op jit(solution)/shard_map/ppermute | solution.py:423
  14.8 6.4 %collective-permute-start.14 = (bf16[136,512]{1,0:T(8,128)(2,1)S(1)}, bf16[136,512]{1,0:T(8,128)(2,1)S(1)}, u32[]{:S(2)}, u32[]{:S(2)}) collective-permute-start(bf16[136,512]{1,0:T(8,128)(2,1)S(1)} %collective-permute-done.refs_2_), channel_id=1, source_target_pairs={{0,1},{1,0},{2,3},{3,2},{4,5},{5,4},{6,7},{7,6},{8,9},{9,8},{10,11... | collective-permute-start | bytes 417800 | tf_op jit(solution)/shard_map/ppermute | solution.py:423
  14.8 6.9 %collective-permute-start.15 = (bf16[136,512]{1,0:T(8,128)(2,1)S(1)}, bf16[136,512]{1,0:T(8,128)(2,1)S(1)}, u32[]{:S(2)}, u32[]{:S(2)}) collective-permute-start(bf16[136,512]{1,0:T(8,128)(2,1)S(1)} %collective-permute-done.4.refs_3_), channel_id=1, source_target_pairs={{0,1},{1,0},{2,3},{3,2},{4,5},{5,4},{6,7},{7,6},{8,9},{9,8},{10,11... | collective-permute-start | bytes 417800 | tf_op jit(solution)/shard_map/ppermute | solution.py:423
  15.4 6.4 %collective-permute-start.12 = (bf16[136,512]{1,0:T(8,128)(2,1)S(1)}, bf16[136,512]{1,0:T(8,128)(2,1)S(1)}, u32[]{:S(2)}, u32[]{:S(2)}) collective-permute-start(bf16[136,512]{1,0:T(8,128)(2,1)S(1)} %collective-permute-done.1.refs_2_), channel_id=1, source_target_pairs={{0,1},{1,0},{2,3},{3,2},{4,5},{5,4},{6,7},{7,6},{8,9},{9,8},{10,11... | collective-permute-start | bytes 417800 | tf_op jit(solution)/shard_map/ppermute | solution.py:423
  17.9 7.8 %collective-permute-start.13 = (bf16[136,512]{1,0:T(8,128)(2,1)S(1)}, bf16[136,512]{1,0:T(8,128)(2,1)S(1)}, u32[]{:S(2)}, u32[]{:S(2)}) collective-permute-start(bf16[136,512]{1,0:T(8,128)(2,1)S(1)} %collective-permute-done.5.refs_3_), channel_id=1, source_target_pairs={{0,1},{1,0},{2,3},{3,2},{4,5},{5,4},{6,7},{7,6},{8,9},{9,8},{10,11... | collective-permute-start | bytes 417800 | tf_op jit(solution)/shard_map/ppermute | solution.py:423
  27.9 6.8 %collective-permute-start.17 = (bf16[64,1024]{1,0:T(8,128)(2,1)S(1)}, bf16[64,1024]{1,0:T(8,128)(2,1)S(1)}, u32[]{:S(2)}, u32[]{:S(2)}) collective-permute-start(bf16[64,1024]{1,0:T(8,128)(2,1)S(1)} %get-tuple-element.76), channel_id=1, source_target_pairs={{0,4},{1,5},{4,8},{5,9},{8,12},{9,13},{12,14},{13,15},{14,10},{15,... | collective-permute-start | bytes 393224 | tf_op jit(solution)/shard_map/ppermute | solution.py:426
  30.8 6.4 %collective-permute-start.21 = (bf16[64,1024]{1,0:T(8,128)(2,1)S(1)}, bf16[64,1024]{1,0:T(8,128)(2,1)S(1)}, u32[]{:S(2)}, u32[]{:S(2)}) collective-permute-start(bf16[64,1024]{1,0:T(8,128)(2,1)S(1)} %get-tuple-element.75), channel_id=1, source_target_pairs={{4,0},{5,1},{8,4},{9,5},{12,8},{13,9},{14,12},{15,13},{10,14},{11,... | collective-permute-start | bytes 393224 | tf_op jit(solution)/shard_map/ppermute | solution.py:427
  30.8 6.7 %collective-permute-start.26 = (bf16[64,1024]{1,0:T(8,128)(2,1)S(1)}, bf16[64,1024]{1,0:T(8,128)(2,1)S(1)}, u32[]{:S(2)}, u32[]{:S(2)}) collective-permute-start(bf16[64,1024]{1,0:T(8,128)(2,1)S(1)} %get-tuple-element.75), channel_id=1, source_target_pairs={{0,4},{1,5},{4,8},{5,9},{8,12},{9,13},{12,14},{13,15},{14,10},{15,... | collective-permute-start | bytes 393224 | tf_op jit(solution)/shard_map/ppermute | solution.py:426
  32.8 7.2 %collective-permute-start.29 = (bf16[64,1024]{1,0:T(8,128)(2,1)S(1)}, bf16[64,1024]{1,0:T(8,128)(2,1)S(1)}, u32[]{:S(2)}, u32[]{:S(2)}) collective-permute-start(bf16[64,1024]{1,0:T(8,128)(2,1)S(1)} %get-tuple-element.76), channel_id=1, source_target_pairs={{4,0},{5,1},{8,4},{9,5},{12,8},{13,9},{14,12},{15,13},{10,14},{11,... | collective-permute-start | bytes 393224 | tf_op jit(solution)/shard_map/ppermute | solution.py:427
  32.8 13.5 %collective-permute-start.25 = (bf16[128,1024]{1,0:T(8,128)(2,1)S(1)}, bf16[128,1024]{1,0:T(8,128)(2,1)S(1)}, u32[]{:S(2)}, u32[]{:S(2)}) collective-permute-start(bf16[128,1024]{1,0:T(8,128)(2,1)S(1)} %get-tuple-element.49.mine), channel_id=1, source_target_pairs={{0,1},{1,0},{2,3},{3,2},{4,5},{5,4},{6,7},{7,6},{8,9},{9,8},{10,11... | collective-permute-start | bytes 786440 | tf_op jit(solution)/shard_map/ppermute | solution.py:423
  34.7 6.0 %collective-permute-start.18 = (bf16[64,1024]{1,0:T(8,128)(2,1)S(1)}, bf16[64,1024]{1,0:T(8,128)(2,1)S(1)}, u32[]{:S(2)}, u32[]{:S(2)}) collective-permute-start(bf16[64,1024]{1,0:T(8,128)(2,1)S(1)} %collective-permute-done.17.refs_0_), channel_id=1, source_target_pairs={{0,4},{1,5},{4,8},{5,9},{8,12},{9,13},{12,14},{13,15},{14,10},{15,... | collective-permute-start | bytes 393224 | tf_op jit(solution)/shard_map/ppermute | solution.py:426
  37.2 6.3 %collective-permute-start.22 = (bf16[64,1024]{1,0:T(8,128)(2,1)S(1)}, bf16[64,1024]{1,0:T(8,128)(2,1)S(1)}, u32[]{:S(2)}, u32[]{:S(2)}) collective-permute-start(bf16[64,1024]{1,0:T(8,128)(2,1)S(1)} %collective-permute-done.21.refs_1_), channel_id=1, source_target_pairs={{4,0},{5,1},{8,4},{9,5},{12,8},{13,9},{14,12},{15,13},{10,14},{11,... | collective-permute-start | bytes 393224 | tf_op jit(solution)/shard_map/ppermute | solution.py:427
  37.5 6.4 %collective-permute-start.27 = (bf16[64,1024]{1,0:T(8,128)(2,1)S(1)}, bf16[64,1024]{1,0:T(8,128)(2,1)S(1)}, u32[]{:S(2)}, u32[]{:S(2)}) collective-permute-start(bf16[64,1024]{1,0:T(8,128)(2,1)S(1)} %collective-permute-done.26.refs_0_), channel_id=1, source_target_pairs={{0,4},{1,5},{4,8},{5,9},{8,12},{9,13},{12,14},{13,15},{14,10},{15,... | collective-permute-start | bytes 393224 | tf_op jit(solution)/shard_map/ppermute | solution.py:426
  40.0 6.4 %collective-permute-start.30 = (bf16[64,1024]{1,0:T(8,128)(2,1)S(1)}, bf16[64,1024]{1,0:T(8,128)(2,1)S(1)}, u32[]{:S(2)}, u32[]{:S(2)}) collective-permute-start(bf16[64,1024]{1,0:T(8,128)(2,1)S(1)} %collective-permute-done.29.refs_1_), channel_id=1, source_target_pairs={{4,0},{5,1},{8,4},{9,5},{12,8},{13,9},{14,12},{15,13},{10,14},{11,... | collective-permute-start | bytes 393224 | tf_op jit(solution)/shard_map/ppermute | solution.py:427
  40.7 14.4 %collective-permute-start.19 = (bf16[64,1024]{1,0:T(8,128)(2,1)S(1)}, bf16[64,1024]{1,0:T(8,128)(2,1)S(1)}, u32[]{:S(2)}, u32[]{:S(2)}) collective-permute-start(bf16[64,1024]{1,0:T(8,128)(2,1)S(1)} %collective-permute-done.18.refs_2_), channel_id=1, source_target_pairs={{0,4},{1,5},{4,8},{5,9},{8,12},{9,13},{12,14},{13,15},{14,10},{15,... | collective-permute-start | bytes 393224 | tf_op jit(solution)/shard_map/ppermute | solution.py:426
  43.5 13.7 %collective-permute-start.23 = (bf16[64,1024]{1,0:T(8,128)(2,1)S(1)}, bf16[64,1024]{1,0:T(8,128)(2,1)S(1)}, u32[]{:S(2)}, u32[]{:S(2)}) collective-permute-start(bf16[64,1024]{1,0:T(8,128)(2,1)S(1)} %collective-permute-done.22.refs_3_), channel_id=1, source_target_pairs={{4,0},{5,1},{8,4},{9,5},{12,8},{13,9},{14,12},{15,13},{10,14},{11,... | collective-permute-start | bytes 393224 | tf_op jit(solution)/shard_map/ppermute | solution.py:427
  43.8 17.5 %collective-permute-start.28 = (bf16[64,1024]{1,0:T(8,128)(2,1)S(1)}, bf16[64,1024]{1,0:T(8,128)(2,1)S(1)}, u32[]{:S(2)}, u32[]{:S(2)}) collective-permute-start(bf16[64,1024]{1,0:T(8,128)(2,1)S(1)} %collective-permute-done.27.refs_0_), channel_id=1, source_target_pairs={{0,4},{1,5},{4,8},{5,9},{8,12},{9,13},{12,14},{13,15},{14,10},{15,... | collective-permute-start | bytes 393224 | tf_op jit(solution)/shard_map/ppermute | solution.py:426
  46.3 15.1 %collective-permute-start.31 = (bf16[64,1024]{1,0:T(8,128)(2,1)S(1)}, bf16[64,1024]{1,0:T(8,128)(2,1)S(1)}, u32[]{:S(2)}, u32[]{:S(2)}) collective-permute-start(bf16[64,1024]{1,0:T(8,128)(2,1)S(1)} %collective-permute-done.30.refs_1_), channel_id=1, source_target_pairs={{4,0},{5,1},{8,4},{9,5},{12,8},{13,9},{14,12},{15,13},{10,14},{11,... | collective-permute-start | bytes 393224 | tf_op jit(solution)/shard_map/ppermute | solution.py:427
  55.1 8.7 %collective-permute-start.20 = (bf16[64,1024]{1,0:T(8,128)(2,1)S(1)}, bf16[64,1024]{1,0:T(8,128)(2,1)S(1)}, u32[]{:S(2)}, u32[]{:S(2)}) collective-permute-start(bf16[64,1024]{1,0:T(8,128)(2,1)S(1)} %collective-permute-done.19.refs_2_), channel_id=1, source_target_pairs={{0,4},{1,5},{4,8},{5,9},{8,12},{9,13},{12,14},{13,15},{14,10},{15,... | collective-permute-start | bytes 393224 | tf_op jit(solution)/shard_map/ppermute | solution.py:426
  57.2 6.6 %collective-permute-start.24 = (bf16[64,1024]{1,0:T(8,128)(2,1)S(1)}, bf16[64,1024]{1,0:T(8,128)(2,1)S(1)}, u32[]{:S(2)}, u32[]{:S(2)}) collective-permute-start(bf16[64,1024]{1,0:T(8,128)(2,1)S(1)} %collective-permute-done.23.refs_3_), channel_id=1, source_target_pairs={{4,0},{5,1},{8,4},{9,5},{12,8},{13,9},{14,12},{15,13},{10,14},{11,... | collective-permute-start | bytes 393224 | tf_op jit(solution)/shard_map/ppermute | solution.py:427
  (17 other events, 114.7 us)

commit v3 on v2

--- a/solution.py
+++ b/solution.py
@@ -169,29 +169,24 @@
     pairs, wide = stacks.shape[0], stacks.shape[2]
     half = wide // 2
     tops, totals, accs = new
-    masked = left is not None
-    if masked:
+    found_tops, found_totals = [], []
+    if left is not None:
         valid = lax.broadcasted_iota(jnp.int32, (n, wide), 0) < left
     for i in range(pairs):
         score = jnp.dot(keys[:n, i * PAIR : (i + 1) * PAIR], stacks[i], preferred_element_type=F32)
-        if masked:
+        if left is not None:
             score = jnp.where(valid, score, NEG)
         scores[i, :n] = score
         top = jnp.max(score, axis=0, keepdims=True)
-        tops[i : i + 1] = top if old is None else jnp.maximum(old[0][i : i + 1], top)
-    for i in range(pairs):
-        top = tops[i : i + 1]
-        weights = jnp.exp(scores[i, :n] - top)
-        if masked:
-            weights = jnp.where(valid, weights, 0.0)
-        total = jnp.sum(weights, axis=0, keepdims=True)
+        found_tops.append(top if old is None else jnp.maximum(old[0][i : i + 1], top))
+    for i in range(pairs):
+        weights = jnp.exp(scores[i, :n] - found_tops[i])
+        found_totals.append(jnp.sum(weights, axis=0, keepdims=True))
+        probs[i, :n] = weights.astype(BF16)
+    for i in range(pairs):
         if old is not None:
-            total = total + old[1][i : i + 1] * jnp.exp(old[0][i : i + 1] - top)
-        totals[i : i + 1] = total
-        probs[i, :n] = weights.astype(BF16)
-    for i in range(pairs):
-        if old is not None:
-            fade = jnp.exp(old[0][i : i + 1] - tops[i : i + 1])
+            fade = jnp.exp(old[0][i : i + 1] - found_tops[i])
+            found_totals[i] = found_totals[i] + old[1][i : i + 1] * fade
         for h in range(2):
             rows = slice(i * PAIR + h * HEAD_DIM, i * PAIR + (h + 1) * HEAD_DIM)
             cols = slice(h * half, (h + 1) * half)
@@ -199,6 +194,8 @@
             if old is not None:
                 part = part + old[2][rows, :] * fade[:, cols]
             accs[rows, :] = part
+    for i in range(pairs):
+        tops[i : i + 1], totals[i : i + 1] = found_tops[i], found_totals[i]
 
 
 def attend_lazily(n, stacks, keys, values, scores, probs, old, new):
@@ -351,58 +348,65 @@
     attend_lazily(block.shape[0], stacks, keys, values, scores, probs, old, (tops, totals, accs))
 
 
-def last_kernel(n_pieces, part, *refs):
+def export_kernel(stacks, tops, totals, accs, own_stacks, own_tops, own_totals, own_accs, away):
+    pairs, width, rows = tops.shape[0], accs.shape[0], accs.shape[1] // 2
+    own_accs[...] = accs[:, :rows]
+    away[:width] = accs[:, rows:]
+    for h in range(2):
+        mine = slice(h * 2 * rows, h * 2 * rows + rows)
+        cols = slice(h * rows, (h + 1) * rows)
+        own_tops[:, cols] = tops[:, mine]
+        own_totals[:, cols] = totals[:, mine]
+        for i in range(pairs):
+            own_stacks[i, :, cols] = stacks[i, :, mine]
+            theirs = slice(h * 2 * rows + rows, (h + 1) * 2 * rows)
+            at = width + 2 * i + h
+            away[at : at + 1] = tops[i : i + 1, theirs]
+            away[at + 2 * pairs : at + 2 * pairs + 1] = totals[i : i + 1, theirs]
+
+
+def end_kernel(n_pieces, *refs):
     sources = refs[:n_pieces]
-    (w_qkv, stacks, old_tops, old_totals, old_accs, tops, totals, accs, away,
-     keys, values, scores, probs) = refs[n_pieces:]
-    pairs, lines, rows = tops.shape[0], accs.shape[0], accs.shape[1] // 2
-    width = old_accs.shape[0]
-    block = jnp.concatenate([s[...] for s in sources], axis=0)
-    project(block, w_qkv, width + part * lines, 2 * width + part * lines, keys, values)
-    span = slice(part * pairs, (part + 1) * pairs)
-    old = (old_tops.at[span], old_totals.at[span], old_accs.at[part * lines : (part + 1) * lines])
-    attend_lazily(
-        block.shape[0], stacks.at[span], keys, values, scores, probs, old, (tops, totals, accs)
-    )
-    away[:lines] = accs[:, rows:]
+    (w_qkv, stacks, old_tops, old_totals, old_accs, far, mixed, w_out, out, tops, totals, accs,
+     keys, values, scores, probs, joined, staged, sems) = refs[n_pieces:]
+    next_kernel(n_pieces, *sources, w_qkv, stacks, old_tops, old_totals, old_accs, tops, totals, accs,
+                keys, values, scores, probs)
+    pairs, width, rows = tops.shape[0], accs.shape[0], accs.shape[1]
     for i in range(pairs):
         for h in range(2):
-            there = slice(h * 2 * rows + rows, (h + 1) * 2 * rows)
-            at = lines + 2 * i + h
-            away[at : at + 1] = tops[i : i + 1, there]
-            away[at + 2 * pairs : at + 2 * pairs + 1] = totals[i : i + 1, there]
-
-
-def final_kernel(part, tops, totals, accs, far, base, w_out, out, joined, merged, sums):
-    pairs, lines, rows = tops.shape[0], accs.shape[0], accs.shape[1] // 2
-    for i in range(pairs):
-        for h in range(2):
-            at = lines + 2 * i + h
-            here = slice(h * 2 * rows, h * 2 * rows + rows)
-            span = slice(i * PAIR + h * HEAD_DIM, i * PAIR + (h + 1) * HEAD_DIM)
+            at = width + 2 * i + h
+            here = slice(h * rows, (h + 1) * rows)
+            lines = slice(i * PAIR + h * HEAD_DIM, i * PAIR + (h + 1) * HEAD_DIM)
             near_top, far_top = tops[i : i + 1, here], far[at : at + 1]
             top = jnp.maximum(near_top, far_top)
             near_fade, far_fade = jnp.exp(near_top - top), jnp.exp(far_top - top)
             far_total = far[at + 2 * pairs : at + 2 * pairs + 1]
-            sums[i : i + 1, h * rows : (h + 1) * rows] = totals[i : i + 1, here] * near_fade + far_total * far_fade
-            merged[span] = accs[span, :rows] * near_fade + far[span] * far_fade
-    finish(merged, sums, joined)
-    share = jnp.dot(joined[...], w_out[part * lines : (part + 1) * lines], preferred_element_type=F32)
-    out[...] = (base[...] + share).astype(out.dtype)
+            totals[i : i + 1, here] = totals[i : i + 1, here] * near_fade + far_total * far_fade
+            accs[lines] = accs[lines] * near_fade + far[lines] * far_fade
+    finish(accs, totals, joined)
+    copies = []
+    for q in range(width // WIDE):
+        cols = slice(q * WIDE, (q + 1) * WIDE)
+        share = jnp.dot(joined[...], w_out[:, cols], preferred_element_type=F32)
+        staged[:, cols] = (mixed[:, cols] + share).astype(BF16)
+        copies.append(pltpu.make_async_copy(staged.at[:, cols], out.at[:, cols], sems.at[q]))
+        copies[-1].start()
+    for copy in copies:
+        copy.wait()
 
 
 def on_chip(x):
     return pltpu.with_memory_space_constraint(x, VMEM)
 
 
-def call(kernel, args, outs, scratch, flops, limit, aliases=None, scalars=0):
+def call(kernel, args, outs, scratch, flops, limit, aliases=None, scalars=0, space=VMEM):
     specs = [pl.BlockSpec(memory_space=pltpu.SMEM)] * scalars
     specs += [pl.BlockSpec(memory_space=VMEM)] * (len(args) - scalars)
     return pl.pallas_call(
         kernel,
         out_shape=outs,
         in_specs=specs,
-        out_specs=jax.tree.map(lambda _: pl.BlockSpec(memory_space=VMEM), outs, is_leaf=lambda o: hasattr(o, "shape")),
+        out_specs=jax.tree.map(lambda _: pl.BlockSpec(memory_space=space), outs, is_leaf=lambda o: hasattr(o, "shape")),
         scratch_shapes=scratch,
         compiler_params=pltpu.CompilerParams(vmem_limit_bytes=limit << 20),
         cost_estimate=pl.CostEstimate(flops=flops, bytes_accessed=1 << 20, transcendentals=0),
@@ -512,34 +516,28 @@
             functools.partial(next_kernel, n), sources + [w_self_qkv, stacks, *kept],
             state(2 * rows), work(keys, 2 * rows), n << 29, 20,
         )
+    own_stacks, *own, away = call(
+        export_kernel, [stacks, *kept],
+        (VMEM((pairs, PAIR, 2 * rows), BF16), *state(rows), VMEM((width + 4 * pairs, rows), F32)),
+        [], 1 << 20, 8,
+    )
+    far = cross_over(away)
     sources = arrivals[-1]
-    n = len(sources)
-    parts, lines = pairs // 2, width // 2
-    done = []
-    for part in range(2):
-        *near, away = call(
-            functools.partial(last_kernel, n, part), sources + [w_self_qkv, stacks, *kept],
-            (
-                VMEM((parts, 4 * rows), F32), VMEM((parts, 4 * rows), F32), VMEM((lines, 2 * rows), F32),
-                VMEM((lines + 4 * parts, rows), F32),
-            ),
-            [
-                VMEM((rows, lines), BF16), VMEM((lines, rows), BF16),
-                VMEM((parts, rows, 4 * rows), F32), VMEM((parts, rows, 4 * rows), BF16),
-            ],
-            1 << 29, 16,
-        )
-        far = cross_over(away)
-        done.append([*near, far])
-    out = mixed
-    for part in range(2):
-        whole = jax.ShapeDtypeStruct((rows, width), BF16) if part else VMEM((rows, width), F32)
-        out = call(
-            functools.partial(final_kernel, part), [*done[part], out, w_self_out], whole,
-            [VMEM((rows, lines), BF16), VMEM((lines, rows), F32), VMEM((parts, 2 * rows), F32)],
-            1 << 29, 12,
-        )
-    return out
+    others = swapped(*sources)
+    own = call(
+        functools.partial(next_kernel, 2), [*sources, w_self_qkv, own_stacks, *own],
+        state(rows), work(rows, rows), 1 << 29, 16,
+    )
+    return call(
+        functools.partial(end_kernel, 2),
+        [*others, w_self_qkv, own_stacks, *own, far, mixed, w_self_out],
+        jax.ShapeDtypeStruct((rows, width), BF16),
+        [
+            *state(rows), *work(rows, rows), VMEM((rows, width), BF16), VMEM((rows, width), BF16),
+            pltpu.SemaphoreType.DMA((width // WIDE,)),
+        ],
+        1 << 30, 16, space=pl.ANY,
+    )
 
 
 def solution(mesh):

time: 70.3 us -> 73.6 us (1.047)
  waiting for transfers between devices: 16.7 us -> 21.7 us
  Pallas kernels: 24.9 us -> 23.8 us
    ppermute x11, waiting for transfers between devices: 12.6 us -> 16.4 us  [both_ways(): fore = lax.ppermute(fore, 'frame', ahead)]
    ppermute x11, waiting for transfers between devices: 2.31 us -> 4.08 us  [both_ways(): aft = lax.ppermute(aft, 'frame', behind)]
    pallas_call x14 -> x13, Pallas kernels: 23.9 us -> 22.8 us  [call(): pl.pallas_call(kernel, out_shape=outs, in_specs=specs, out_specs=jax.tree...]
    ppermute x12 -> x13, waiting for transfers between devices: 1.82 us -> 1.2 us  [cross_over(): return lax.ppermute(x, 'frame', swap)]
    ppermute x12 -> x13, starting transfers between devices: 1.67 us -> 1.11 us  [cross_over(): return lax.ppermute(x, 'frame', swap)]
  transfers between devices with their start and end apart: 34 -> 35, of which waited for: 13 -> 15; matrix products, arithmetic and copies ran while one was open for 0% -> 0% of each run, Pallas kernels for 29% -> 23%
where the time goes in v3:
time: 73.6 us; the launch traced here: 73.4 us
  starting transfers between devices  27.2 us (37%)
  Pallas kernels  23.8 us (32%)
  waiting for transfers between devices  21.7 us (29%)
    ppermute x11, starting transfers between devices, both_ways(): fore = lax.ppermute(fore, 'frame', ahead)  25.2 us
    pallas_call x13, Pallas kernels, call(): pl.pallas_call(kernel, out_shape=outs, in_specs=specs, out_specs=jax.tree...  22.8 us
    ppermute x11, waiting for transfers between devices, both_ways(): fore = lax.ppermute(fore, 'frame', ahead)  16.4 us
    ppermute x11, waiting for transfers between devices, both_ways(): aft = lax.ppermute(aft, 'frame', behind)  4.08 us
  transfers between devices with their start and end apart: 35, of which 15 were waited for; matrix products, arithmetic and copies ran while one was open for 0% of the time, Pallas kernels for 23%

profile of v3, /device:TPU:0, one launch (start us, length us, event | category | flops | bytes accessed | tf_op | source)
XLA Modules:
  0.0 73.4 jit_solution(9101406903364501711)
XLA Ops:
  1.1 3.1 %collective-permute-start = (bf16[136,512]{1,0:T(8,128)(2,1)S(1)}, bf16[136,512]{1,0:T(8,128)(2,1)S(1)}, u32[]{:S(2)}, u32[]{:S(2)}) collective-permute-start(bf16[136,512]{1,0:T(8,128)(2,1)S(1)} %tag.1.refs_0_), channel_id=1, source_target_pairs={{0,4},{1,5},{4,8},{5,9},{8,12},{9,13},{12,14},{13,15},{14,10},{15,... | collective-permute-start | bytes 417800 | tf_op jit(solution)/shard_map/ppermute | solution.py:430
  4.2 3.6 %collective-permute-done.refs_2_ = bf16[136,512]{1,0:T(8,128)(2,1)S(1)} collective-permute-done((bf16[136,512]{1,0:T(8,128)(2,1)S(1)}, bf16[136,512]{1,0:T(8,128)(2,1)S(1)}, u32[]{:S(2)}, u32[]{:S(2)}) %collective-permute-start) | collective-permute-done | bytes 139296 | tf_op jit(solution)/shard_map/ppermute | solution.py:430
  7.8 1.8 %collective-permute-start.1 = (bf16[136,512]{1,0:T(8,128)(2,1)S(1)}, bf16[136,512]{1,0:T(8,128)(2,1)S(1)}, u32[]{:S(2)}, u32[]{:S(2)}) collective-permute-start(bf16[136,512]{1,0:T(8,128)(2,1)S(1)} %collective-permute-done.refs_2_), channel_id=1, source_target_pairs={{0,4},{1,5},{4,8},{5,9},{8,12},{9,13},{12,14},{13,15},{14,10},{15,... | collective-permute-start | bytes 417800 | tf_op jit(solution)/shard_map/ppermute | solution.py:430
  9.8 3.0 %collective-permute-done.1.refs_2_ = bf16[136,512]{1,0:T(8,128)(2,1)S(1)} collective-permute-done((bf16[136,512]{1,0:T(8,128)(2,1)S(1)}, bf16[136,512]{1,0:T(8,128)(2,1)S(1)}, u32[]{:S(2)}, u32[]{:S(2)}) %collective-permute-start.1) | collective-permute-done | bytes 139296 | tf_op jit(solution)/shard_map/ppermute | solution.py:430
  12.8 1.8 %collective-permute-start.2 = (bf16[136,512]{1,0:T(8,128)(2,1)S(1)}, bf16[136,512]{1,0:T(8,128)(2,1)S(1)}, u32[]{:S(2)}, u32[]{:S(2)}) collective-permute-start(bf16[136,512]{1,0:T(8,128)(2,1)S(1)} %collective-permute-done.1.refs_2_), channel_id=1, source_target_pairs={{0,4},{1,5},{4,8},{5,9},{8,12},{9,13},{12,14},{13,15},{14,10},{15,... | collective-permute-start | bytes 417800 | tf_op jit(solution)/shard_map/ppermute | solution.py:430
  15.5 2.4 %collective-permute-done.2.refs_2_ = bf16[136,512]{1,0:T(8,128)(2,1)S(1)} collective-permute-done((bf16[136,512]{1,0:T(8,128)(2,1)S(1)}, bf16[136,512]{1,0:T(8,128)(2,1)S(1)}, u32[]{:S(2)}, u32[]{:S(2)}) %collective-permute-start.2) | collective-permute-done | bytes 139296 | tf_op jit(solution)/shard_map/ppermute | solution.py:430
  19.7 1.6 %collective-permute-start.8 = (bf16[72,512]{1,0:T(8,128)(2,1)S(1)}, bf16[72,512]{1,0:T(8,128)(2,1)S(1)}, u32[]{:S(2)}, u32[]{:S(2)}) collective-permute-start(bf16[72,512]{1,0:T(8,128)(2,1)S(1)} %slice.18), channel_id=1, source_target_pairs={{0,4},{1,5},{4,8},{5,9},{8,12},{9,13},{12,14},{13,15},{14,10},{15,... | collective-permute-start | bytes 221192 | tf_op jit(solution)/shard_map/ppermute | solution.py:430
  24.0 1.6 %collective-permute-done.9.refs_3_ = bf16[72,512]{1,0:T(8,128)(2,1)S(1)} collective-permute-done((bf16[72,512]{1,0:T(8,128)(2,1)S(1)}, bf16[72,512]{1,0:T(8,128)(2,1)S(1)}, u32[]{:S(2)}, u32[]{:S(2)}) %collective-permute-start.9) | collective-permute-done | bytes 73760 | tf_op jit(solution)/shard_map/ppermute | solution.py:431
  27.9 2.8 %collective-permute-start.17 = (bf16[64,1024]{1,0:T(8,128)(2,1)S(1)}, bf16[64,1024]{1,0:T(8,128)(2,1)S(1)}, u32[]{:S(2)}, u32[]{:S(2)}) collective-permute-start(bf16[64,1024]{1,0:T(8,128)(2,1)S(1)} %get-tuple-element.76), channel_id=1, source_target_pairs={{0,4},{1,5},{4,8},{5,9},{8,12},{9,13},{12,14},{13,15},{14,10},{15,... | collective-permute-start | bytes 393224 | tf_op jit(solution)/shard_map/ppermute | solution.py:430
  30.7 2.0 %collective-permute-start.28 = (bf16[64,1024]{1,0:T(8,128)(2,1)S(1)}, bf16[64,1024]{1,0:T(8,128)(2,1)S(1)}, u32[]{:S(2)}, u32[]{:S(2)}) collective-permute-start(bf16[64,1024]{1,0:T(8,128)(2,1)S(1)} %get-tuple-element.75), channel_id=1, source_target_pairs={{0,4},{1,5},{4,8},{5,9},{8,12},{9,13},{12,14},{13,15},{14,10},{15,... | collective-permute-start | bytes 393224 | tf_op jit(solution)/shard_map/ppermute | solution.py:430
  32.8 1.9 %collective-permute-done.17.refs_0_ = bf16[64,1024]{1,0:T(8,128)(2,1)S(1)} collective-permute-done((bf16[64,1024]{1,0:T(8,128)(2,1)S(1)}, bf16[64,1024]{1,0:T(8,128)(2,1)S(1)}, u32[]{:S(2)}, u32[]{:S(2)}) %collective-permute-start.17) | collective-permute-done | bytes 131104 | tf_op jit(solution)/shard_map/ppermute | solution.py:430
  34.6 2.5 %collective-permute-start.18 = (bf16[64,1024]{1,0:T(8,128)(2,1)S(1)}, bf16[64,1024]{1,0:T(8,128)(2,1)S(1)}, u32[]{:S(2)}, u32[]{:S(2)}) collective-permute-start(bf16[64,1024]{1,0:T(8,128)(2,1)S(1)} %collective-permute-done.17.refs_0_), channel_id=1, source_target_pairs={{0,4},{1,5},{4,8},{5,9},{8,12},{9,13},{12,14},{13,15},{14,10},{15,... | collective-permute-start | bytes 393224 | tf_op jit(solution)/shard_map/ppermute | solution.py:430
  37.4 2.5 %collective-permute-start.29 = (bf16[64,1024]{1,0:T(8,128)(2,1)S(1)}, bf16[64,1024]{1,0:T(8,128)(2,1)S(1)}, u32[]{:S(2)}, u32[]{:S(2)}) collective-permute-start(bf16[64,1024]{1,0:T(8,128)(2,1)S(1)} %collective-permute-done.28.refs_0_), channel_id=1, source_target_pairs={{0,4},{1,5},{4,8},{5,9},{8,12},{9,13},{12,14},{13,15},{14,10},{15,... | collective-permute-start | bytes 393224 | tf_op jit(solution)/shard_map/ppermute | solution.py:430
  40.7 2.5 %collective-permute-start.19 = (bf16[64,1024]{1,0:T(8,128)(2,1)S(1)}, bf16[64,1024]{1,0:T(8,128)(2,1)S(1)}, u32[]{:S(2)}, u32[]{:S(2)}) collective-permute-start(bf16[64,1024]{1,0:T(8,128)(2,1)S(1)} %collective-permute-done.18.refs_2_), channel_id=1, source_target_pairs={{0,4},{1,5},{4,8},{5,9},{8,12},{9,13},{12,14},{13,15},{14,10},{15,... | collective-permute-start | bytes 393224 | tf_op jit(solution)/shard_map/ppermute | solution.py:430
  43.8 2.5 %collective-permute-start.30 = (bf16[64,1024]{1,0:T(8,128)(2,1)S(1)}, bf16[64,1024]{1,0:T(8,128)(2,1)S(1)}, u32[]{:S(2)}, u32[]{:S(2)}) collective-permute-start(bf16[64,1024]{1,0:T(8,128)(2,1)S(1)} %collective-permute-done.29.refs_0_), channel_id=1, source_target_pairs={{0,4},{1,5},{4,8},{5,9},{8,12},{9,13},{12,14},{13,15},{14,10},{15,... | collective-permute-start | bytes 393224 | tf_op jit(solution)/shard_map/ppermute | solution.py:430
  46.3 2.0 %shard_map.87 = (bf16[8,128,512]{2,1,0:T(8,128)(2,1)S(1)}, f32[8,512]{1,0:T(8,128)S(1)}, f32[8,512]{1,0:T(8,128)S(1)}, f32[1024,256]{1,0:T(8,128)S(1)}) custom-call(bf16[128,1024]{1,0:T(8,128)(2,1)S(1)} %get-tuple-element.49.mine, bf16[128,1024]{1,0:T(8,128)(2,1)S(1)} %collective-permute-done.27.other, bf16[1024,3072]{1,0:T(8,128)(2,1)S(1)} %bitcast.1), custom_call_target="tpu_custom_call" | custom-call | flops 1073741824 | bytes 1048576 | tf_op jit(solution)/shard_map/pallas_call | solution.py:405
  48.4 2.5 %shard_map.88 = (f32[8,512]{1,0:T(8,128)S(1)}, f32[8,512]{1,0:T(8,128)S(1)}, f32[1024,256]{1,0:T(8,128)S(1)}) custom-call(bf16[64,1024]{1,0:T(8,128)(2,1)S(1)} %collective-permute-done.17.refs_0_, bf16[64,1024]{1,0:T(8,128)(2,1)S(1)} %collective-permute-done.22.refs_1_, bf16[1024,3072]{1,0:T(8,128)(2,1)S(1)} %bitcast.1, ...), custom_call_target="tpu_custom_call" | custom-call | flops 1073741824 | bytes 1048576 | tf_op jit(solution)/shard_map/pallas_call | solution.py:405
  50.9 4.1 %shard_map.89 = (f32[8,512]{1,0:T(8,128)S(1)}, f32[8,512]{1,0:T(8,128)S(1)}, f32[1024,256]{1,0:T(8,128)S(1)}) custom-call(bf16[64,1024]{1,0:T(8,128)(2,1)S(1)} %collective-permute-done.28.refs_0_, bf16[64,1024]{1,0:T(8,128)(2,1)S(1)} %collective-permute-done.31.refs_1_, bf16[64,1024]{1,0:T(8,128)(2,1)S(1)} %collective-permute-done.18.refs_2_, ...), custom_call_target="tpu_custom_call" | custom-call | flops 2147483648 | bytes 1048576 | tf_op jit(solution)/shard_map/pallas_call | solution.py:405
  54.9 4.0 %shard_map.90 = (f32[8,512]{1,0:T(8,128)S(1)}, f32[8,512]{1,0:T(8,128)S(1)}, f32[1024,256]{1,0:T(8,128)S(1)}) custom-call(bf16[64,1024]{1,0:T(8,128)(2,1)S(1)} %collective-permute-done.29.refs_0_, bf16[64,1024]{1,0:T(8,128)(2,1)S(1)} %collective-permute-done.32.refs_1_, bf16[64,1024]{1,0:T(8,128)(2,1)S(1)} %collective-permute-done.19.refs_2_, ...), custom_call_target="tpu_custom_call" | custom-call | flops 2147483648 | bytes 1048576 | tf_op jit(solution)/shard_map/pallas_call | solution.py:405
  59.0 2.3 %shard_map.91 = (f32[8,512]{1,0:T(8,128)S(1)}, f32[8,512]{1,0:T(8,128)S(1)}, f32[1024,256]{1,0:T(8,128)S(1)}) custom-call(bf16[64,1024]{1,0:T(8,128)(2,1)S(1)} %collective-permute-done.30.refs_0_, bf16[64,1024]{1,0:T(8,128)(2,1)S(1)} %collective-permute-done.33.refs_1_, bf16[1024,3072]{1,0:T(8,128)(2,1)S(1)} %bitcast.1, ...), custom_call_target="tpu_custom_call" | custom-call | flops 1073741824 | bytes 1048576 | tf_op jit(solution)/shard_map/pallas_call | solution.py:405
  61.6 2.1 %collective-permute-start.20 = (bf16[64,1024]{1,0:T(8,128)(2,1)S(1)}, bf16[64,1024]{1,0:T(8,128)(2,1)S(1)}, u32[]{:S(2)}, u32[]{:S(2)}) collective-permute-start(bf16[64,1024]{1,0:T(8,128)(2,1)S(1)} %collective-permute-done.19.refs_2_), channel_id=1, source_target_pairs={{0,4},{1,5},{4,8},{5,9},{8,12},{9,13},{12,14},{13,15},{14,10},{15,... | collective-permute-start | bytes 393224 | tf_op jit(solution)/shard_map/ppermute | solution.py:430
  63.7 3.8 %collective-permute-done.20.refs_0_ = bf16[64,1024]{1,0:T(8,128)(2,1)S(1)} collective-permute-done((bf16[64,1024]{1,0:T(8,128)(2,1)S(1)}, bf16[64,1024]{1,0:T(8,128)(2,1)S(1)}, u32[]{:S(2)}, u32[]{:S(2)}) %collective-permute-start.20) | collective-permute-done | bytes 131104 | tf_op jit(solution)/shard_map/ppermute | solution.py:430
  67.5 1.7 %collective-permute-done.25.refs_1_ = bf16[64,1024]{1,0:T(8,128)(2,1)S(1)} collective-permute-done((bf16[64,1024]{1,0:T(8,128)(2,1)S(1)}, bf16[64,1024]{1,0:T(8,128)(2,1)S(1)}, u32[]{:S(2)}, u32[]{:S(2)}) %collective-permute-start.25) | collective-permute-done | bytes 131104 | tf_op jit(solution)/shard_map/ppermute | solution.py:431
  70.8 2.4 %shard_map.94 = bf16[128,1024]{1,0:T(8,128)(2,1)} custom-call(bf16[64,1024]{1,0:T(8,128)(2,1)S(1)} %collective-permute-done.21.refs_0_, bf16[64,1024]{1,0:T(8,128)(2,1)S(1)} %collective-permute-done.26.refs_1_, bf16[1024,3072]{1,0:T(8,128)(2,1)S(1)} %bitcast.1, bf16[8,128,256]{2,1,0:T(8,128)(2,1)S(1)} %get-tuple-element.66.refs_3_, ...), custom_call_target="tpu_custom_call" | custom-call | flops 1073741824 | bytes 1048576 | tf_op jit(solution)/shard_map/pallas_call | solution.py:405
  (78 shorter events, 12.5 us)
Async XLA Ops:
  1.1 6.7 %collective-permute-start = (bf16[136,512]{1,0:T(8,128)(2,1)S(1)}, bf16[136,512]{1,0:T(8,128)(2,1)S(1)}, u32[]{:S(2)}, u32[]{:S(2)}) collective-permute-start(bf16[136,512]{1,0:T(8,128)(2,1)S(1)} %tag.1.refs_0_), channel_id=1, source_target_pairs={{0,4},{1,5},{4,8},{5,9},{8,12},{9,13},{12,14},{13,15},{14,10},{15,... | collective-permute-start | bytes 417800 | tf_op jit(solution)/shard_map/ppermute | solution.py:430
  4.2 5.4 %collective-permute-start.4 = (bf16[136,512]{1,0:T(8,128)(2,1)S(1)}, bf16[136,512]{1,0:T(8,128)(2,1)S(1)}, u32[]{:S(2)}, u32[]{:S(2)}) collective-permute-start(bf16[136,512]{1,0:T(8,128)(2,1)S(1)} %tag.1.refs_0_), channel_id=1, source_target_pairs={{4,0},{5,1},{8,4},{9,5},{12,8},{13,9},{14,12},{15,13},{10,14},{11,... | collective-permute-start | bytes 417800 | tf_op jit(solution)/shard_map/ppermute | solution.py:431
  9.6 5.1 %collective-permute-start.5 = (bf16[136,512]{1,0:T(8,128)(2,1)S(1)}, bf16[136,512]{1,0:T(8,128)(2,1)S(1)}, u32[]{:S(2)}, u32[]{:S(2)}) collective-permute-start(bf16[136,512]{1,0:T(8,128)(2,1)S(1)} %collective-permute-done.4.refs_3_), channel_id=1, source_target_pairs={{4,0},{5,1},{8,4},{9,5},{12,8},{13,9},{14,12},{15,13},{10,14},{11,... | collective-permute-start | bytes 417800 | tf_op jit(solution)/shard_map/ppermute | solution.py:431
  9.8 5.6 %collective-permute-start.16 = (bf16[136,512]{1,0:T(8,128)(2,1)S(1)}, bf16[136,512]{1,0:T(8,128)(2,1)S(1)}, u32[]{:S(2)}, u32[]{:S(2)}) collective-permute-start(bf16[136,512]{1,0:T(8,128)(2,1)S(1)} %tag.1.refs_0_), channel_id=1, source_target_pairs={{0,1},{1,0},{2,3},{3,2},{4,5},{5,4},{6,7},{7,6},{8,9},{9,8},{10,11... | collective-permute-start | bytes 417800 | tf_op jit(solution)/shard_map/ppermute | solution.py:427
  14.8 6.4 %collective-permute-start.14 = (bf16[136,512]{1,0:T(8,128)(2,1)S(1)}, bf16[136,512]{1,0:T(8,128)(2,1)S(1)}, u32[]{:S(2)}, u32[]{:S(2)}) collective-permute-start(bf16[136,512]{1,0:T(8,128)(2,1)S(1)} %collective-permute-done.refs_2_), channel_id=1, source_target_pairs={{0,1},{1,0},{2,3},{3,2},{4,5},{5,4},{6,7},{7,6},{8,9},{9,8},{10,11... | collective-permute-start | bytes 417800 | tf_op jit(solution)/shard_map/ppermute | solution.py:427
  14.8 6.9 %collective-permute-start.15 = (bf16[136,512]{1,0:T(8,128)(2,1)S(1)}, bf16[136,512]{1,0:T(8,128)(2,1)S(1)}, u32[]{:S(2)}, u32[]{:S(2)}) collective-permute-start(bf16[136,512]{1,0:T(8,128)(2,1)S(1)} %collective-permute-done.4.refs_3_), channel_id=1, source_target_pairs={{0,1},{1,0},{2,3},{3,2},{4,5},{5,4},{6,7},{7,6},{8,9},{9,8},{10,11... | collective-permute-start | bytes 417800 | tf_op jit(solution)/shard_map/ppermute | solution.py:427
  15.4 6.4 %collective-permute-start.12 = (bf16[136,512]{1,0:T(8,128)(2,1)S(1)}, bf16[136,512]{1,0:T(8,128)(2,1)S(1)}, u32[]{:S(2)}, u32[]{:S(2)}) collective-permute-start(bf16[136,512]{1,0:T(8,128)(2,1)S(1)} %collective-permute-done.1.refs_2_), channel_id=1, source_target_pairs={{0,1},{1,0},{2,3},{3,2},{4,5},{5,4},{6,7},{7,6},{8,9},{9,8},{10,11... | collective-permute-start | bytes 417800 | tf_op jit(solution)/shard_map/ppermute | solution.py:427
  17.9 7.8 %collective-permute-start.13 = (bf16[136,512]{1,0:T(8,128)(2,1)S(1)}, bf16[136,512]{1,0:T(8,128)(2,1)S(1)}, u32[]{:S(2)}, u32[]{:S(2)}) collective-permute-start(bf16[136,512]{1,0:T(8,128)(2,1)S(1)} %collective-permute-done.5.refs_3_), channel_id=1, source_target_pairs={{0,1},{1,0},{2,3},{3,2},{4,5},{5,4},{6,7},{7,6},{8,9},{9,8},{10,11... | collective-permute-start | bytes 417800 | tf_op jit(solution)/shard_map/ppermute | solution.py:427
  27.9 6.7 %collective-permute-start.17 = (bf16[64,1024]{1,0:T(8,128)(2,1)S(1)}, bf16[64,1024]{1,0:T(8,128)(2,1)S(1)}, u32[]{:S(2)}, u32[]{:S(2)}) collective-permute-start(bf16[64,1024]{1,0:T(8,128)(2,1)S(1)} %get-tuple-element.76), channel_id=1, source_target_pairs={{0,4},{1,5},{4,8},{5,9},{8,12},{9,13},{12,14},{13,15},{14,10},{15,... | collective-permute-start | bytes 393224 | tf_op jit(solution)/shard_map/ppermute | solution.py:430
  30.7 6.4 %collective-permute-start.22 = (bf16[64,1024]{1,0:T(8,128)(2,1)S(1)}, bf16[64,1024]{1,0:T(8,128)(2,1)S(1)}, u32[]{:S(2)}, u32[]{:S(2)}) collective-permute-start(bf16[64,1024]{1,0:T(8,128)(2,1)S(1)} %get-tuple-element.75), channel_id=1, source_target_pairs={{4,0},{5,1},{8,4},{9,5},{12,8},{13,9},{14,12},{15,13},{10,14},{11,... | collective-permute-start | bytes 393224 | tf_op jit(solution)/shard_map/ppermute | solution.py:431
  30.7 6.7 %collective-permute-start.28 = (bf16[64,1024]{1,0:T(8,128)(2,1)S(1)}, bf16[64,1024]{1,0:T(8,128)(2,1)S(1)}, u32[]{:S(2)}, u32[]{:S(2)}) collective-permute-start(bf16[64,1024]{1,0:T(8,128)(2,1)S(1)} %get-tuple-element.75), channel_id=1, source_target_pairs={{0,4},{1,5},{4,8},{5,9},{8,12},{9,13},{12,14},{13,15},{14,10},{15,... | collective-permute-start | bytes 393224 | tf_op jit(solution)/shard_map/ppermute | solution.py:430
  32.8 7.2 %collective-permute-start.31 = (bf16[64,1024]{1,0:T(8,128)(2,1)S(1)}, bf16[64,1024]{1,0:T(8,128)(2,1)S(1)}, u32[]{:S(2)}, u32[]{:S(2)}) collective-permute-start(bf16[64,1024]{1,0:T(8,128)(2,1)S(1)} %get-tuple-element.76), channel_id=1, source_target_pairs={{4,0},{5,1},{8,4},{9,5},{12,8},{13,9},{14,12},{15,13},{10,14},{11,... | collective-permute-start | bytes 393224 | tf_op jit(solution)/shard_map/ppermute | solution.py:431
  32.8 13.5 %collective-permute-start.27 = (bf16[128,1024]{1,0:T(8,128)(2,1)S(1)}, bf16[128,1024]{1,0:T(8,128)(2,1)S(1)}, u32[]{:S(2)}, u32[]{:S(2)}) collective-permute-start(bf16[128,1024]{1,0:T(8,128)(2,1)S(1)} %get-tuple-element.49.mine), channel_id=1, source_target_pairs={{0,1},{1,0},{2,3},{3,2},{4,5},{5,4},{6,7},{7,6},{8,9},{9,8},{10,11... | collective-permute-start | bytes 786440 | tf_op jit(solution)/shard_map/ppermute | solution.py:427
  34.6 6.0 %collective-permute-start.18 = (bf16[64,1024]{1,0:T(8,128)(2,1)S(1)}, bf16[64,1024]{1,0:T(8,128)(2,1)S(1)}, u32[]{:S(2)}, u32[]{:S(2)}) collective-permute-start(bf16[64,1024]{1,0:T(8,128)(2,1)S(1)} %collective-permute-done.17.refs_0_), channel_id=1, source_target_pairs={{0,4},{1,5},{4,8},{5,9},{8,12},{9,13},{12,14},{13,15},{14,10},{15,... | collective-permute-start | bytes 393224 | tf_op jit(solution)/shard_map/ppermute | solution.py:430
  37.1 6.3 %collective-permute-start.23 = (bf16[64,1024]{1,0:T(8,128)(2,1)S(1)}, bf16[64,1024]{1,0:T(8,128)(2,1)S(1)}, u32[]{:S(2)}, u32[]{:S(2)}) collective-permute-start(bf16[64,1024]{1,0:T(8,128)(2,1)S(1)} %collective-permute-done.22.refs_1_), channel_id=1, source_target_pairs={{4,0},{5,1},{8,4},{9,5},{12,8},{13,9},{14,12},{15,13},{10,14},{11,... | collective-permute-start | bytes 393224 | tf_op jit(solution)/shard_map/ppermute | solution.py:431
  37.4 6.4 %collective-permute-start.29 = (bf16[64,1024]{1,0:T(8,128)(2,1)S(1)}, bf16[64,1024]{1,0:T(8,128)(2,1)S(1)}, u32[]{:S(2)}, u32[]{:S(2)}) collective-permute-start(bf16[64,1024]{1,0:T(8,128)(2,1)S(1)} %collective-permute-done.28.refs_0_), channel_id=1, source_target_pairs={{0,4},{1,5},{4,8},{5,9},{8,12},{9,13},{12,14},{13,15},{14,10},{15,... | collective-permute-start | bytes 393224 | tf_op jit(solution)/shard_map/ppermute | solution.py:430
  39.9 6.4 %collective-permute-start.32 = (bf16[64,1024]{1,0:T(8,128)(2,1)S(1)}, bf16[64,1024]{1,0:T(8,128)(2,1)S(1)}, u32[]{:S(2)}, u32[]{:S(2)}) collective-permute-start(bf16[64,1024]{1,0:T(8,128)(2,1)S(1)} %collective-permute-done.31.refs_1_), channel_id=1, source_target_pairs={{4,0},{5,1},{8,4},{9,5},{12,8},{13,9},{14,12},{15,13},{10,14},{11,... | collective-permute-start | bytes 393224 | tf_op jit(solution)/shard_map/ppermute | solution.py:431
  40.7 14.3 %collective-permute-start.19 = (bf16[64,1024]{1,0:T(8,128)(2,1)S(1)}, bf16[64,1024]{1,0:T(8,128)(2,1)S(1)}, u32[]{:S(2)}, u32[]{:S(2)}) collective-permute-start(bf16[64,1024]{1,0:T(8,128)(2,1)S(1)} %collective-permute-done.18.refs_2_), channel_id=1, source_target_pairs={{0,4},{1,5},{4,8},{5,9},{8,12},{9,13},{12,14},{13,15},{14,10},{15,... | collective-permute-start | bytes 393224 | tf_op jit(solution)/shard_map/ppermute | solution.py:430
  43.4 11.5 %collective-permute-start.24 = (bf16[64,1024]{1,0:T(8,128)(2,1)S(1)}, bf16[64,1024]{1,0:T(8,128)(2,1)S(1)}, u32[]{:S(2)}, u32[]{:S(2)}) collective-permute-start(bf16[64,1024]{1,0:T(8,128)(2,1)S(1)} %collective-permute-done.23.refs_3_), channel_id=1, source_target_pairs={{4,0},{5,1},{8,4},{9,5},{12,8},{13,9},{14,12},{15,13},{10,14},{11,... | collective-permute-start | bytes 393224 | tf_op jit(solution)/shard_map/ppermute | solution.py:431
  43.8 15.2 %collective-permute-start.30 = (bf16[64,1024]{1,0:T(8,128)(2,1)S(1)}, bf16[64,1024]{1,0:T(8,128)(2,1)S(1)}, u32[]{:S(2)}, u32[]{:S(2)}) collective-permute-start(bf16[64,1024]{1,0:T(8,128)(2,1)S(1)} %collective-permute-done.29.refs_0_), channel_id=1, source_target_pairs={{0,4},{1,5},{4,8},{5,9},{8,12},{9,13},{12,14},{13,15},{14,10},{15,... | collective-permute-start | bytes 393224 | tf_op jit(solution)/shard_map/ppermute | solution.py:430
  46.3 12.7 %collective-permute-start.33 = (bf16[64,1024]{1,0:T(8,128)(2,1)S(1)}, bf16[64,1024]{1,0:T(8,128)(2,1)S(1)}, u32[]{:S(2)}, u32[]{:S(2)}) collective-permute-start(bf16[64,1024]{1,0:T(8,128)(2,1)S(1)} %collective-permute-done.32.refs_1_), channel_id=1, source_target_pairs={{4,0},{5,1},{8,4},{9,5},{12,8},{13,9},{14,12},{15,13},{10,14},{11,... | collective-permute-start | bytes 393224 | tf_op jit(solution)/shard_map/ppermute | solution.py:431
  61.5 9.1 %collective-permute-start.34 = (f32[1056,128]{1,0:T(8,128)S(1)}, f32[1056,128]{1,0:T(8,128)S(1)}, u32[]{:S(2)}, u32[]{:S(2)}) collective-permute-start(f32[1056,128]{1,0:T(8,128)S(1)} %get-tuple-element.73), channel_id=1, source_target_pairs={{0,1},{1,0},{2,3},{3,2},{4,5},{5,4},{6,7},{7,6},{8,9},{9,8},{10,11... | collective-permute-start | bytes 1622024 | tf_op jit(solution)/shard_map/ppermute | solution.py:427
  61.6 5.9 %collective-permute-start.20 = (bf16[64,1024]{1,0:T(8,128)(2,1)S(1)}, bf16[64,1024]{1,0:T(8,128)(2,1)S(1)}, u32[]{:S(2)}, u32[]{:S(2)}) collective-permute-start(bf16[64,1024]{1,0:T(8,128)(2,1)S(1)} %collective-permute-done.19.refs_2_), channel_id=1, source_target_pairs={{0,4},{1,5},{4,8},{5,9},{8,12},{9,13},{12,14},{13,15},{14,10},{15,... | collective-permute-start | bytes 393224 | tf_op jit(solution)/shard_map/ppermute | solution.py:430
  63.7 5.6 %collective-permute-start.25 = (bf16[64,1024]{1,0:T(8,128)(2,1)S(1)}, bf16[64,1024]{1,0:T(8,128)(2,1)S(1)}, u32[]{:S(2)}, u32[]{:S(2)}) collective-permute-start(bf16[64,1024]{1,0:T(8,128)(2,1)S(1)} %collective-permute-done.24.refs_3_), channel_id=1, source_target_pairs={{4,0},{5,1},{8,4},{9,5},{12,8},{13,9},{14,12},{15,13},{10,14},{11,... | collective-permute-start | bytes 393224 | tf_op jit(solution)/shard_map/ppermute | solution.py:431
  (18 other events, 119.6 us)

commit v4 on v2

--- a/solution.py
+++ b/solution.py
@@ -169,29 +169,24 @@
     pairs, wide = stacks.shape[0], stacks.shape[2]
     half = wide // 2
     tops, totals, accs = new
-    masked = left is not None
-    if masked:
+    found_tops, found_totals = [], []
+    if left is not None:
         valid = lax.broadcasted_iota(jnp.int32, (n, wide), 0) < left
     for i in range(pairs):
         score = jnp.dot(keys[:n, i * PAIR : (i + 1) * PAIR], stacks[i], preferred_element_type=F32)
-        if masked:
+        if left is not None:
             score = jnp.where(valid, score, NEG)
         scores[i, :n] = score
         top = jnp.max(score, axis=0, keepdims=True)
-        tops[i : i + 1] = top if old is None else jnp.maximum(old[0][i : i + 1], top)
-    for i in range(pairs):
-        top = tops[i : i + 1]
-        weights = jnp.exp(scores[i, :n] - top)
-        if masked:
-            weights = jnp.where(valid, weights, 0.0)
-        total = jnp.sum(weights, axis=0, keepdims=True)
+        found_tops.append(top if old is None else jnp.maximum(old[0][i : i + 1], top))
+    for i in range(pairs):
+        weights = jnp.exp(scores[i, :n] - found_tops[i])
+        found_totals.append(jnp.sum(weights, axis=0, keepdims=True))
+        probs[i, :n] = weights.astype(BF16)
+    for i in range(pairs):
         if old is not None:
-            total = total + old[1][i : i + 1] * jnp.exp(old[0][i : i + 1] - top)
-        totals[i : i + 1] = total
-        probs[i, :n] = weights.astype(BF16)
-    for i in range(pairs):
-        if old is not None:
-            fade = jnp.exp(old[0][i : i + 1] - tops[i : i + 1])
+            fade = jnp.exp(old[0][i : i + 1] - found_tops[i])
+            found_totals[i] = found_totals[i] + old[1][i : i + 1] * fade
         for h in range(2):
             rows = slice(i * PAIR + h * HEAD_DIM, i * PAIR + (h + 1) * HEAD_DIM)
             cols = slice(h * half, (h + 1) * half)
@@ -199,6 +194,8 @@
             if old is not None:
                 part = part + old[2][rows, :] * fade[:, cols]
             accs[rows, :] = part
+    for i in range(pairs):
+        tops[i : i + 1], totals[i : i + 1] = found_tops[i], found_totals[i]
 
 
 def attend_lazily(n, stacks, keys, values, scores, probs, old, new):
@@ -373,7 +370,7 @@
             away[at + 2 * pairs : at + 2 * pairs + 1] = totals[i : i + 1, there]
 
 
-def final_kernel(part, tops, totals, accs, far, base, w_out, out, joined, merged, sums):
+def final_kernel(part, tops, totals, accs, far, base, w_out, out, joined, merged, sums, *rest):
     pairs, lines, rows = tops.shape[0], accs.shape[0], accs.shape[1] // 2
     for i in range(pairs):
         for h in range(2):
@@ -387,22 +384,33 @@
             sums[i : i + 1, h * rows : (h + 1) * rows] = totals[i : i + 1, here] * near_fade + far_total * far_fade
             merged[span] = accs[span, :rows] * near_fade + far[span] * far_fade
     finish(merged, sums, joined)
-    share = jnp.dot(joined[...], w_out[part * lines : (part + 1) * lines], preferred_element_type=F32)
-    out[...] = (base[...] + share).astype(out.dtype)
+    copies = []
+    for q in range(out.shape[1] // WIDE):
+        cols = slice(q * WIDE, (q + 1) * WIDE)
+        share = jnp.dot(joined[...], w_out[part * lines : (part + 1) * lines, cols], preferred_element_type=F32)
+        if not rest:
+            out[:, cols] = base[:, cols] + share
+            continue
+        staged, sems = rest
+        staged[:, cols] = (base[:, cols] + share).astype(BF16)
+        copies.append(pltpu.make_async_copy(staged.at[:, cols], out.at[:, cols], sems.at[q]))
+        copies[-1].start()
+    for copy in copies:
+        copy.wait()
 
 
 def on_chip(x):
     return pltpu.with_memory_space_constraint(x, VMEM)
 
 
-def call(kernel, args, outs, scratch, flops, limit, aliases=None, scalars=0):
+def call(kernel, args, outs, scratch, flops, limit, aliases=None, scalars=0, space=VMEM):
     specs = [pl.BlockSpec(memory_space=pltpu.SMEM)] * scalars
     specs += [pl.BlockSpec(memory_space=VMEM)] * (len(args) - scalars)
     return pl.pallas_call(
         kernel,
         out_shape=outs,
         in_specs=specs,
-        out_specs=jax.tree.map(lambda _: pl.BlockSpec(memory_space=VMEM), outs, is_leaf=lambda o: hasattr(o, "shape")),
+        out_specs=jax.tree.map(lambda _: pl.BlockSpec(memory_space=space), outs, is_leaf=lambda o: hasattr(o, "shape")),
         scratch_shapes=scratch,
         compiler_params=pltpu.CompilerParams(vmem_limit_bytes=limit << 20),
         cost_estimate=pl.CostEstimate(flops=flops, bytes_accessed=1 << 20, transcendentals=0),
@@ -536,8 +544,9 @@
         whole = jax.ShapeDtypeStruct((rows, width), BF16) if part else VMEM((rows, width), F32)
         out = call(
             functools.partial(final_kernel, part), [*done[part], out, w_self_out], whole,
-            [VMEM((rows, lines), BF16), VMEM((lines, rows), F32), VMEM((parts, 2 * rows), F32)],
-            1 << 29, 12,
+            [VMEM((rows, lines), BF16), VMEM((lines, rows), F32), VMEM((parts, 2 * rows), F32)]
+            + ([VMEM((rows, width), BF16), pltpu.SemaphoreType.DMA((width // WIDE,))] if part else []),
+            1 << 29, 12, space=pl.ANY if part else VMEM,
         )
     return out
 

time: 70.3 us -> 69.9 us (level)
  no operation moved by 1% of the time
where the time goes in v4:
time: 69.9 us; the launch traced here: 69.4 us
  starting transfers between devices  27.8 us (40%)
  Pallas kernels  24.4 us (35%)
  waiting for transfers between devices  16.8 us (24%)
    ppermute x11, starting transfers between devices, both_ways(): fore = lax.ppermute(fore, 'frame', ahead)  25.2 us
    pallas_call x14, Pallas kernels, call(): pl.pallas_call(kernel, out_shape=outs, in_specs=specs, out_specs=jax.tree...  23.4 us
    ppermute x11, waiting for transfers between devices, both_ways(): fore = lax.ppermute(fore, 'frame', ahead)  12.6 us
    ppermute x11, waiting for transfers between devices, both_ways(): aft = lax.ppermute(aft, 'frame', behind)  2.36 us
    ppermute x12, waiting for transfers between devices, cross_over(): return lax.ppermute(x, 'frame', swap)  1.83 us
    ppermute x12, starting transfers between devices, cross_over(): return lax.ppermute(x, 'frame', swap)  1.66 us
  transfers between devices with their start and end apart: 34, of which 13 were waited for; matrix products, arithmetic and copies ran while one was open for 0% of the time, Pallas kernels for 29%

profile of v4, /device:TPU:0, one launch (start us, length us, event | category | flops | bytes accessed | tf_op | source)
XLA Modules:
  0.0 69.4 jit_solution(18277235473883236029)
XLA Ops:
  1.1 3.1 %collective-permute-start = (bf16[136,512]{1,0:T(8,128)(2,1)S(1)}, bf16[136,512]{1,0:T(8,128)(2,1)S(1)}, u32[]{:S(2)}, u32[]{:S(2)}) collective-permute-start(bf16[136,512]{1,0:T(8,128)(2,1)S(1)} %tag.1.refs_0_), channel_id=1, source_target_pairs={{0,4},{1,5},{4,8},{5,9},{8,12},{9,13},{12,14},{13,15},{14,10},{15,... | collective-permute-start | bytes 417800 | tf_op jit(solution)/shard_map/ppermute | solution.py:434
  4.2 3.6 %collective-permute-done.refs_2_ = bf16[136,512]{1,0:T(8,128)(2,1)S(1)} collective-permute-done((bf16[136,512]{1,0:T(8,128)(2,1)S(1)}, bf16[136,512]{1,0:T(8,128)(2,1)S(1)}, u32[]{:S(2)}, u32[]{:S(2)}) %collective-permute-start) | collective-permute-done | bytes 139296 | tf_op jit(solution)/shard_map/ppermute | solution.py:434
  7.8 1.8 %collective-permute-start.1 = (bf16[136,512]{1,0:T(8,128)(2,1)S(1)}, bf16[136,512]{1,0:T(8,128)(2,1)S(1)}, u32[]{:S(2)}, u32[]{:S(2)}) collective-permute-start(bf16[136,512]{1,0:T(8,128)(2,1)S(1)} %collective-permute-done.refs_2_), channel_id=1, source_target_pairs={{0,4},{1,5},{4,8},{5,9},{8,12},{9,13},{12,14},{13,15},{14,10},{15,... | collective-permute-start | bytes 417800 | tf_op jit(solution)/shard_map/ppermute | solution.py:434
  9.8 3.0 %collective-permute-done.1.refs_2_ = bf16[136,512]{1,0:T(8,128)(2,1)S(1)} collective-permute-done((bf16[136,512]{1,0:T(8,128)(2,1)S(1)}, bf16[136,512]{1,0:T(8,128)(2,1)S(1)}, u32[]{:S(2)}, u32[]{:S(2)}) %collective-permute-start.1) | collective-permute-done | bytes 139296 | tf_op jit(solution)/shard_map/ppermute | solution.py:434
  12.8 1.8 %collective-permute-start.2 = (bf16[136,512]{1,0:T(8,128)(2,1)S(1)}, bf16[136,512]{1,0:T(8,128)(2,1)S(1)}, u32[]{:S(2)}, u32[]{:S(2)}) collective-permute-start(bf16[136,512]{1,0:T(8,128)(2,1)S(1)} %collective-permute-done.1.refs_2_), channel_id=1, source_target_pairs={{0,4},{1,5},{4,8},{5,9},{8,12},{9,13},{12,14},{13,15},{14,10},{15,... | collective-permute-start | bytes 417800 | tf_op jit(solution)/shard_map/ppermute | solution.py:434
  15.5 2.4 %collective-permute-done.2.refs_2_ = bf16[136,512]{1,0:T(8,128)(2,1)S(1)} collective-permute-done((bf16[136,512]{1,0:T(8,128)(2,1)S(1)}, bf16[136,512]{1,0:T(8,128)(2,1)S(1)}, u32[]{:S(2)}, u32[]{:S(2)}) %collective-permute-start.2) | collective-permute-done | bytes 139296 | tf_op jit(solution)/shard_map/ppermute | solution.py:434
  17.9 1.4 %shard_map.83 = (f32[8,256]{1,0:T(8,128)S(1)}, f32[8,256]{1,0:T(8,128)S(1)}, f32[1024,128]{1,0:T(8,128)S(1)}) custom-call(bf16[136,512]{1,0:T(8,128)(2,1)S(1)} %tag.1.refs_0_, bf16[136,512]{1,0:T(8,128)(2,1)S(1)} %collective-permute-done.16.refs_1_, bf16[136,512]{1,0:T(8,128)(2,1)S(1)} %collective-permute-done.refs_2_, ...), custom_call_target="tpu_custom_call" | custom-call | flops 1073741824 | bytes 1048576 | tf_op jit(solution)/shard_map/pallas_call | solution.py:409
  19.7 1.6 %collective-permute-start.8 = (bf16[72,512]{1,0:T(8,128)(2,1)S(1)}, bf16[72,512]{1,0:T(8,128)(2,1)S(1)}, u32[]{:S(2)}, u32[]{:S(2)}) collective-permute-start(bf16[72,512]{1,0:T(8,128)(2,1)S(1)} %slice.18), channel_id=1, source_target_pairs={{0,4},{1,5},{4,8},{5,9},{8,12},{9,13},{12,14},{13,15},{14,10},{15,... | collective-permute-start | bytes 221192 | tf_op jit(solution)/shard_map/ppermute | solution.py:434
  24.0 1.6 %collective-permute-done.9.refs_3_ = bf16[72,512]{1,0:T(8,128)(2,1)S(1)} collective-permute-done((bf16[72,512]{1,0:T(8,128)(2,1)S(1)}, bf16[72,512]{1,0:T(8,128)(2,1)S(1)}, u32[]{:S(2)}, u32[]{:S(2)}) %collective-permute-start.9) | collective-permute-done | bytes 73760 | tf_op jit(solution)/shard_map/ppermute | solution.py:435
  27.9 2.8 %collective-permute-start.17 = (bf16[64,1024]{1,0:T(8,128)(2,1)S(1)}, bf16[64,1024]{1,0:T(8,128)(2,1)S(1)}, u32[]{:S(2)}, u32[]{:S(2)}) collective-permute-start(bf16[64,1024]{1,0:T(8,128)(2,1)S(1)} %get-tuple-element.76), channel_id=1, source_target_pairs={{0,4},{1,5},{4,8},{5,9},{8,12},{9,13},{12,14},{13,15},{14,10},{15,... | collective-permute-start | bytes 393224 | tf_op jit(solution)/shard_map/ppermute | solution.py:434
  30.7 2.0 %collective-permute-start.26 = (bf16[64,1024]{1,0:T(8,128)(2,1)S(1)}, bf16[64,1024]{1,0:T(8,128)(2,1)S(1)}, u32[]{:S(2)}, u32[]{:S(2)}) collective-permute-start(bf16[64,1024]{1,0:T(8,128)(2,1)S(1)} %get-tuple-element.75), channel_id=1, source_target_pairs={{0,4},{1,5},{4,8},{5,9},{8,12},{9,13},{12,14},{13,15},{14,10},{15,... | collective-permute-start | bytes 393224 | tf_op jit(solution)/shard_map/ppermute | solution.py:434
  32.8 1.9 %collective-permute-done.17.refs_0_ = bf16[64,1024]{1,0:T(8,128)(2,1)S(1)} collective-permute-done((bf16[64,1024]{1,0:T(8,128)(2,1)S(1)}, bf16[64,1024]{1,0:T(8,128)(2,1)S(1)}, u32[]{:S(2)}, u32[]{:S(2)}) %collective-permute-start.17) | collective-permute-done | bytes 131104 | tf_op jit(solution)/shard_map/ppermute | solution.py:434
  34.6 2.5 %collective-permute-start.18 = (bf16[64,1024]{1,0:T(8,128)(2,1)S(1)}, bf16[64,1024]{1,0:T(8,128)(2,1)S(1)}, u32[]{:S(2)}, u32[]{:S(2)}) collective-permute-start(bf16[64,1024]{1,0:T(8,128)(2,1)S(1)} %collective-permute-done.17.refs_0_), channel_id=1, source_target_pairs={{0,4},{1,5},{4,8},{5,9},{8,12},{9,13},{12,14},{13,15},{14,10},{15,... | collective-permute-start | bytes 393224 | tf_op jit(solution)/shard_map/ppermute | solution.py:434
  37.4 2.5 %collective-permute-start.27 = (bf16[64,1024]{1,0:T(8,128)(2,1)S(1)}, bf16[64,1024]{1,0:T(8,128)(2,1)S(1)}, u32[]{:S(2)}, u32[]{:S(2)}) collective-permute-start(bf16[64,1024]{1,0:T(8,128)(2,1)S(1)} %collective-permute-done.26.refs_0_), channel_id=1, source_target_pairs={{0,4},{1,5},{4,8},{5,9},{8,12},{9,13},{12,14},{13,15},{14,10},{15,... | collective-permute-start | bytes 393224 | tf_op jit(solution)/shard_map/ppermute | solution.py:434
  40.7 2.5 %collective-permute-start.19 = (bf16[64,1024]{1,0:T(8,128)(2,1)S(1)}, bf16[64,1024]{1,0:T(8,128)(2,1)S(1)}, u32[]{:S(2)}, u32[]{:S(2)}) collective-permute-start(bf16[64,1024]{1,0:T(8,128)(2,1)S(1)} %collective-permute-done.18.refs_2_), channel_id=1, source_target_pairs={{0,4},{1,5},{4,8},{5,9},{8,12},{9,13},{12,14},{13,15},{14,10},{15,... | collective-permute-start | bytes 393224 | tf_op jit(solution)/shard_map/ppermute | solution.py:434
  43.8 2.5 %collective-permute-start.28 = (bf16[64,1024]{1,0:T(8,128)(2,1)S(1)}, bf16[64,1024]{1,0:T(8,128)(2,1)S(1)}, u32[]{:S(2)}, u32[]{:S(2)}) collective-permute-start(bf16[64,1024]{1,0:T(8,128)(2,1)S(1)} %collective-permute-done.27.refs_0_), channel_id=1, source_target_pairs={{0,4},{1,5},{4,8},{5,9},{8,12},{9,13},{12,14},{13,15},{14,10},{15,... | collective-permute-start | bytes 393224 | tf_op jit(solution)/shard_map/ppermute | solution.py:434
  46.3 2.0 %shard_map.87 = (bf16[8,128,512]{2,1,0:T(8,128)(2,1)S(1)}, f32[8,512]{1,0:T(8,128)S(1)}, f32[8,512]{1,0:T(8,128)S(1)}, f32[1024,256]{1,0:T(8,128)S(1)}) custom-call(bf16[128,1024]{1,0:T(8,128)(2,1)S(1)} %get-tuple-element.49.mine, bf16[128,1024]{1,0:T(8,128)(2,1)S(1)} %collective-permute-done.25.other, bf16[1024,3072]{1,0:T(8,128)(2,1)S(1)} %bitcast.1), custom_call_target="tpu_custom_call" | custom-call | flops 1073741824 | bytes 1048576 | tf_op jit(solution)/shard_map/pallas_call | solution.py:409
  48.4 2.5 %shard_map.88 = (f32[8,512]{1,0:T(8,128)S(1)}, f32[8,512]{1,0:T(8,128)S(1)}, f32[1024,256]{1,0:T(8,128)S(1)}) custom-call(bf16[64,1024]{1,0:T(8,128)(2,1)S(1)} %collective-permute-done.17.refs_0_, bf16[64,1024]{1,0:T(8,128)(2,1)S(1)} %collective-permute-done.21.refs_1_, bf16[1024,3072]{1,0:T(8,128)(2,1)S(1)} %bitcast.1, ...), custom_call_target="tpu_custom_call" | custom-call | flops 1073741824 | bytes 1048576 | tf_op jit(solution)/shard_map/pallas_call | solution.py:409
  50.9 4.1 %shard_map.89 = (f32[8,512]{1,0:T(8,128)S(1)}, f32[8,512]{1,0:T(8,128)S(1)}, f32[1024,256]{1,0:T(8,128)S(1)}) custom-call(bf16[64,1024]{1,0:T(8,128)(2,1)S(1)} %collective-permute-done.26.refs_0_, bf16[64,1024]{1,0:T(8,128)(2,1)S(1)} %collective-permute-done.29.refs_1_, bf16[64,1024]{1,0:T(8,128)(2,1)S(1)} %collective-permute-done.18.refs_2_, ...), custom_call_target="tpu_custom_call" | custom-call | flops 2147483648 | bytes 1048576 | tf_op jit(solution)/shard_map/pallas_call | solution.py:409
  54.9 2.1 %collective-permute-start.20 = (bf16[64,1024]{1,0:T(8,128)(2,1)S(1)}, bf16[64,1024]{1,0:T(8,128)(2,1)S(1)}, u32[]{:S(2)}, u32[]{:S(2)}) collective-permute-start(bf16[64,1024]{1,0:T(8,128)(2,1)S(1)} %collective-permute-done.19.refs_2_), channel_id=1, source_target_pairs={{0,4},{1,5},{4,8},{5,9},{8,12},{9,13},{12,14},{13,15},{14,10},{15,... | collective-permute-start | bytes 393224 | tf_op jit(solution)/shard_map/ppermute | solution.py:434
  57.0 4.0 %shard_map.90 = (f32[8,512]{1,0:T(8,128)S(1)}, f32[8,512]{1,0:T(8,128)S(1)}, f32[1024,256]{1,0:T(8,128)S(1)}) custom-call(bf16[64,1024]{1,0:T(8,128)(2,1)S(1)} %collective-permute-done.27.refs_0_, bf16[64,1024]{1,0:T(8,128)(2,1)S(1)} %collective-permute-done.30.refs_1_, bf16[64,1024]{1,0:T(8,128)(2,1)S(1)} %collective-permute-done.19.refs_2_, ...), custom_call_target="tpu_custom_call" | custom-call | flops 2147483648 | bytes 1048576 | tf_op jit(solution)/shard_map/pallas_call | solution.py:409
  61.1 2.4 %shard_map.91 = (f32[8,512]{1,0:T(8,128)S(1)}, f32[8,512]{1,0:T(8,128)S(1)}, f32[1024,256]{1,0:T(8,128)S(1)}) custom-call(bf16[64,1024]{1,0:T(8,128)(2,1)S(1)} %collective-permute-done.28.refs_0_, bf16[64,1024]{1,0:T(8,128)(2,1)S(1)} %collective-permute-done.31.refs_1_, bf16[1024,3072]{1,0:T(8,128)(2,1)S(1)} %bitcast.1, ...), custom_call_target="tpu_custom_call" | custom-call | flops 1073741824 | bytes 1048576 | tf_op jit(solution)/shard_map/pallas_call | solution.py:409
  63.4 1.5 %shard_map.93 = (f32[4,512]{1,0:T(4,128)S(1)}, f32[4,512]{1,0:T(4,128)S(1)}, f32[512,256]{1,0:T(8,128)S(1)}, f32[528,128]{1,0:T(8,128)S(1)}) custom-call(bf16[64,1024]{1,0:T(8,128)(2,1)S(1)} %collective-permute-done.20.refs_0_, bf16[64,1024]{1,0:T(8,128)(2,1)S(1)} %collective-permute-done.24.refs_1_, bf16[1024,3072]{1,0:T(8,128)(2,1)S(1)} %bitcast.1, ...), custom_call_target="tpu_custom_call" | custom-call | flops 536870912 | bytes 1048576 | tf_op jit(solution)/shard_map/pallas_call | solution.py:409
  65.0 1.5 %shard_map.92 = (f32[4,512]{1,0:T(4,128)S(1)}, f32[4,512]{1,0:T(4,128)S(1)}, f32[512,256]{1,0:T(8,128)S(1)}, f32[528,128]{1,0:T(8,128)S(1)}) custom-call(bf16[64,1024]{1,0:T(8,128)(2,1)S(1)} %collective-permute-done.20.refs_0_, bf16[64,1024]{1,0:T(8,128)(2,1)S(1)} %collective-permute-done.24.refs_1_, bf16[1024,3072]{1,0:T(8,128)(2,1)S(1)} %bitcast.1, ...), custom_call_target="tpu_custom_call" | custom-call | flops 536870912 | bytes 1048576 | tf_op jit(solution)/shard_map/pallas_call | solution.py:409
  (77 shorter events, 12.1 us)
Async XLA Ops:
  1.1 6.7 %collective-permute-start = (bf16[136,512]{1,0:T(8,128)(2,1)S(1)}, bf16[136,512]{1,0:T(8,128)(2,1)S(1)}, u32[]{:S(2)}, u32[]{:S(2)}) collective-permute-start(bf16[136,512]{1,0:T(8,128)(2,1)S(1)} %tag.1.refs_0_), channel_id=1, source_target_pairs={{0,4},{1,5},{4,8},{5,9},{8,12},{9,13},{12,14},{13,15},{14,10},{15,... | collective-permute-start | bytes 417800 | tf_op jit(solution)/shard_map/ppermute | solution.py:434
  4.2 5.4 %collective-permute-start.4 = (bf16[136,512]{1,0:T(8,128)(2,1)S(1)}, bf16[136,512]{1,0:T(8,128)(2,1)S(1)}, u32[]{:S(2)}, u32[]{:S(2)}) collective-permute-start(bf16[136,512]{1,0:T(8,128)(2,1)S(1)} %tag.1.refs_0_), channel_id=1, source_target_pairs={{4,0},{5,1},{8,4},{9,5},{12,8},{13,9},{14,12},{15,13},{10,14},{11,... | collective-permute-start | bytes 417800 | tf_op jit(solution)/shard_map/ppermute | solution.py:435
  7.8 5.1 %collective-permute-start.1 = (bf16[136,512]{1,0:T(8,128)(2,1)S(1)}, bf16[136,512]{1,0:T(8,128)(2,1)S(1)}, u32[]{:S(2)}, u32[]{:S(2)}) collective-permute-start(bf16[136,512]{1,0:T(8,128)(2,1)S(1)} %collective-permute-done.refs_2_), channel_id=1, source_target_pairs={{0,4},{1,5},{4,8},{5,9},{8,12},{9,13},{12,14},{13,15},{14,10},{15,... | collective-permute-start | bytes 417800 | tf_op jit(solution)/shard_map/ppermute | solution.py:434
  9.6 5.1 %collective-permute-start.5 = (bf16[136,512]{1,0:T(8,128)(2,1)S(1)}, bf16[136,512]{1,0:T(8,128)(2,1)S(1)}, u32[]{:S(2)}, u32[]{:S(2)}) collective-permute-start(bf16[136,512]{1,0:T(8,128)(2,1)S(1)} %collective-permute-done.4.refs_3_), channel_id=1, source_target_pairs={{4,0},{5,1},{8,4},{9,5},{12,8},{13,9},{14,12},{15,13},{10,14},{11,... | collective-permute-start | bytes 417800 | tf_op jit(solution)/shard_map/ppermute | solution.py:435
  9.8 5.6 %collective-permute-start.16 = (bf16[136,512]{1,0:T(8,128)(2,1)S(1)}, bf16[136,512]{1,0:T(8,128)(2,1)S(1)}, u32[]{:S(2)}, u32[]{:S(2)}) collective-permute-start(bf16[136,512]{1,0:T(8,128)(2,1)S(1)} %tag.1.refs_0_), channel_id=1, source_target_pairs={{0,1},{1,0},{2,3},{3,2},{4,5},{5,4},{6,7},{7,6},{8,9},{9,8},{10,11... | collective-permute-start | bytes 417800 | tf_op jit(solution)/shard_map/ppermute | solution.py:431
  14.8 6.4 %collective-permute-start.14 = (bf16[136,512]{1,0:T(8,128)(2,1)S(1)}, bf16[136,512]{1,0:T(8,128)(2,1)S(1)}, u32[]{:S(2)}, u32[]{:S(2)}) collective-permute-start(bf16[136,512]{1,0:T(8,128)(2,1)S(1)} %collective-permute-done.refs_2_), channel_id=1, source_target_pairs={{0,1},{1,0},{2,3},{3,2},{4,5},{5,4},{6,7},{7,6},{8,9},{9,8},{10,11... | collective-permute-start | bytes 417800 | tf_op jit(solution)/shard_map/ppermute | solution.py:431
  14.8 6.9 %collective-permute-start.15 = (bf16[136,512]{1,0:T(8,128)(2,1)S(1)}, bf16[136,512]{1,0:T(8,128)(2,1)S(1)}, u32[]{:S(2)}, u32[]{:S(2)}) collective-permute-start(bf16[136,512]{1,0:T(8,128)(2,1)S(1)} %collective-permute-done.4.refs_3_), channel_id=1, source_target_pairs={{0,1},{1,0},{2,3},{3,2},{4,5},{5,4},{6,7},{7,6},{8,9},{9,8},{10,11... | collective-permute-start | bytes 417800 | tf_op jit(solution)/shard_map/ppermute | solution.py:431
  15.4 6.4 %collective-permute-start.12 = (bf16[136,512]{1,0:T(8,128)(2,1)S(1)}, bf16[136,512]{1,0:T(8,128)(2,1)S(1)}, u32[]{:S(2)}, u32[]{:S(2)}) collective-permute-start(bf16[136,512]{1,0:T(8,128)(2,1)S(1)} %collective-permute-done.1.refs_2_), channel_id=1, source_target_pairs={{0,1},{1,0},{2,3},{3,2},{4,5},{5,4},{6,7},{7,6},{8,9},{9,8},{10,11... | collective-permute-start | bytes 417800 | tf_op jit(solution)/shard_map/ppermute | solution.py:431
  17.9 7.8 %collective-permute-start.13 = (bf16[136,512]{1,0:T(8,128)(2,1)S(1)}, bf16[136,512]{1,0:T(8,128)(2,1)S(1)}, u32[]{:S(2)}, u32[]{:S(2)}) collective-permute-start(bf16[136,512]{1,0:T(8,128)(2,1)S(1)} %collective-permute-done.5.refs_3_), channel_id=1, source_target_pairs={{0,1},{1,0},{2,3},{3,2},{4,5},{5,4},{6,7},{7,6},{8,9},{9,8},{10,11... | collective-permute-start | bytes 417800 | tf_op jit(solution)/shard_map/ppermute | solution.py:431
  27.9 6.7 %collective-permute-start.17 = (bf16[64,1024]{1,0:T(8,128)(2,1)S(1)}, bf16[64,1024]{1,0:T(8,128)(2,1)S(1)}, u32[]{:S(2)}, u32[]{:S(2)}) collective-permute-start(bf16[64,1024]{1,0:T(8,128)(2,1)S(1)} %get-tuple-element.76), channel_id=1, source_target_pairs={{0,4},{1,5},{4,8},{5,9},{8,12},{9,13},{12,14},{13,15},{14,10},{15,... | collective-permute-start | bytes 393224 | tf_op jit(solution)/shard_map/ppermute | solution.py:434
  30.7 6.4 %collective-permute-start.21 = (bf16[64,1024]{1,0:T(8,128)(2,1)S(1)}, bf16[64,1024]{1,0:T(8,128)(2,1)S(1)}, u32[]{:S(2)}, u32[]{:S(2)}) collective-permute-start(bf16[64,1024]{1,0:T(8,128)(2,1)S(1)} %get-tuple-element.75), channel_id=1, source_target_pairs={{4,0},{5,1},{8,4},{9,5},{12,8},{13,9},{14,12},{15,13},{10,14},{11,... | collective-permute-start | bytes 393224 | tf_op jit(solution)/shard_map/ppermute | solution.py:435
  30.7 6.7 %collective-permute-start.26 = (bf16[64,1024]{1,0:T(8,128)(2,1)S(1)}, bf16[64,1024]{1,0:T(8,128)(2,1)S(1)}, u32[]{:S(2)}, u32[]{:S(2)}) collective-permute-start(bf16[64,1024]{1,0:T(8,128)(2,1)S(1)} %get-tuple-element.75), channel_id=1, source_target_pairs={{0,4},{1,5},{4,8},{5,9},{8,12},{9,13},{12,14},{13,15},{14,10},{15,... | collective-permute-start | bytes 393224 | tf_op jit(solution)/shard_map/ppermute | solution.py:434
  32.8 7.2 %collective-permute-start.29 = (bf16[64,1024]{1,0:T(8,128)(2,1)S(1)}, bf16[64,1024]{1,0:T(8,128)(2,1)S(1)}, u32[]{:S(2)}, u32[]{:S(2)}) collective-permute-start(bf16[64,1024]{1,0:T(8,128)(2,1)S(1)} %get-tuple-element.76), channel_id=1, source_target_pairs={{4,0},{5,1},{8,4},{9,5},{12,8},{13,9},{14,12},{15,13},{10,14},{11,... | collective-permute-start | bytes 393224 | tf_op jit(solution)/shard_map/ppermute | solution.py:435
  32.8 13.5 %collective-permute-start.25 = (bf16[128,1024]{1,0:T(8,128)(2,1)S(1)}, bf16[128,1024]{1,0:T(8,128)(2,1)S(1)}, u32[]{:S(2)}, u32[]{:S(2)}) collective-permute-start(bf16[128,1024]{1,0:T(8,128)(2,1)S(1)} %get-tuple-element.49.mine), channel_id=1, source_target_pairs={{0,1},{1,0},{2,3},{3,2},{4,5},{5,4},{6,7},{7,6},{8,9},{9,8},{10,11... | collective-permute-start | bytes 786440 | tf_op jit(solution)/shard_map/ppermute | solution.py:431
  34.6 6.0 %collective-permute-start.18 = (bf16[64,1024]{1,0:T(8,128)(2,1)S(1)}, bf16[64,1024]{1,0:T(8,128)(2,1)S(1)}, u32[]{:S(2)}, u32[]{:S(2)}) collective-permute-start(bf16[64,1024]{1,0:T(8,128)(2,1)S(1)} %collective-permute-done.17.refs_0_), channel_id=1, source_target_pairs={{0,4},{1,5},{4,8},{5,9},{8,12},{9,13},{12,14},{13,15},{14,10},{15,... | collective-permute-start | bytes 393224 | tf_op jit(solution)/shard_map/ppermute | solution.py:434
  37.1 6.3 %collective-permute-start.22 = (bf16[64,1024]{1,0:T(8,128)(2,1)S(1)}, bf16[64,1024]{1,0:T(8,128)(2,1)S(1)}, u32[]{:S(2)}, u32[]{:S(2)}) collective-permute-start(bf16[64,1024]{1,0:T(8,128)(2,1)S(1)} %collective-permute-done.21.refs_1_), channel_id=1, source_target_pairs={{4,0},{5,1},{8,4},{9,5},{12,8},{13,9},{14,12},{15,13},{10,14},{11,... | collective-permute-start | bytes 393224 | tf_op jit(solution)/shard_map/ppermute | solution.py:435
  37.4 6.4 %collective-permute-start.27 = (bf16[64,1024]{1,0:T(8,128)(2,1)S(1)}, bf16[64,1024]{1,0:T(8,128)(2,1)S(1)}, u32[]{:S(2)}, u32[]{:S(2)}) collective-permute-start(bf16[64,1024]{1,0:T(8,128)(2,1)S(1)} %collective-permute-done.26.refs_0_), channel_id=1, source_target_pairs={{0,4},{1,5},{4,8},{5,9},{8,12},{9,13},{12,14},{13,15},{14,10},{15,... | collective-permute-start | bytes 393224 | tf_op jit(solution)/shard_map/ppermute | solution.py:434
  39.9 6.4 %collective-permute-start.30 = (bf16[64,1024]{1,0:T(8,128)(2,1)S(1)}, bf16[64,1024]{1,0:T(8,128)(2,1)S(1)}, u32[]{:S(2)}, u32[]{:S(2)}) collective-permute-start(bf16[64,1024]{1,0:T(8,128)(2,1)S(1)} %collective-permute-done.29.refs_1_), channel_id=1, source_target_pairs={{4,0},{5,1},{8,4},{9,5},{12,8},{13,9},{14,12},{15,13},{10,14},{11,... | collective-permute-start | bytes 393224 | tf_op jit(solution)/shard_map/ppermute | solution.py:435
  40.7 14.3 %collective-permute-start.19 = (bf16[64,1024]{1,0:T(8,128)(2,1)S(1)}, bf16[64,1024]{1,0:T(8,128)(2,1)S(1)}, u32[]{:S(2)}, u32[]{:S(2)}) collective-permute-start(bf16[64,1024]{1,0:T(8,128)(2,1)S(1)} %collective-permute-done.18.refs_2_), channel_id=1, source_target_pairs={{0,4},{1,5},{4,8},{5,9},{8,12},{9,13},{12,14},{13,15},{14,10},{15,... | collective-permute-start | bytes 393224 | tf_op jit(solution)/shard_map/ppermute | solution.py:434
  43.4 13.6 %collective-permute-start.23 = (bf16[64,1024]{1,0:T(8,128)(2,1)S(1)}, bf16[64,1024]{1,0:T(8,128)(2,1)S(1)}, u32[]{:S(2)}, u32[]{:S(2)}) collective-permute-start(bf16[64,1024]{1,0:T(8,128)(2,1)S(1)} %collective-permute-done.22.refs_3_), channel_id=1, source_target_pairs={{4,0},{5,1},{8,4},{9,5},{12,8},{13,9},{14,12},{15,13},{10,14},{11,... | collective-permute-start | bytes 393224 | tf_op jit(solution)/shard_map/ppermute | solution.py:435
  43.8 17.3 %collective-permute-start.28 = (bf16[64,1024]{1,0:T(8,128)(2,1)S(1)}, bf16[64,1024]{1,0:T(8,128)(2,1)S(1)}, u32[]{:S(2)}, u32[]{:S(2)}) collective-permute-start(bf16[64,1024]{1,0:T(8,128)(2,1)S(1)} %collective-permute-done.27.refs_0_), channel_id=1, source_target_pairs={{0,4},{1,5},{4,8},{5,9},{8,12},{9,13},{12,14},{13,15},{14,10},{15,... | collective-permute-start | bytes 393224 | tf_op jit(solution)/shard_map/ppermute | solution.py:434
  46.3 14.8 %collective-permute-start.31 = (bf16[64,1024]{1,0:T(8,128)(2,1)S(1)}, bf16[64,1024]{1,0:T(8,128)(2,1)S(1)}, u32[]{:S(2)}, u32[]{:S(2)}) collective-permute-start(bf16[64,1024]{1,0:T(8,128)(2,1)S(1)} %collective-permute-done.30.refs_1_), channel_id=1, source_target_pairs={{4,0},{5,1},{8,4},{9,5},{12,8},{13,9},{14,12},{15,13},{10,14},{11,... | collective-permute-start | bytes 393224 | tf_op jit(solution)/shard_map/ppermute | solution.py:435
  54.9 8.5 %collective-permute-start.20 = (bf16[64,1024]{1,0:T(8,128)(2,1)S(1)}, bf16[64,1024]{1,0:T(8,128)(2,1)S(1)}, u32[]{:S(2)}, u32[]{:S(2)}) collective-permute-start(bf16[64,1024]{1,0:T(8,128)(2,1)S(1)} %collective-permute-done.19.refs_2_), channel_id=1, source_target_pairs={{0,4},{1,5},{4,8},{5,9},{8,12},{9,13},{12,14},{13,15},{14,10},{15,... | collective-permute-start | bytes 393224 | tf_op jit(solution)/shard_map/ppermute | solution.py:434
  57.0 6.4 %collective-permute-start.24 = (bf16[64,1024]{1,0:T(8,128)(2,1)S(1)}, bf16[64,1024]{1,0:T(8,128)(2,1)S(1)}, u32[]{:S(2)}, u32[]{:S(2)}) collective-permute-start(bf16[64,1024]{1,0:T(8,128)(2,1)S(1)} %collective-permute-done.23.refs_3_), channel_id=1, source_target_pairs={{4,0},{5,1},{8,4},{9,5},{12,8},{13,9},{14,12},{15,13},{10,14},{11,... | collective-permute-start | bytes 393224 | tf_op jit(solution)/shard_map/ppermute | solution.py:435
  (17 other events, 114.6 us)
